TPU v7x, 256 devices: a whole 4x4x8 slice. The times are simulated.
256 devices in a mesh: dp: 8 (over y, core), seq: 32 (over x, z).
Axes of the slice: x: 4, y: 4, z: 8, core: 2. Of those that a mesh axis runs over, the one named last changes fastest.
Arguments:
- x_in: bfloat16 [8, 8192, 2048], P('dp', 'seq'), may hold values from -0.37 to 0.37
- b_in: bfloat16 [8, 8192, 128], P('dp', 'seq'), may hold values from -7.4 to 7.4
- c_in: bfloat16 [8, 8192, 128], P('dp', 'seq'), may hold values from -0.12988281 to 0.12988281
- dt: float32 [8, 32, 8192], P('dp', None, 'seq'), may hold values from 0.2 to 32768, as said below
- a_log: float32 [32], replicated, may hold values from -14 to -2, as said below
- skip: float32 [32], replicated, may hold values from 1 to 3
- cotangent: bfloat16 [8, 8192, 2048], P('dp', 'seq'), may hold values from -0.29882812 to 0.29882812
Outputs:
- y_out: bfloat16 [8, 8192, 2048], P('dp', 'seq')
- grad_x: bfloat16 [8, 8192, 2048], P('dp', 'seq')
- grad_b: bfloat16 [8, 8192, 128], P('dp', 'seq')
- grad_c: bfloat16 [8, 8192, 128], P('dp', 'seq')
- grad_dt: float32 [8, 32, 8192], P('dp', None, 'seq')
- grad_alog: float32 [32], replicated
- derivative_bypass: float32 [32], replicated
Inputs may be any that keep to these rules, and one draw needn't show every extreme that they name: `dt`: positive step sizes. Each head's decay rate exp(a_log) is positive.
All inputs are finite; a program needn't handle non-finite values.
Results may differ from a plain program's by a relative error of at most 0.018.
Values sent between devices are 32-bit elements; how exact they have to be, the bound alone decides.
No kernel may reach another device: no remote copies, remote signals or barrier semaphores. Data moves between devices by JAX's collectives and lax.ppermute only.
A program may use at most 128 MiB of HBM per device.

v0:
```python
import jax
import jax.numpy as jnp
from jax import lax
from jax.sharding import PartitionSpec as P

GROUP = 256


def entering(part, axis, combine, identity, reverse):
    count = lax.axis_size(axis)
    place = lax.axis_index(axis)
    ahead = count - 1 - place if reverse else place
    gathered = jax.tree.map(lambda a: lax.all_gather(a, axis), part)
    state = jax.tree.map(lambda a, e: jnp.zeros_like(a) + jnp.asarray(e, a.dtype), part, identity)

    def one(lap, state):
        source = count - 1 - lap if reverse else lap
        return combine(
            state, jax.tree.map(lambda a: lax.dynamic_index_in_dim(a, source, 0, False), gathered)
        )

    return lax.fori_loop(0, ahead, one, state)


def piece_state(x_block, b_block, log_decay):
    span = x_block.shape[0]
    head_count = log_decay.shape[0]
    feat_width = x_block.shape[1]
    head_size = feat_width // head_count
    cum_log = jnp.cumsum(log_decay, axis=1)
    to_end = jnp.exp(cum_log[:, -1:] - cum_log)
    scaled = (
        x_block.reshape(span, head_count, head_size).astype(jnp.float32) * to_end.T[:, :, None]
    ).astype(jnp.bfloat16)
    block_state = lax.dot_general(
        scaled.reshape(span, feat_width),
        b_block,
        (((0,), (0,)), ((), ())),
        preferred_element_type=jnp.float32,
    )
    return (jnp.exp(cum_log[:, -1]), block_state.reshape(head_count, head_size, b_block.shape[1]))


def piece_out(x_block, b_block, c_block, log_decay, skip_gain, state_in):
    span = x_block.shape[0]
    head_count = log_decay.shape[0]
    feat_width = x_block.shape[1]
    head_size = feat_width // head_count
    cum_log = jnp.cumsum(log_decay, axis=1)
    inner_cb = jnp.dot(c_block, b_block.T, preferred_element_type=jnp.float32)
    row_ids = lax.broadcasted_iota(jnp.int32, (span, span), 0)
    col_ids = lax.broadcasted_iota(jnp.int32, (span, span), 1)
    lower = (row_ids >= col_ids)[None]
    differ = jnp.where(lower, cum_log[:, :, None] - cum_log[:, None, :], 0.0)
    weights = jnp.where(lower, inner_cb[None] * jnp.exp(differ), 0.0).astype(jnp.bfloat16)
    x_heads = x_block.reshape(span, head_count, head_size)
    inner = jnp.einsum("htu,uhp->thp", weights, x_heads, preferred_element_type=jnp.float32)
    state_low = state_in.astype(jnp.bfloat16)
    carried = jnp.einsum("tn,hpn->thp", c_block, state_low, preferred_element_type=jnp.float32)
    carried = carried * jnp.exp(cum_log).T[:, :, None]
    result = inner + carried + skip_gain[None, :, None] * x_heads.astype(jnp.float32)
    return result.reshape(span, feat_width)


def combine(earlier, later):
    return (earlier[0] * later[0], later[0][:, None, None] * earlier[1] + later[1])


def shards(x_in, b_in, c_in, dt, a_log, skip, cotangent):
    seq_len = x_in.shape[1]
    feat_width = x_in.shape[2]
    state_dim = b_in.shape[2]
    head_count = a_log.shape[0]
    head_size = feat_width // head_count
    block_count = seq_len // GROUP
    x_blocks = x_in[0].reshape(block_count, GROUP, feat_width)
    b_blocks = b_in[0].reshape(block_count, GROUP, state_dim)
    c_blocks = c_in[0].reshape(block_count, GROUP, state_dim)
    decay_rate = jnp.exp(a_log)
    la_flat = -decay_rate[:, None] * dt[0]
    la_blocks = la_flat.reshape(head_count, block_count, GROUP).transpose(1, 0, 2)
    (gains, block_states), state_pull = jax.vjp(
        jax.vmap(piece_state), x_blocks, b_blocks, la_blocks
    )
    total_state = jnp.zeros((head_count, head_size, state_dim), jnp.float32)
    block_id = 0
    total_state = gains[block_id][:, None, None] * total_state + block_states[block_id]
    tails = [jnp.ones((head_count,), jnp.float32)]
    for block_id in reversed(range(block_count)):
        tails.insert(0, gains[block_id] * tails[0])
    identity = (jnp.ones_like(tails[0]), jnp.zeros_like(total_state))
    incoming = entering((tails[0], total_state), "seq", combine, identity, False)[1]
    start_states = [incoming]
    start_stack = jnp.stack(start_states)
    y_full, out_pull = jax.vjp(
        jax.vmap(piece_out, in_axes=(0, 0, 0, 0, None, 0)),
        x_blocks,
        b_blocks,
        c_blocks,
        la_blocks,
        skip,
        start_stack,
    )
    y_out = y_full.reshape(seq_len, feat_width).astype(jnp.bfloat16)[None]
    upstream = cotangent[0].reshape(block_count, GROUP, feat_width).astype(jnp.float32)
    grad_x_out, grad_b_out, grad_c, grad_la_out, skip_term, grad_starts = out_pull(upstream)
    local_adjoint = [jnp.zeros_like(total_state)]
    for block_id in reversed(range(block_count)):
        local_adjoint.insert(
            0, grad_starts[block_id] + gains[block_id][:, None, None] * local_adjoint[0]
        )
    outgoing = entering((tails[0], local_adjoint[0]), "seq", combine, identity, True)[1]
    block_id = 0
    adjoint_next = local_adjoint[block_id + 1] + tails[block_id + 1][:, None, None] * outgoing
    grad_blocks = [adjoint_next]
    grad_gains = [jnp.sum(adjoint_next * start_states[block_id], axis=(1, 2))]
    grad_x_state, grad_b_state, grad_la_state = state_pull(
        (jnp.stack(grad_gains), jnp.stack(grad_blocks))
    )
    grad_x = (grad_x_out + grad_x_state).reshape(seq_len, feat_width)[None]
    grad_b = (grad_b_out + grad_b_state).reshape(seq_len, state_dim)[None]
    grad_c = grad_c.reshape(seq_len, state_dim)[None]
    grad_la = (grad_la_out + grad_la_state).transpose(1, 0, 2).reshape(head_count, seq_len)
    grad_dt = (grad_la * -decay_rate[:, None])[None]
    alog_term = jnp.sum(grad_la * la_flat, axis=1)
    grad_alog, derivative_bypass = lax.psum((alog_term, skip_term), ("dp", "seq"))
    return (y_out, grad_x, grad_b, grad_c, grad_dt, grad_alog, derivative_bypass)


def solution(mesh):
    placed = (
        P("dp", "seq", None),
        P("dp", "seq", None),
        P("dp", "seq", None),
        P("dp", None, "seq"),
        P(),
        P(),
        P("dp", "seq", None),
    )
    return jax.shard_map(
        shards,
        mesh=mesh,
        in_specs=placed,
        out_specs=(
            P("dp", "seq", None),
            P("dp", "seq", None),
            P("dp", "seq", None),
            P("dp", "seq", None),
            P("dp", None, "seq"),
            P(),
            P(),
        ),
        check_vma=False,
    )
```

profile of v0, /device:TPU:1, one launch (start us, length us, event | category | flops | bytes accessed | tf_op | source)
XLA Modules:
  0.0 704.1 jit_solution(7298282943825043774)
XLA Ops:
  10.2 1.5 copy.155
  11.7 1.6 fusion.43
  17.1 37.0 %all-gather = f32[32,32,1]{1,2,0:T(1,128)S(1)} all-gather(f32[1,32,1]{1,2,0:T(1,128)S(1)} %get-tuple-element.236), channel_id=2, replica_groups=mesh['dp'=8,'seq'=32] {'seq'}, dimensions={0}, use_global_device_ids=true | all-gather | bytes 4224 | tf_op jit(solution)/shard_map/all_gather | solution.py:13
  54.1 198.4 %all-gather.8.cloned.1.call-done = f32[1024,64,128]{2,1,0:T(8,128)} async-done(((f32[32,64,128]{2,1,0:T(8,128)}), f32[1024,64,128]{2,1,0:T(8,128)}) %all-gather.8.cloned.1.call-update) | async-done | bytes 33554448 | tf_op jit(solution)/shard_map/all_gather | solution.py:13
  252.6 46.2 %while.27 = (s32[]{:T(128)}, f32[32,64,128]{2,1,0:T(8,128)S(1)}, s32[]{:T(128)}, f32[32,32]{1,0:T(8,128)S(1)}, f32[32,32,64,128]{3,2,1,0:T(8,128)}, /*index=5*/s32[]{:T(128)}, s32[]{:T(128)}, s32[]{:T(128)}, s32[]{:T(128)}) while((s32[]{:T(128)}, f32[32,64,128]{2,1,0:T(8,128)S(1)}, s32[]{:T(128)}, f32[32,32]{1,0:T(8,128)S(1)}, ...), condition=%wide.region_5.6_spmd, body=%wide.region_4.5_spmd.sunk | while | flops 524294 | bytes 3146267 | solution.py:22
  252.7 1.4 bitcast_add_fusion.9
  254.2 1.4 bitcast_add_fusion.9
  255.7 1.4 bitcast_add_fusion.9
  257.1 1.4 bitcast_add_fusion.9
  258.6 1.4 bitcast_add_fusion.9
  260.1 1.4 bitcast_add_fusion.9
  261.6 1.4 bitcast_add_fusion.9
  278.0 1.4 bitcast_add_fusion.9
  279.5 1.4 bitcast_add_fusion.9
  299.3 3.5 multiply_reduce_fusion.2
  304.9 1.6 copy.153
  306.5 2.0 multiply_reduce_fusion.1
  309.5 2.1 convolution_add_fusion
  313.6 1.6 copy.174
  316.3 7.1 %fusion.1 = (f32[32,256]{1,0:T(8,128)}, f32[32,256]{1,0:T(8,128)}, bf16[256,256]{1,0:T(8,128)(2,1)}) fusion(f32[32,256]{1,0:T(8,128)S(1)} %bitcast_add_fusion.4, f32[256,256]{1,0:T(8,128)S(1)} %fusion.35, pred[256,256]{1,0:T(8,128)(4,1)S(1)} %iota_compare_fusion, bf16[32,64,256]{2,1,0:T(8,128)(2,1)} %bitcast.208, bf16[256,32,64]{0,2,1:T(8,128)(2,1)} %bitcast.205), kind=kOutput, calls=%fused_computation.10 | convolution fusion | flops 293519360 | bytes 2654208 | tf_op jit(solution)/shard_map/transpose(jvp(vmap(htu,uhp->thp)))/dot_general | solution.py:57
  323.4 1.5 copy.159
  324.9 1.5 copy.160
  326.4 1.8 fusion.17
  329.6 3.9 fusion.15
  334.8 2.3 copy.171
  337.8 2.4 fusion.21
  340.2 198.4 %all-gather.6.cloned.1.call-done = f32[1024,64,128]{2,1,0:T(8,128)} async-done(((f32[32,64,128]{2,1,0:T(8,128)}), f32[1024,64,128]{2,1,0:T(8,128)}) %all-gather.6.cloned.1.call-update) | async-done | bytes 33554448 | tf_op jit(solution)/shard_map/all_gather | solution.py:13
  541.2 1.8 fusion.10
  543.3 2.5 reduce-window.26
  546.0 2.5 reduce-window.24
  549.5 4.8 fusion.9
  557.3 140.0 %all-reduce.2 = (f32[32]{0:T(128)}, f32[32]{0:T(128)}) all-reduce(f32[32]{0:T(128)S(1)} %get-tuple-element.221, f32[32]{0:T(128)S(1)} %copy-done.28), channel_id=1, replica_groups=mesh['dp'=8,'seq'=32] {'dp','seq'}, use_global_device_ids=true, to_apply=%region_18.19 | all-reduce | flops 64 | bytes 512 | tf_op jit(solution)/shard_map/psum | solution.py:126
  (172 shorter events, 55.7 us)
Async XLA Ops:
  7.2 7.1 %copy-start = (bf16[1,256,128]{2,1,0:T(8,128)(2,1)S(1)}, bf16[1,256,128]{2,1,0:T(8,128)(2,1)}, u32[]{:S(2)}) copy-start(bf16[1,256,128]{2,1,0:T(8,128)(2,1)} %param.13) | copy-start | bytes 196612
  7.2 245.3 %all-gather.8.cloned.1.call-start = ((), (), s32[]{:S(2)}) async-start(), calls=%async_computation.1 | async-start | bytes 34603008 | tf_op jit(solution)/shard_map/all_gather | solution.py:13
  10.1 5.5 copy-start.16
  10.1 5.5 copy-start.27
  11.6 5.4 copy-start.3
  11.7 4.1 copy-start.8
  13.3 1.0 copy-start.4
  15.7 523.0 %all-gather.6.cloned.1.call-start = ((), (), s32[]{:S(2)}) async-start(), calls=%async_computation | async-start | bytes 34603008 | tf_op jit(solution)/shard_map/all_gather | solution.py:13
  17.1 286.6 %copy-start.24 = (f32[32]{0:T(128)}, f32[32]{0:T(128)S(1)}, u32[]{:S(2)}) copy-start(f32[32]{0:T(128)S(1)} %get-tuple-element.235) | copy-start | bytes 388
  252.6 46.3 %copy-start.7 = (bf16[1,256,128]{2,1,0:T(8,128)(2,1)S(1)}, bf16[1,256,128]{2,1,0:T(8,128)(2,1)}, u32[]{:S(2)}) copy-start(bf16[1,256,128]{2,1,0:T(8,128)(2,1)} %param.12) | copy-start | bytes 196612
  298.9 4.0 copy-start.23
  308.5 1.0 copy-start.2
  315.3 8.1 %copy-start.19 = (pred[256,256]{1,0:T(8,128)(4,1)}, pred[256,256]{1,0:T(8,128)(4,1)S(1)}, u32[]{:S(2)}) copy-start(pred[256,256]{1,0:T(8,128)(4,1)S(1)} %iota_compare_fusion) | copy-start | bytes 196612
  316.1 7.3 %copy-start.21 = (f32[32,256]{1,0:T(8,128)}, f32[32,256]{1,0:T(8,128)S(1)}, u32[]{:S(2)}) copy-start(f32[32,256]{1,0:T(8,128)S(1)} %bitcast_add_fusion.4) | copy-start | bytes 98308
  316.3 7.1 %copy-start.15 = (f32[256,256]{1,0:T(8,128)}, f32[256,256]{1,0:T(8,128)S(1)}, u32[]{:S(2)}) copy-start(f32[256,256]{1,0:T(8,128)S(1)} %fusion.35) | copy-start | bytes 786436
  316.3 13.3 %copy-start.29 = (f32[32]{0:T(128)S(1)}, f32[32]{0:T(128)}, u32[]{:S(2)}) copy-start(f32[32]{0:T(128)} %param.16) | copy-start | bytes 388
  329.6 3.9 copy-start.13
  538.8 1.2 copy-start.5
  539.0 2.2 copy-start.6
  540.0 3.1 copy-start.25
  540.0 3.1 copy-start.26
  541.1 2.0 copy-start.10
  541.1 2.0 copy-start.11
  541.1 7.5 %copy-start.9 = (bf16[256,256]{1,0:T(8,128)(2,1)S(1)}, bf16[256,256]{1,0:T(8,128)(2,1)}, u32[]{:S(2)}) copy-start(bf16[256,256]{1,0:T(8,128)(2,1)} %get-tuple-element.198) | copy-start | bytes 393220
  541.1 7.5 %copy-start.14 = (bf16[256,128]{1,0:T(8,128)(2,1)S(1)}, bf16[256,128]{1,0:T(8,128)(2,1)}, u32[]{:S(2)}) copy-start(bf16[256,128]{1,0:T(8,128)(2,1)} %fusion.16) | copy-start | bytes 196612
  541.1 8.3 %copy-start.1 = (bf16[1,256,2048]{1,2,0:T(8,128)(2,1)S(1)}, bf16[1,256,2048]{1,2,0:T(8,128)(2,1)}, u32[]{:S(2)}) copy-start(bf16[1,256,2048]{1,2,0:T(8,128)(2,1)} %copy.149) | copy-start | bytes 3145732
  541.2 8.3 %copy-start.17 = (f32[256,32]{0,1:T(8,128)S(1)}, f32[256,32]{0,1:T(8,128)}, u32[]{:S(2)}) copy-start(f32[256,32]{0,1:T(8,128)} %copy-done.16) | copy-start | bytes 98308
  541.2 8.3 %copy-start.20 = (pred[256,256]{1,0:T(8,128)(4,1)S(1)}, pred[256,256]{1,0:T(8,128)(4,1)}, u32[]{:S(2)}) copy-start(pred[256,256]{1,0:T(8,128)(4,1)} %copy-done.19) | copy-start | bytes 196612
  541.2 8.3 %copy-start.22 = (f32[32,256]{1,0:T(8,128)S(1)}, f32[32,256]{1,0:T(8,128)}, u32[]{:S(2)}) copy-start(f32[32,256]{1,0:T(8,128)} %copy-done.21) | copy-start | bytes 98308
  541.2 8.3 %copy-start.30 = (f32[32]{0:T(128)S(1)}, f32[32]{0:T(128)}, u32[]{:S(2)}) copy-start(f32[32]{0:T(128)} %param.16) | copy-start | bytes 388
  549.5 6.7 copy-start.18
  549.5 7.8 %copy-start.28 = (f32[32]{0:T(128)S(1)}, f32[32]{0:T(128)}, u32[]{:S(2)}) copy-start(f32[32]{0:T(128)} %reduce_sum.129) | copy-start | bytes 388
  (1 other events, 0.6 us)
Sparse Core Ops, SparseCore 0:
  15.8 236.6 all-gather.7
  311.7 226.9 all-gather.5
where the time goes:
time: 707 us; the launch traced here: 704 us
  waiting for transfers between devices  397 us (56%)
  blocking collectives  177 us (25%)
  other arithmetic  65.5 us (9%)
  matrix products  27.8 us (4%)
  local copies, waits for them, and re-layouts  21.1 us (3%)
  between operations  14.5 us (2%)
    all_gather x2, waiting for transfers between devices, entering(): gathered = jax.tree.map(lambda a: lax.all_gather(a, axis), part)  397 us
    psum x1, blocking collectives, shards(): lax.psum((alog_term, skip_term), ('dp', 'seq'))  140 us
    add x31, other arithmetic, combine(): later[0][:, None, None] * earlier[1] + later[1]  44.9 us
    all_gather x1, blocking collectives, entering(): gathered = jax.tree.map(lambda a: lax.all_gather(a, axis), part)  37 us
    dot_general x3, matrix products, piece_out(): jnp.einsum('htu,uhp->thp', weights, x_heads, preferred_element_type=jnp.f...  15.8 us
  transfers between devices with their start and end apart: 2, of which 2 were waited for; matrix products, arithmetic and copies ran while one was open for 4% of the time, Pallas kernels for 0%

commit v1 on v0

v1 whole, which is shorter than its diff:
```python
import jax
import jax.numpy as jnp
from jax import lax
from jax.experimental import pallas as pl
from jax.experimental.pallas import tpu as pltpu
from jax.sharding import PartitionSpec as P

GROUP = 256
HEADS = 32
SIZE = 64
STATE = 128
STEP = 8
WIDE = STEP * SIZE
GRID = HEADS // STEP
HALF = HEADS // 2
HALF_STEPS = GRID // 2
ROWS = SIZE + 8

F32 = jnp.float32
BF16 = jnp.bfloat16
EXACT = lax.Precision.HIGHEST
VMEM_LIMIT = 60 * 1024 * 1024


def dot(a, b, ca, cb, precision=None):
    return lax.dot_general(
        a, b, (((ca,), (cb,)), ((), ())), precision=precision, preferred_element_type=F32
    )


def iota(shape, dim):
    return lax.broadcasted_iota(jnp.int32, shape, dim)


def triangle():
    shape = (GROUP, GROUP)
    return jnp.where(iota(shape, 0) <= iota(shape, 1), 1.0, 0.0).astype(F32)


def column(row):
    shape = (HEADS, HEADS)
    eye = iota(shape, 0) == iota(shape, 1)
    return jnp.sum(jnp.where(eye, jnp.broadcast_to(row, shape), 0.0), axis=1, keepdims=True)


def as_row(col):
    shape = (HEADS, HEADS)
    eye = iota(shape, 0) == iota(shape, 1)
    return jnp.sum(jnp.where(eye, jnp.broadcast_to(col, shape), 0.0), axis=0, keepdims=True)


def spread(rows):
    return jnp.concatenate(
        [jnp.broadcast_to(rows[j : j + 1], (SIZE, GROUP)) for j in range(STEP)], axis=0
    )


def per_head(full):
    return jnp.concatenate(
        [
            jnp.sum(full[j * SIZE : (j + 1) * SIZE], axis=0, keepdims=True)
            for j in range(STEP)
        ],
        axis=0,
    )


def head_rows(step):
    return pl.ds(pl.multiple_of(step * STEP, STEP), STEP)


def keeps_adjoint(step):
    even = lax.rem(lax.axis_index("seq"), 2) == 0
    return even == (step < HALF_STEPS)


def unpaired(step):
    place = lax.axis_index("seq")
    edge = (place == 0) | (place == lax.axis_size("seq") - 1)
    return jnp.where(edge & (step >= HALF_STEPS), 0.0, 1.0).astype(F32)


def store_half(step, low_ref, high_ref, head, value):
    @pl.when(step < HALF_STEPS)
    def _():
        low_ref[head] = value

    @pl.when(step >= HALF_STEPS)
    def _():
        high_ref[head] = value


def states_kernel(
    x_ref, g_ref, b_ref, c_ref, dt_ref, alog_ref,
    low_ref, high_ref, keep_ref, xt_ref, gt_ref, cum_ref,
):
    step = pl.program_id(0)

    @pl.when(step == 0)
    def _():
        rate = jnp.exp(column(alog_ref[...]))
        cum_ref[...] = dot(-rate * dt_ref[...], triangle(), 1, 0, EXACT)

    cum = cum_ref[head_rows(step), :]
    last = cum[:, GROUP - 1 :]
    to_end = jnp.exp(last - cum)
    from_start = jnp.exp(cum)
    gain = jnp.exp(last)
    xt = x_ref[...].T
    gt = g_ref[...].T
    xt_ref[...] = xt
    gt_ref[...] = gt
    scaled = (xt.astype(F32) * spread(to_end)).astype(BF16)
    raised = (gt.astype(F32) * spread(from_start)).astype(BF16)
    state = dot(scaled, b_ref[...], 1, 0)
    adjoint = dot(raised, c_ref[...], 1, 0)
    first = keeps_adjoint(step)
    paired = unpaired(step)
    send = jnp.where(first, state, adjoint) * paired
    keep = jnp.where(first, adjoint, state)
    for j in range(STEP):
        store_half(step, low_ref, high_ref, j, send[j * SIZE : (j + 1) * SIZE])
        keep_ref[j, :SIZE, :] = keep[j * SIZE : (j + 1) * SIZE]
        keep_ref[j, SIZE:, :] = jnp.broadcast_to(gain[j : j + 1], (8, STATE))


def of_half(step, low_ref, high_ref, head):
    return jnp.where(step < HALF_STEPS, low_ref[head], high_ref[head])


def join_kernel(keep_ref, low_ref, high_ref, out_ref):
    step = pl.program_id(0)
    for j in range(STEP):
        other = of_half(step, low_ref, high_ref, j)
        out_ref[j, :SIZE, :] = keep_ref[j, :SIZE, :] + keep_ref[j, SIZE : SIZE + 1, :] * other
        out_ref[j, SIZE:, :] = keep_ref[j, SIZE:, :]


def scan_kernel(part_ref, out_ref):
    count = part_ref.shape[0]
    low = lax.axis_index("seq") < HALF

    def matrix(k):
        return part_ref[k, :SIZE, :]

    def gain(k):
        return part_ref[k, SIZE : SIZE + 1, :]

    def pair(first, second, carried, mine):
        return gain(first) * gain(second) * carried + matrix(mine)

    nothing = jnp.zeros((SIZE, STATE), F32)

    @pl.when(low)
    def _():
        state = nothing
        for k in range(0, count, 2):
            out_ref[k] = state
            state = pair(k, k + 1, state, k + 1)
        adjoint = nothing
        for k in reversed(range(0, count, 2)):
            out_ref[k + 1] = adjoint
            adjoint = pair(k, k + 1, adjoint, k)

    @pl.when(jnp.logical_not(low))
    def _():
        state = matrix(0)
        for k in range(1, count - 1, 2):
            out_ref[k] = state
            state = pair(k, k + 1, state, k + 1)
        out_ref[count - 1] = state
        adjoint = matrix(count - 1)
        for k in reversed(range(1, count - 1, 2)):
            out_ref[k + 1] = adjoint
            adjoint = pair(k, k + 1, adjoint, k)
        out_ref[0] = adjoint


def pass_on_kernel(mine_ref, low_ref, high_ref, cum_ref, out_low_ref, out_high_ref):
    step = pl.program_id(0)
    gain = jnp.exp(cum_ref[head_rows(step), :][:, GROUP - 1 :]) * unpaired(step)
    for j in range(STEP):
        sent = of_half(step, low_ref, high_ref, j)
        store_half(step, out_low_ref, out_high_ref, j, sent + gain[j : j + 1] * mine_ref[j])


def inner_kernel(
    g_ref, xt_ref, gt_ref, b_ref, c_ref, cum_ref, skip_ref,
    y_ref, gx_ref, row_ref, skiprow_ref, gb_ref, gc_ref,
    cb_s, acc_s,
):
    step = pl.program_id(0)
    half = GROUP // 2

    @pl.when(step == 0)
    def _():
        cb_s[...] = dot(c_ref[...], b_ref[...], 1, 1)
        acc_s[...] = jnp.zeros_like(acc_s)

    cum = cum_ref[head_rows(step), :]
    cum_t = cum.T
    square = (half, half)
    lower = iota(square, 0) >= iota(square, 1)
    nothing = jnp.zeros((SIZE, GROUP), BF16)
    for j in range(STEP):
        low, high = j * SIZE, (j + 1) * SIZE
        early, late = cum[j : j + 1, :half], cum[j : j + 1, half:]
        start, end = cum_t[:half, j : j + 1], cum_t[half:, j : j + 1]
        e00 = jnp.where(lower, jnp.exp(start - early), 0.0)
        e10 = jnp.exp(end - early)
        e11 = jnp.where(lower, jnp.exp(end - late), 0.0)
        w00 = (cb_s[:half, :half] * e00).astype(BF16)
        w10 = (cb_s[half:, :half] * e10).astype(BF16)
        w11 = (cb_s[half:, half:] * e11).astype(BF16)
        weights = jnp.concatenate(
            [
                jnp.concatenate([w00, jnp.zeros(square, BF16)], axis=1),
                jnp.concatenate([w10, w11], axis=1),
            ],
            axis=0,
        )
        xt = xt_ref[low:high, :]
        gt = gt_ref[low:high, :]
        yt = dot(xt, weights, 1, 1)
        gxt = dot(gt, weights, 1, 0)
        pair = (j // 2) * 2 * SIZE
        two = [xt, nothing] if j % 2 == 0 else [nothing, xt]
        gw = dot(g_ref[:, pair : pair + 2 * SIZE], jnp.concatenate(two, axis=0), 1, 0)
        acc_s[:half, :half] += gw[:half, :half] * e00
        acc_s[half:, :half] += gw[half:, :half] * e10
        acc_s[half:, half:] += gw[half:, half:] * e11
        xf = xt.astype(F32)
        gf = gt.astype(F32)
        row_ref[pl.ds(step * STEP + j, 1), :] = jnp.sum(gf * yt - xf * gxt, axis=0, keepdims=True)
        skiprow_ref[pl.ds(step * STEP + j, 1), :] = jnp.sum(gf * xf, axis=0, keepdims=True)
        skip = skip_ref[step * STEP + j]
        y_ref[low:high, :] = (yt + skip * xf).astype(BF16)
        gx_ref[low:high, :] = (gxt + skip * gf).astype(BF16)

    @pl.when(step == GRID - 1)
    def _():
        acc = acc_s[...].astype(BF16)
        gc_ref[...] = dot(acc, b_ref[...], 1, 0)
        gb_ref[...] = dot(acc, c_ref[...], 0, 0)


def outer_kernel(
    yt_ref, gxt_ref, xt_ref, gt_ref, mine_ref, low_ref, high_ref, b_ref, c_ref, cum_ref, row_ref, skiprow_ref,
    gbi_ref, gci_ref, dt_ref, alog_ref,
    y_ref, gx_ref, gb_ref, gc_ref, gdt_ref, sums_ref,
    row_s, gbt_s, gct_s,
):
    step = pl.program_id(0)

    @pl.when(step == 0)
    def _():
        gbt_s[...] = jnp.zeros_like(gbt_s)
        gct_s[...] = jnp.zeros_like(gct_s)

    cum = cum_ref[head_rows(step), :]
    last = cum[:, GROUP - 1 :]
    to_end = jnp.exp(last - cum)
    from_start = jnp.exp(cum)
    gain = jnp.exp(last)
    mine = jnp.concatenate([mine_ref[j] for j in range(STEP)], axis=0)
    other = jnp.concatenate([of_half(step, low_ref, high_ref, j) for j in range(STEP)], axis=0)
    first = keeps_adjoint(step)
    state_f = jnp.where(first, mine, other)
    adjoint_f = jnp.where(first, other, mine)
    product = state_f * adjoint_f
    product = jnp.concatenate(
        [
            jnp.sum(product[j * SIZE : (j + 1) * SIZE], axis=0, keepdims=True)
            for j in range(STEP)
        ],
        axis=0,
    )
    overlap = jnp.sum(product, axis=1, keepdims=True)
    state = state_f.astype(BF16)
    adjoint = adjoint_f.astype(BF16)
    xf = xt_ref[...].astype(F32)
    gf = gt_ref[...].astype(F32)
    start_w = spread(from_start)
    end_w = spread(to_end)
    carried = dot(state, c_ref[...], 1, 1) * start_w
    gscaled = dot(adjoint, b_ref[...], 1, 1) * end_w
    y_ref[...] = (yt_ref[...].astype(F32) + carried).astype(BF16).T
    gx_ref[...] = (gxt_ref[...].astype(F32) + gscaled).astype(BF16).T
    from_x = per_head(xf * gscaled)
    row = row_ref[head_rows(step), :] + per_head(gf * carried) - from_x
    glast = jnp.sum(from_x, axis=1, keepdims=True) + gain * overlap
    final = iota((STEP, GROUP), 1) == GROUP - 1
    row_s[head_rows(step), :] = row + jnp.where(final, glast, 0.0)
    gct_s[...] += dot(state, (gf * start_w).astype(BF16), 0, 0)
    gbt_s[...] += dot(adjoint, (xf * end_w).astype(BF16), 0, 0)

    @pl.when(step == GRID - 1)
    def _():
        gc_ref[...] = (gci_ref[...] + gct_s[...].T).astype(BF16)
        gb_ref[...] = (gbi_ref[...] + gbt_s[...].T).astype(BF16)
        rate = jnp.exp(column(alog_ref[...]))
        gla = dot(row_s[...], triangle(), 1, 1, EXACT)
        gdt = -rate * gla
        gdt_ref[...] = gdt
        alog = jnp.sum(gdt * dt_ref[...], axis=1, keepdims=True)
        skip = jnp.sum(skiprow_ref[...], axis=1, keepdims=True)
        sums_ref[...] = jnp.concatenate(
            [as_row(alog), as_row(skip), jnp.zeros((1, STATE - 2 * HEADS), F32)], axis=1
        )


def whole(shape):
    return pl.BlockSpec(shape, lambda i: (0,) * len(shape))


def shape_of(shape, dtype=F32):
    return jax.ShapeDtypeStruct(shape, dtype)


WIDE_T = pl.BlockSpec((WIDE, GROUP), lambda i: (i, 0))
WIDE_N = pl.BlockSpec((GROUP, WIDE), lambda i: (0, i))
STEP_SPEC = pl.BlockSpec((STEP, SIZE, STATE), lambda i: (i, 0, 0))
KEEP_SPEC = pl.BlockSpec((STEP, ROWS, STATE), lambda i: (i, 0, 0))
LOW_SPEC = pl.BlockSpec((STEP, SIZE, STATE), lambda i: (jnp.minimum(i, HALF_STEPS - 1), 0, 0))
HIGH_SPEC = pl.BlockSpec((STEP, SIZE, STATE), lambda i: (jnp.maximum(i - HALF_STEPS, 0), 0, 0))


def params(semantics=("arbitrary",)):
    return pltpu.CompilerParams(
        dimension_semantics=semantics, vmem_limit_bytes=VMEM_LIMIT
    )


def swap(low, high):
    count = lax.axis_size("seq")
    low_pairs = [(i, i ^ 1) for i in range(count)]
    high_pairs = [(i, ((i - 1 ^ 1) + 1) % count) for i in range(1, count)] + [(0, count - 1)]
    return lax.ppermute(low, "seq", low_pairs), lax.ppermute(high, "seq", high_pairs)


def shards(x_in, b_in, c_in, dt, a_log, skip, cotangent):
    x, b, c, g, steps = x_in[0], b_in[0], c_in[0], cotangent[0], dt[0]
    alog = a_log[None]
    feat = HEADS * SIZE
    narrow = whole((GROUP, STATE))
    heads = whole((HEADS, GROUP))
    row_spec = whole((1, HEADS))
    half = shape_of((HALF, SIZE, STATE))
    low, high, keep, xt, gt, cum = pl.pallas_call(
        states_kernel,
        grid=(GRID,),
        in_specs=[WIDE_N, WIDE_N, narrow, narrow, heads, row_spec],
        out_specs=[LOW_SPEC, HIGH_SPEC, KEEP_SPEC, WIDE_T, WIDE_T, heads],
        out_shape=[
            half,
            half,
            shape_of((HEADS, ROWS, STATE)),
            shape_of((feat, GROUP), BF16),
            shape_of((feat, GROUP), BF16),
            shape_of((HEADS, GROUP)),
        ],
        compiler_params=params(),
        name="states",
    )(x, g, b, c, steps, alog)
    low_in, high_in = swap(low, high)
    yt, gxt, row, skiprow, gbi, gci = pl.pallas_call(
        inner_kernel,
        grid=(GRID,),
        in_specs=[
            WIDE_N, WIDE_T, WIDE_T, narrow, narrow, heads,
            pl.BlockSpec(memory_space=pltpu.SMEM),
        ],
        out_specs=[WIDE_T, WIDE_T, heads, heads, narrow, narrow],
        out_shape=[
            shape_of((feat, GROUP), BF16),
            shape_of((feat, GROUP), BF16),
            shape_of((HEADS, GROUP)),
            shape_of((HEADS, GROUP)),
            shape_of((GROUP, STATE)),
            shape_of((GROUP, STATE)),
        ],
        scratch_shapes=[pltpu.VMEM((GROUP, GROUP), F32), pltpu.VMEM((GROUP, GROUP), F32)],
        compiler_params=params(),
        cost_estimate=pl.CostEstimate(
            flops=6 * HEADS * GROUP * GROUP * GROUP, bytes_accessed=5 << 20, transcendentals=2 << 20
        ),
        name="inner",
    )(g, xt, gt, b, c, cum, skip)
    joined = pl.pallas_call(
        join_kernel,
        grid=(GRID,),
        in_specs=[KEEP_SPEC, LOW_SPEC, HIGH_SPEC],
        out_specs=KEEP_SPEC,
        out_shape=shape_of((HEADS, ROWS, STATE)),
        compiler_params=params(),
        name="join",
    )(keep, low_in, high_in)
    parts = lax.all_to_all(joined, "seq", 0, 0, tiled=True)
    scanned = pl.pallas_call(
        scan_kernel,
        out_shape=shape_of((HEADS, SIZE, STATE)),
        compiler_params=params(None),
        name="scan",
    )(parts)
    mine = lax.all_to_all(scanned, "seq", 0, 0, tiled=True)
    low_out, high_out = pl.pallas_call(
        pass_on_kernel,
        grid=(GRID,),
        in_specs=[STEP_SPEC, LOW_SPEC, HIGH_SPEC, heads],
        out_specs=[LOW_SPEC, HIGH_SPEC],
        out_shape=[half, half],
        compiler_params=params(),
        name="pass_on",
    )(mine, low, high, cum)
    low_back, high_back = swap(low_out, high_out)
    y, gx, gb, gc, gdt, sums = pl.pallas_call(
        outer_kernel,
        grid=(GRID,),
        in_specs=[
            WIDE_T, WIDE_T, WIDE_T, WIDE_T, STEP_SPEC, LOW_SPEC, HIGH_SPEC,
            narrow, narrow, heads, heads, heads, narrow, narrow, heads, row_spec,
        ],
        out_specs=[WIDE_N, WIDE_N, narrow, narrow, heads, whole((1, STATE))],
        out_shape=[
            shape_of((GROUP, feat), BF16),
            shape_of((GROUP, feat), BF16),
            shape_of((GROUP, STATE), BF16),
            shape_of((GROUP, STATE), BF16),
            shape_of((HEADS, GROUP)),
            shape_of((1, STATE)),
        ],
        scratch_shapes=[
            pltpu.VMEM((HEADS, GROUP), F32),
            pltpu.VMEM((STATE, GROUP), F32),
            pltpu.VMEM((STATE, GROUP), F32),
        ],
        compiler_params=params(),
        name="outer",
    )(yt, gxt, xt, gt, mine, low_back, high_back, b, c, cum, row, skiprow, gbi, gci, steps, alog)
    everyone = lax.axis_size("dp") * lax.axis_size("seq")
    copies = jnp.broadcast_to(sums[None], (everyone, 1, STATE))
    total = jnp.sum(
        lax.all_to_all(copies, ("dp", "seq"), 0, 0, tiled=True), axis=(0, 1)
    )
    return (
        y[None], gx[None], gb[None], gc[None], gdt[None],
        total[:HEADS], total[HEADS : 2 * HEADS],
    )


def solution(mesh):
    placed = (
        P("dp", "seq", None),
        P("dp", "seq", None),
        P("dp", "seq", None),
        P("dp", None, "seq"),
        P(),
        P(),
        P("dp", "seq", None),
    )
    return jax.shard_map(
        shards,
        mesh=mesh,
        in_specs=placed,
        out_specs=(
            P("dp", "seq", None),
            P("dp", "seq", None),
            P("dp", "seq", None),
            P("dp", "seq", None),
            P("dp", None, "seq"),
            P(),
            P(),
        ),
        check_vma=False,
    )
```

time: 707 us -> 157 us (0.22)
  waiting for transfers between devices: 397 us -> 15 us
  blocking collectives: 177 us -> 91.2 us
  other arithmetic: 65.5 us -> 0.05 us
  Pallas kernels: 0 us -> 33.2 us
  matrix products: 27.8 us -> 0 us
  local copies, waits for them, and re-layouts: 21.1 us -> 2.92 us
  between operations: 14.5 us -> 0.67 us
  starting transfers between devices: 0.08 us -> 13.2 us
    all_gather x2 -> x0, waiting for transfers between devices: 397 us -> none  [entering(): gathered = jax.tree.map(lambda a: lax.all_gather(a, axis), part)]
    psum x1 -> x0, blocking collectives: 140 us -> none  [shards(): lax.psum((alog_term, skip_term), ('dp', 'seq'))]
    all_to_all x0 -> x3, blocking collectives: none -> 91.2 us  [the longest x1 34.8 us: shards(): parts = lax.all_to_all(joined, 'seq', 0, 0, tiled=True)]
    add x32 -> x0, other arithmetic: 46.2 us -> none  [the longest x31 44.9 us: combine(): later[0][:, None, None] * earlier[1] + later[1]]
    all_gather x1 -> x0, blocking collectives: 37 us -> none  [entering(): gathered = jax.tree.map(lambda a: lax.all_gather(a, axis), part)]
    pallas_call x0 -> x6, Pallas kernels: none -> 33.2 us  [the longest x1 7.41 us: shards(): pl.pallas_call(states_kernel, grid=(GRID,), in_specs=[WIDE_N, WIDE_N, nar...]
    dot_general x12 -> x0, matrix products: 27.8 us -> none  [the longest x3 15.8 us: piece_out(): jnp.einsum('htu,uhp->thp', weights, x_heads, preferred_element_type=jnp.f...]
    ppermute x0 -> x4, waiting for transfers between devices: none -> 15 us  [the longest x2 10.9 us: swap(): lax.ppermute(high, 'seq', high_pairs)]
  transfers between devices with their start and end apart: 2 -> 4, of which waited for: 2 -> 3; matrix products, arithmetic and copies ran while one was open for 4% -> 0% of each run, Pallas kernels for 0% -> 5%
where the time goes in v1:
time: 157 us; the launch traced here: 156 us
  blocking collectives  91.2 us (58%)
  Pallas kernels  33.2 us (21%)
  waiting for transfers between devices  15 us (10%)
  starting transfers between devices  13.2 us (8%)
  local copies, waits for them, and re-layouts  2.92 us (2%)
    all_to_all x1, blocking collectives, shards(): parts = lax.all_to_all(joined, 'seq', 0, 0, tiled=True)  34.8 us
    all_to_all x1, blocking collectives, shards(): mine = lax.all_to_all(scanned, 'seq', 0, 0, tiled=True)  31.4 us
    all_to_all x1, blocking collectives, shards(): lax.all_to_all(copies, ('dp', 'seq'), 0, 0, tiled=True)  24.9 us
    ppermute x2, waiting for transfers between devices, swap(): lax.ppermute(high, 'seq', high_pairs)  10.9 us
    ppermute x2, starting transfers between devices, swap(): lax.ppermute(high, 'seq', high_pairs)  8.3 us
    pallas_call x1, Pallas kernels, shards(): pl.pallas_call(states_kernel, grid=(GRID,), in_specs=[WIDE_N, WIDE_N, nar...  7.41 us
    pallas_call x1, Pallas kernels, shards(): pl.pallas_call(inner_kernel, grid=(GRID,), in_specs=[WIDE_N, WIDE_T, WIDE...  7.12 us
    pallas_call x1, Pallas kernels, shards(): pl.pallas_call(outer_kernel, grid=(GRID,), in_specs=[WIDE_T, WIDE_T, WIDE...  6.92 us
  transfers between devices with their start and end apart: 4, of which 3 were waited for; matrix products, arithmetic and copies ran while one was open for 0% of the time, Pallas kernels for 5%

profile of v1, /device:TPU:1, one launch (start us, length us, event | category | flops | bytes accessed | tf_op | source)
XLA Modules:
  0.0 156.2 jit_solution(4622485530255853523)
XLA Ops:
  0.6 7.4 %states.1 = (f32[16,64,128]{2,1,0:T(8,128)}, f32[16,64,128]{2,1,0:T(8,128)}, f32[32,72,128]{2,1,0:T(8,128)}, bf16[2048,256]{1,0:T(8,128)(2,1)}, bf16[2048,256]{1,0:T(8,128)(2,1)}, /*index=5*/f32[32,256]{1,0:T(8,128)}) custom-call(bf16[256,2048]{1,0:T(8,128)(2,1)} %bitcast.13, bf16[256,2048]{1,0:T(8,128)(2,1)} %bitcast.14, bf16[256,128]{1,0:T(8,128)(2,1)} %bitcast.17, ...), custom_call_target="tpu_custom_call" | custom-call | tf_op jit(solution)/shard_map/states/pallas_call | solution.py:349
  8.0 2.6 %collective-permute-start = (f32[16,64,128]{2,1,0:T(8,128)}, f32[16,64,128]{2,1,0:T(8,128)S(1)}, u32[]{:S(2)}, u32[]{:S(2)}) collective-permute-start(f32[16,64,128]{2,1,0:T(8,128)} %get-tuple-element.33.low_ref), channel_id=1, source_target_pairs={{0,1},{1,0},{2,3},{3,2},{4,5},{5,4},{6,7},{7,6},{8,9},{9,8},{10,11... | collective-permute-start | bytes 1572872 | tf_op jit(solution)/shard_map/ppermute | solution.py:338
  10.6 6.9 %collective-permute-start.1 = (f32[16,64,128]{2,1,0:T(8,128)}, f32[16,64,128]{2,1,0:T(8,128)S(1)}, u32[]{:S(2)}, u32[]{:S(2)}) collective-permute-start(f32[16,64,128]{2,1,0:T(8,128)} %get-tuple-element.34.high_ref), channel_id=1, source_target_pairs={{1,2},{2,1},{3,4},{4,3},{5,6},{6,5},{7,8},{8,7},{9,10},{10,9},{11,... | collective-permute-start | bytes 1572872 | tf_op jit(solution)/shard_map/ppermute | solution.py:338
  17.5 4.0 %collective-permute-done.low_ref = f32[16,64,128]{2,1,0:T(8,128)S(1)} collective-permute-done((f32[16,64,128]{2,1,0:T(8,128)}, f32[16,64,128]{2,1,0:T(8,128)S(1)}, u32[]{:S(2)}, u32[]{:S(2)}) %collective-permute-start) | collective-permute-done | bytes 524320 | tf_op jit(solution)/shard_map/ppermute | solution.py:338
  21.5 0.0 copy-start
  21.5 7.5 %collective-permute-done.1.high_ref = f32[16,64,128]{2,1,0:T(8,128)S(1)} collective-permute-done((f32[16,64,128]{2,1,0:T(8,128)}, f32[16,64,128]{2,1,0:T(8,128)S(1)}, u32[]{:S(2)}, u32[]{:S(2)}) %collective-permute-start.1) | collective-permute-done | bytes 524320 | tf_op jit(solution)/shard_map/ppermute | solution.py:338
  29.0 0.0 copy-start.1
  29.0 0.0 copy-done
  29.0 0.8 copy-done.1
  29.8 3.7 %join.1 = f32[32,72,128]{2,1,0:T(8,128)} custom-call(f32[32,72,128]{2,1,0:T(8,128)} %get-tuple-element.32.keep_ref, f32[16,64,128]{2,1,0:T(8,128)} %copy-done, f32[16,64,128]{2,1,0:T(8,128)} %copy-done.1), custom_call_target="tpu_custom_call" | custom-call | tf_op jit(solution)/shard_map/join/pallas_call | solution.py:389
  33.5 34.8 %all_to_all.15.part_ref = f32[32,72,128]{2,1,0:T(8,128)} all-to-all(f32[32,72,128]{2,1,0:T(8,128)} %join.1), channel_id=1, replica_groups=mesh['dp'=8,'seq'=32] {'seq'}, dimensions={0} | all-to-all | bytes 2359296 | tf_op jit(solution)/shard_map/all_to_all | solution.py:398
  68.3 2.3 %scan.1 = f32[32,64,128]{2,1,0:T(8,128)} custom-call(f32[32,72,128]{2,1,0:T(8,128)} %all_to_all.15.part_ref), custom_call_target="tpu_custom_call" | custom-call | tf_op jit(solution)/shard_map/scan/pallas_call | solution.py:399
  70.7 31.4 %all_to_all.16.mine_ref = f32[32,64,128]{2,1,0:T(8,128)} all-to-all(f32[32,64,128]{2,1,0:T(8,128)} %scan.1), channel_id=1, replica_groups=mesh['dp'=8,'seq'=32] {'seq'}, dimensions={0} | all-to-all | bytes 2097152 | tf_op jit(solution)/shard_map/all_to_all | solution.py:405
  102.1 5.7 %pass_on.1 = (f32[16,64,128]{2,1,0:T(8,128)}, f32[16,64,128]{2,1,0:T(8,128)}) custom-call(f32[32,64,128]{2,1,0:T(8,128)} %all_to_all.16.mine_ref, f32[16,64,128]{2,1,0:T(8,128)} %get-tuple-element.33.low_ref, f32[16,64,128]{2,1,0:T(8,128)} %get-tuple-element.34.high_ref, f32[32,256]{1,0:T(8,128)} %get-tuple-element.29.cum_ref), custom_call_target="tpu_custom_call" | custom-call | tf_op jit(solution)/shard_map/pass_on/pallas_call | solution.py:406
  107.8 2.4 %collective-permute-start.2 = (f32[16,64,128]{2,1,0:T(8,128)}, f32[16,64,128]{2,1,0:T(8,128)S(1)}, u32[]{:S(2)}, u32[]{:S(2)}) collective-permute-start(f32[16,64,128]{2,1,0:T(8,128)} %get-tuple-element.35), channel_id=1, source_target_pairs={{0,1},{1,0},{2,3},{3,2},{4,5},{5,4},{6,7},{7,6},{8,9},{9,8},{10,11... | collective-permute-start | bytes 1572872 | tf_op jit(solution)/shard_map/ppermute | solution.py:338
  110.2 1.4 collective-permute-start.3
  111.6 7.1 %inner.1 = (bf16[2048,256]{1,0:T(8,128)(2,1)}, bf16[2048,256]{1,0:T(8,128)(2,1)}, f32[32,256]{1,0:T(8,128)}, f32[32,256]{1,0:T(8,128)}, f32[256,128]{1,0:T(8,128)}, /*index=5*/f32[256,128]{1,0:T(8,128)}) custom-call(bf16[256,2048]{1,0:T(8,128)(2,1)} %bitcast.15, bf16[2048,256]{1,0:T(8,128)(2,1)} %get-tuple-element.27.xt_ref, ...), custom_call_target="tpu_custom_call" | custom-call | flops 3221225472 | bytes 5242880 | tf_op jit(solution)/shard_map/inner/pallas_call | solution.py:366
  118.7 0.0 collective-permute-done.2.low_ref
  118.7 0.0 copy-start.2
  118.7 3.4 %collective-permute-done.3.high_ref = f32[16,64,128]{2,1,0:T(8,128)S(1)} collective-permute-done((f32[16,64,128]{2,1,0:T(8,128)}, f32[16,64,128]{2,1,0:T(8,128)S(1)}, u32[]{:S(2)}, u32[]{:S(2)}) %collective-permute-start.3) | collective-permute-done | bytes 524320 | tf_op jit(solution)/shard_map/ppermute | solution.py:338
  122.2 0.0 copy-start.3
  122.2 0.0 copy-done.2
  122.2 0.8 copy-done.3
  123.0 6.9 %outer.1 = (bf16[256,2048]{1,0:T(8,128)(2,1)}, bf16[256,2048]{1,0:T(8,128)(2,1)}, bf16[256,128]{1,0:T(8,128)(2,1)}, bf16[256,128]{1,0:T(8,128)(2,1)}, f32[32,256]{1,0:T(8,128)}, /*index=5*/f32[1,128]{1,0:T(1,128)}) custom-call(bf16[2048,256]{1,0:T(8,128)(2,1)} %get-tuple-element.30.yt_ref, bf16[2048,256]{1,0:T(8,128)(2,1)} %get-tuple-element.31.gxt_ref, ...), custom_call_target="tpu_custom_call" | custom-call | tf_op jit(solution)/shard_map/outer/pallas_call | solution.py:416
  129.9 0.7 broadcast_in_dim.33
  130.6 24.9 %all_to_all.17 = f32[256,1,128]{2,1,0:T(1,128)S(1)} all-to-all(f32[256,1,128]{2,1,0:T(1,128)S(1)} %broadcast_in_dim.33), channel_id=1, replica_groups=mesh['dp'=8,'seq'=32] {'dp','seq'}, dimensions={0} | all-to-all | bytes 262144 | tf_op jit(solution)/shard_map/all_to_all | solution.py:443
  155.6 0.6 fusion
  (1 shorter events, 0.0 us)
Async XLA Ops:
  8.0 13.5 %collective-permute-start = (f32[16,64,128]{2,1,0:T(8,128)}, f32[16,64,128]{2,1,0:T(8,128)S(1)}, u32[]{:S(2)}, u32[]{:S(2)}) collective-permute-start(f32[16,64,128]{2,1,0:T(8,128)} %get-tuple-element.33.low_ref), channel_id=1, source_target_pairs={{0,1},{1,0},{2,3},{3,2},{4,5},{5,4},{6,7},{7,6},{8,9},{9,8},{10,11... | collective-permute-start | bytes 1572872 | tf_op jit(solution)/shard_map/ppermute | solution.py:338
  10.6 18.4 %collective-permute-start.1 = (f32[16,64,128]{2,1,0:T(8,128)}, f32[16,64,128]{2,1,0:T(8,128)S(1)}, u32[]{:S(2)}, u32[]{:S(2)}) collective-permute-start(f32[16,64,128]{2,1,0:T(8,128)} %get-tuple-element.34.high_ref), channel_id=1, source_target_pairs={{1,2},{2,1},{3,4},{4,3},{5,6},{6,5},{7,8},{8,7},{9,10},{10,9},{11,... | collective-permute-start | bytes 1572872 | tf_op jit(solution)/shard_map/ppermute | solution.py:338
  21.5 7.5 %copy-start = (f32[16,64,128]{2,1,0:T(8,128)}, f32[16,64,128]{2,1,0:T(8,128)S(1)}, u32[]{:S(2)}) copy-start(f32[16,64,128]{2,1,0:T(8,128)S(1)} %collective-permute-done.low_ref) | copy-start | bytes 1572868
  29.0 0.8 copy-start.1
  107.8 11.0 %collective-permute-start.2 = (f32[16,64,128]{2,1,0:T(8,128)}, f32[16,64,128]{2,1,0:T(8,128)S(1)}, u32[]{:S(2)}, u32[]{:S(2)}) collective-permute-start(f32[16,64,128]{2,1,0:T(8,128)} %get-tuple-element.35), channel_id=1, source_target_pairs={{0,1},{1,0},{2,3},{3,2},{4,5},{5,4},{6,7},{7,6},{8,9},{9,8},{10,11... | collective-permute-start | bytes 1572872 | tf_op jit(solution)/shard_map/ppermute | solution.py:338
  110.2 12.0 %collective-permute-start.3 = (f32[16,64,128]{2,1,0:T(8,128)}, f32[16,64,128]{2,1,0:T(8,128)S(1)}, u32[]{:S(2)}, u32[]{:S(2)}) collective-permute-start(f32[16,64,128]{2,1,0:T(8,128)} %get-tuple-element.36), channel_id=1, source_target_pairs={{1,2},{2,1},{3,4},{4,3},{5,6},{6,5},{7,8},{8,7},{9,10},{10,9},{11,... | collective-permute-start | bytes 1572872 | tf_op jit(solution)/shard_map/ppermute | solution.py:338
  118.7 3.4 %copy-start.2 = (f32[16,64,128]{2,1,0:T(8,128)}, f32[16,64,128]{2,1,0:T(8,128)S(1)}, u32[]{:S(2)}) copy-start(f32[16,64,128]{2,1,0:T(8,128)S(1)} %collective-permute-done.2.low_ref) | copy-start | bytes 1572868
  122.2 0.8 copy-start.3

commit v2 on v0

v2 whole, which is shorter than its diff:
```python
import jax
import jax.numpy as jnp
from jax import lax
from jax.experimental import pallas as pl
from jax.experimental.pallas import tpu as pltpu
from jax.sharding import PartitionSpec as P

GROUP = 256
HEADS = 32
SIZE = 64
STATE = 128
STEP = 8
WIDE = STEP * SIZE
GRID = HEADS // STEP
HALF = HEADS // 2
HALF_STEPS = GRID // 2

F32 = jnp.float32
BF16 = jnp.bfloat16
EXACT = lax.Precision.HIGHEST
VMEM_LIMIT = 24 * 1024 * 1024


def dot(a, b, ca, cb, precision=None):
    return lax.dot_general(
        a, b, (((ca,), (cb,)), ((), ())), precision=precision, preferred_element_type=F32
    )


def iota(shape, dim):
    return lax.broadcasted_iota(jnp.int32, shape, dim)


def triangle():
    shape = (GROUP, GROUP)
    return jnp.where(iota(shape, 0) <= iota(shape, 1), 1.0, 0.0).astype(F32)


def column(row):
    shape = (HEADS, HEADS)
    eye = iota(shape, 0) == iota(shape, 1)
    return jnp.sum(jnp.where(eye, jnp.broadcast_to(row, shape), 0.0), axis=1, keepdims=True)


def as_row(col):
    shape = (HEADS, HEADS)
    eye = iota(shape, 0) == iota(shape, 1)
    return jnp.sum(jnp.where(eye, jnp.broadcast_to(col, shape), 0.0), axis=0, keepdims=True)


def spread(rows):
    return jnp.concatenate(
        [jnp.broadcast_to(rows[j : j + 1], (SIZE, GROUP)) for j in range(STEP)], axis=0
    )


def per_head(full):
    return jnp.concatenate(
        [
            jnp.sum(full[j * SIZE : (j + 1) * SIZE], axis=0, keepdims=True)
            for j in range(STEP)
        ],
        axis=0,
    )


def head_rows(step):
    return pl.ds(pl.multiple_of(step * STEP, STEP), STEP)


def keeps_adjoint(step):
    even = lax.rem(lax.axis_index("seq"), 2) == 0
    return even == (step < HALF_STEPS)


def unpaired(step):
    place = lax.axis_index("seq")
    edge = (place == 0) | (place == lax.axis_size("seq") - 1)
    return jnp.where(edge & (step >= HALF_STEPS), 0.0, 1.0).astype(F32)


def states_kernel(
    x_hbm, g_hbm, b_hbm, c_hbm, dt_hbm, alog_hbm,
    low_ref, high_ref, keep_ref, gain_ref, xt_ref, gt_ref, cum_ref,
    x_s, g_s, b_s, c_s, dt_s, alog_s, sems,
):
    def copy(source, target, slot):
        made = pltpu.make_async_copy(source, target, sems.at[slot])
        made.start()
        return made

    alog_copy = copy(alog_hbm, alog_s, 0)
    dt_copy = copy(dt_hbm, dt_s, 1)
    b_copy = copy(b_hbm, b_s, 2)
    c_copy = copy(c_hbm, c_s, 3)
    inputs = []
    for i in range(GRID):
        lanes = pl.ds(i * WIDE, WIDE)
        inputs.append(
            (
                copy(x_hbm.at[:, lanes], x_s.at[i], 4 + 2 * i),
                copy(g_hbm.at[:, lanes], g_s.at[i], 5 + 2 * i),
            )
        )
    alog_copy.wait()
    dt_copy.wait()
    rate = jnp.exp(column(alog_s[...]))
    cum_all = dot(-rate * dt_s[...], triangle(), 1, 0, EXACT)
    cum_ref[...] = cum_all
    b_copy.wait()
    c_copy.wait()
    for i in range(GRID):
        for made in inputs[i]:
            made.wait()
        cum = cum_all[i * STEP : (i + 1) * STEP]
        last = cum[:, GROUP - 1 :]
        to_end = jnp.exp(last - cum)
        from_start = jnp.exp(cum)
        gain = jnp.exp(last)
        xt = x_s[i].T
        gt = g_s[i].T
        rows = pl.ds(i * WIDE, WIDE)
        xt_ref[rows, :] = xt
        gt_ref[rows, :] = gt
        scaled = (xt.astype(F32) * spread(to_end)).astype(BF16)
        raised = (gt.astype(F32) * spread(from_start)).astype(BF16)
        state = dot(scaled, b_s[...], 1, 0)
        adjoint = dot(raised, c_s[...], 1, 0)
        first = keeps_adjoint(i)
        send = jnp.where(first, state, adjoint) * unpaired(i)
        keep = jnp.where(first, adjoint, state)
        send_ref = low_ref if i < HALF_STEPS else high_ref
        base = i % HALF_STEPS * STEP
        for j in range(STEP):
            part = slice(j * SIZE, (j + 1) * SIZE)
            send_ref[base + j] = send[part]
            keep_ref[i * STEP + j] = keep[part]
            gain_ref[i * STEP + j] = jnp.broadcast_to(gain[j : j + 1], (1, STATE))


def join_kernel(keep_ref, low_ref, high_ref, cum_ref, out_ref):
    gain = jnp.exp(cum_ref[:, GROUP - 1 :])
    for h in range(HEADS):
        other = low_ref[h] if h < HALF else high_ref[h - HALF]
        out_ref[h] = keep_ref[h] + gain[h : h + 1] * other


def scan_kernel(part_ref, gain_ref, out_ref):
    count = part_ref.shape[0]
    low = lax.axis_index("seq") < HALF

    def pair(first, second, carried, mine):
        return gain_ref[first] * gain_ref[second] * carried + part_ref[mine]

    nothing = jnp.zeros((SIZE, STATE), F32)

    @pl.when(low)
    def _():
        state = nothing
        for k in range(0, count, 2):
            out_ref[k] = state
            state = pair(k, k + 1, state, k + 1)
        adjoint = nothing
        for k in reversed(range(0, count, 2)):
            out_ref[k + 1] = adjoint
            adjoint = pair(k, k + 1, adjoint, k)

    @pl.when(jnp.logical_not(low))
    def _():
        state = part_ref[0]
        for k in range(1, count - 1, 2):
            out_ref[k] = state
            state = pair(k, k + 1, state, k + 1)
        out_ref[count - 1] = state
        adjoint = part_ref[count - 1]
        for k in reversed(range(1, count - 1, 2)):
            out_ref[k + 1] = adjoint
            adjoint = pair(k, k + 1, adjoint, k)
        out_ref[0] = adjoint


def pass_on_kernel(mine_ref, low_ref, high_ref, cum_ref, out_low_ref, out_high_ref):
    gain = jnp.exp(cum_ref[:, GROUP - 1 :])
    low_gain = gain[:HALF] * unpaired(0)
    high_gain = gain[HALF:] * unpaired(GRID - 1)
    for h in range(HALF):
        out_low_ref[h] = low_ref[h] + low_gain[h : h + 1] * mine_ref[h]
        out_high_ref[h] = high_ref[h] + high_gain[h : h + 1] * mine_ref[HALF + h]


def inner_kernel(
    g_ref, xt_ref, gt_ref, b_ref, c_ref, cum_ref, skip_ref,
    y_ref, gx_ref, row_ref, skiprow_ref, gb_ref, gc_ref,
    cb_s, acc_s,
):
    half = GROUP // 2
    cb_s[...] = dot(c_ref[...], b_ref[...], 1, 1)
    acc_s[...] = jnp.zeros_like(acc_s)
    square = (half, half)
    lower = iota(square, 0) >= iota(square, 1)
    nothing = jnp.zeros((SIZE, GROUP), BF16)

    def some_heads(step, carry):
        cum = cum_ref[head_rows(step), :]
        cum_t = cum.T
        rows = []
        skips = []
        for j in range(STEP):
            early, late = cum[j : j + 1, :half], cum[j : j + 1, half:]
            start, end = cum_t[:half, j : j + 1], cum_t[half:, j : j + 1]
            e00 = jnp.where(lower, jnp.exp(start - early), 0.0)
            e10 = jnp.exp(end - early)
            e11 = jnp.where(lower, jnp.exp(end - late), 0.0)
            w00 = (cb_s[:half, :half] * e00).astype(BF16)
            w10 = (cb_s[half:, :half] * e10).astype(BF16)
            w11 = (cb_s[half:, half:] * e11).astype(BF16)
            weights = jnp.concatenate(
                [
                    jnp.concatenate([w00, jnp.zeros(square, BF16)], axis=1),
                    jnp.concatenate([w10, w11], axis=1),
                ],
                axis=0,
            )
            features = pl.ds(pl.multiple_of(step * WIDE + j * SIZE, SIZE), SIZE)
            xt = xt_ref[features, :]
            gt = gt_ref[features, :]
            yt = dot(xt, weights, 1, 1)
            gxt = dot(gt, weights, 1, 0)
            pair = pl.ds(pl.multiple_of(step * WIDE + j // 2 * 2 * SIZE, 2 * SIZE), 2 * SIZE)
            two = [xt, nothing] if j % 2 == 0 else [nothing, xt]
            gw = dot(g_ref[:, pair], jnp.concatenate(two, axis=0), 1, 0)
            acc_s[:half, :half] += gw[:half, :half] * e00
            acc_s[half:, :half] += gw[half:, :half] * e10
            acc_s[half:, half:] += gw[half:, half:] * e11
            xf = xt.astype(F32)
            gf = gt.astype(F32)
            rows.append(jnp.sum(gf * yt - xf * gxt, axis=0, keepdims=True))
            skips.append(jnp.sum(gf * xf, axis=0, keepdims=True))
            skip = skip_ref[step * STEP + j]
            y_ref[features, :] = (yt + skip * xf).astype(BF16)
            gx_ref[features, :] = (gxt + skip * gf).astype(BF16)
        row_ref[head_rows(step), :] = jnp.concatenate(rows, axis=0)
        skiprow_ref[head_rows(step), :] = jnp.concatenate(skips, axis=0)
        return carry

    lax.fori_loop(0, GRID, some_heads, 0)
    acc = acc_s[...].astype(BF16)
    gc_ref[...] = dot(acc, b_ref[...], 1, 0)
    gb_ref[...] = dot(acc, c_ref[...], 0, 0)


def halves(own):
    even = lax.rem(lax.axis_index("seq"), 2) == 0
    state_low = even == own
    state = jnp.where(state_low, 0, HALF_STEPS)
    return state_low, state, HALF_STEPS - state


def feature_rows(step):
    return pl.ds(pl.multiple_of(step * WIDE, WIDE), WIDE)


def take(ref, step):
    full = ref[pl.ds(pl.multiple_of(step * STEP, STEP), STEP)]
    return full.reshape(WIDE, STATE).astype(BF16)


def take_half(low_ref, high_ref, low, i):
    part = pl.ds(i * STEP, STEP)
    return jnp.where(low, low_ref[part], high_ref[part]).reshape(WIDE, STATE).astype(BF16)


def carried_rows(state, gt_ref, c_ref, cum_ref, step):
    from_start = jnp.exp(cum_ref[head_rows(step), :])
    gf = gt_ref[feature_rows(step), :].astype(F32)
    raw = dot(state, c_ref[...], 1, 1)
    return raw, gf, from_start, per_head(gf * raw) * from_start


def scaled_rows(adjoint, xt_ref, b_ref, cum_ref, step):
    cum = cum_ref[head_rows(step), :]
    to_end = jnp.exp(cum[:, GROUP - 1 :] - cum)
    xf = xt_ref[feature_rows(step), :].astype(F32)
    raw = dot(adjoint, b_ref[...], 1, 1)
    from_x = per_head(xf * raw) * to_end
    final = iota((STEP, GROUP), 1) == GROUP - 1
    total = jnp.sum(from_x, axis=1, keepdims=True)
    return raw, xf, to_end, jnp.where(final, total, 0.0) - from_x


def give_out(
    i, state_step, adjoint_step, state, adjoint, raws,
    yt_ref, gxt_ref, y_hbm, gx_hbm, out_s, sems, gct, gbt,
):
    raw, gf, from_start, back, xf, to_end = raws
    start_w = spread(from_start)
    end_w = spread(to_end)
    y = yt_ref[feature_rows(state_step), :].astype(F32) + raw * start_w
    out_s[2 * i] = y.astype(BF16).T
    gx = gxt_ref[feature_rows(adjoint_step), :].astype(F32) + back * end_w
    out_s[2 * i + 1] = gx.astype(BF16).T
    copies = []
    for slot, step, target in ((2 * i, state_step, y_hbm), (2 * i + 1, adjoint_step, gx_hbm)):
        lanes = pl.ds(pl.multiple_of(step * WIDE, WIDE), WIDE)
        made = pltpu.make_async_copy(out_s.at[slot], target.at[:, lanes], sems.at[slot])
        made.start()
        copies.append(made)
    gct = gct + dot(state, (gf * start_w).astype(BF16), 0, 0)
    gbt = gbt + dot(adjoint, (xf * end_w).astype(BF16), 0, 0)
    return gct, gbt, copies


def own_kernel(
    mine_ref, yt_ref, gxt_ref, xt_ref, gt_ref, b_ref, c_ref, cum_ref,
    y_hbm, gx_hbm, row_ref, gct_ref, gbt_ref,
    out_s, sems,
):
    _, state_first, adjoint_first = halves(True)
    gct = jnp.zeros((STATE, GROUP), F32)
    gbt = jnp.zeros((STATE, GROUP), F32)
    copies = []
    for i in range(HALF_STEPS):
        state_step, adjoint_step = state_first + i, adjoint_first + i
        state = take(mine_ref, state_step)
        adjoint = take(mine_ref, adjoint_step)
        raw, gf, from_start, row = carried_rows(state, gt_ref, c_ref, cum_ref, state_step)
        row_ref[head_rows(state_step), :] = row
        back, xf, to_end, row = scaled_rows(adjoint, xt_ref, b_ref, cum_ref, adjoint_step)
        row_ref[head_rows(adjoint_step), :] = row
        gct, gbt, made = give_out(
            i, state_step, adjoint_step, state, adjoint, (raw, gf, from_start, back, xf, to_end),
            yt_ref, gxt_ref, y_hbm, gx_hbm, out_s, sems, gct, gbt,
        )
        copies += made
    gct_ref[...] = gct
    gbt_ref[...] = gbt
    for made in copies:
        made.wait()


def sums_kernel(
    mine_ref, low_ref, high_ref, xt_ref, gt_ref, b_ref, c_ref, cum_ref, row_ref, own_row_ref,
    skiprow_ref, dt_ref, alog_ref,
    gdt_ref, sums_ref,
    row_s,
):
    state_low, state_first, adjoint_first = halves(False)
    for i in range(HALF_STEPS):
        state = take_half(low_ref, high_ref, state_low, i)
        adjoint = take_half(high_ref, low_ref, state_low, i)
        row_s[head_rows(state_first + i), :] = carried_rows(
            state, gt_ref, c_ref, cum_ref, state_first + i
        )[-1]
        row_s[head_rows(adjoint_first + i), :] = scaled_rows(
            adjoint, xt_ref, b_ref, cum_ref, adjoint_first + i
        )[-1]
    overlap = jnp.concatenate(
        [
            jnp.sum(mine_ref[:HALF] * low_ref[...], axis=1),
            jnp.sum(mine_ref[HALF:] * high_ref[...], axis=1),
        ],
        axis=0,
    )
    overlap = jnp.sum(overlap, axis=1, keepdims=True) * jnp.exp(cum_ref[:, GROUP - 1 :])
    final = iota((HEADS, GROUP), 1) == GROUP - 1
    row = row_ref[...] + own_row_ref[...] + row_s[...] + jnp.where(final, overlap, 0.0)
    gdt = -jnp.exp(column(alog_ref[...])) * dot(row, triangle(), 1, 1, EXACT)
    gdt_ref[...] = gdt
    alog = jnp.sum(gdt * dt_ref[...], axis=1, keepdims=True)
    skip = jnp.sum(skiprow_ref[...], axis=1, keepdims=True)
    sums = jnp.concatenate(
        [as_row(alog), as_row(skip), jnp.zeros((1, STATE - 2 * HEADS), F32)], axis=1
    )
    sums_ref[...] = jnp.broadcast_to(sums[None], sums_ref.shape)


def other_kernel(
    low_ref, high_ref, yt_ref, gxt_ref, xt_ref, gt_ref, b_ref, c_ref, cum_ref,
    gct_ref, gbt_ref, gci_ref, gbi_ref, y_in, gx_in,
    y_hbm, gx_hbm, gc_ref, gb_ref,
    out_s, sems,
):
    state_low, state_first, adjoint_first = halves(False)
    gct = gct_ref[...]
    gbt = gbt_ref[...]
    copies = []
    for i in range(HALF_STEPS):
        state_step, adjoint_step = state_first + i, adjoint_first + i
        state = take_half(low_ref, high_ref, state_low, i)
        adjoint = take_half(high_ref, low_ref, state_low, i)
        raw, gf, from_start, _ = carried_rows(state, gt_ref, c_ref, cum_ref, state_step)
        back, xf, to_end, _ = scaled_rows(adjoint, xt_ref, b_ref, cum_ref, adjoint_step)
        gct, gbt, made = give_out(
            i, state_step, adjoint_step, state, adjoint, (raw, gf, from_start, back, xf, to_end),
            yt_ref, gxt_ref, y_hbm, gx_hbm, out_s, sems, gct, gbt,
        )
        copies += made
    gc_ref[...] = (gci_ref[...] + gct.T).astype(BF16)
    gb_ref[...] = (gbi_ref[...] + gbt.T).astype(BF16)
    for made in copies:
        made.wait()


def shape_of(shape, dtype=F32):
    return jax.ShapeDtypeStruct(shape, dtype)


def call(kernel, name, out_shape, out_specs=None, cost=None, limit=VMEM_LIMIT, **more):
    if out_specs is not None:
        more["out_specs"] = out_specs
    return pl.pallas_call(
        kernel,
        out_shape=out_shape,
        compiler_params=pltpu.CompilerParams(vmem_limit_bytes=limit),
        cost_estimate=cost,
        name=name,
        **more,
    )


def cost(us):
    return pl.CostEstimate(flops=us * 500_000_000, bytes_accessed=us << 21, transcendentals=0)


def swap(low, high):
    count = lax.axis_size("seq")
    low_pairs = [(i, i ^ 1) for i in range(count)]
    high_pairs = [(i, ((i - 1 ^ 1) + 1) % count) for i in range(1, count)] + [(0, count - 1)]
    return lax.ppermute(low, "seq", low_pairs), lax.ppermute(high, "seq", high_pairs)


def shards(x_in, b_in, c_in, dt, a_log, skip, cotangent):
    x, b, c, g, steps = x_in[0], b_in[0], c_in[0], cotangent[0], dt[0]
    alog = a_log[None]
    feat = HEADS * SIZE
    vmem = pl.BlockSpec(memory_space=pltpu.VMEM)
    hbm = pl.BlockSpec(memory_space=pltpu.HBM)
    half = shape_of((HALF, SIZE, STATE))
    all_heads = shape_of((HEADS, SIZE, STATE))
    wide = shape_of((feat, GROUP), BF16)
    tall = shape_of((GROUP, feat), BF16)
    rows = shape_of((HEADS, GROUP))
    low, high, keep, gain, xt, gt, cum = call(
        states_kernel,
        "states",
        [half, half, all_heads, shape_of((HEADS, 1, STATE)), wide, wide, rows],
        in_specs=[hbm] * 6,
        scratch_shapes=[
            pltpu.VMEM((GRID, GROUP, WIDE), BF16),
            pltpu.VMEM((GRID, GROUP, WIDE), BF16),
            pltpu.VMEM((GROUP, STATE), BF16),
            pltpu.VMEM((GROUP, STATE), BF16),
            pltpu.VMEM((HEADS, GROUP), F32),
            pltpu.VMEM((1, HEADS), F32),
            pltpu.SemaphoreType.DMA((4 + 2 * GRID,)),
        ],
        limit=60 * 1024 * 1024,
    )(x, g, b, c, steps, alog)
    low_in, high_in = swap(low, high)
    gains = lax.all_to_all(gain, "seq", 0, 0, tiled=True)
    yt, gxt, row, skiprow, gbi, gci = call(
        inner_kernel,
        "inner",
        [wide, wide, rows, rows, shape_of((GROUP, STATE)), shape_of((GROUP, STATE))],
        in_specs=[vmem] * 6 + [pl.BlockSpec(memory_space=pltpu.SMEM)],
        scratch_shapes=[pltpu.VMEM((GROUP, GROUP), F32), pltpu.VMEM((GROUP, GROUP), F32)],
        cost=cost(6),
    )(g, xt, gt, b, c, cum, skip)
    low_in, high_in, gains, row = lax.optimization_barrier((low_in, high_in, gains, row))
    joined = call(join_kernel, "join", all_heads)(keep, low_in, high_in, cum)
    parts = lax.all_to_all(joined, "seq", 0, 0, tiled=True)
    scanned = call(scan_kernel, "scan", all_heads)(parts, gains)
    mine = lax.all_to_all(scanned, "seq", 0, 0, tiled=True)
    low_out, high_out = call(pass_on_kernel, "pass_on", [half, half])(mine, low, high, cum)
    low_back, high_back = swap(low_out, high_out)
    out_scratch = [
        pltpu.VMEM((2 * HALF_STEPS, GROUP, WIDE), BF16),
        pltpu.SemaphoreType.DMA((2 * HALF_STEPS,)),
    ]
    part = shape_of((STATE, GROUP))
    y, gx, own_row, gct, gbt = call(
        own_kernel,
        "own",
        [tall, tall, rows, part, part],
        [hbm, hbm, vmem, vmem, vmem],
        scratch_shapes=out_scratch,
        cost=cost(4),
    )(mine, yt, gxt, xt, gt, b, c, cum)
    everyone = lax.axis_size("dp") * lax.axis_size("seq")
    gdt, copies = call(
        sums_kernel,
        "sums",
        [rows, shape_of((everyone, 1, STATE))],
        scratch_shapes=[pltpu.VMEM((HEADS, GROUP), F32)],
    )(mine, low_back, high_back, xt, gt, b, c, cum, row, own_row, skiprow, steps, alog)
    sums = lax.all_to_all(copies, ("dp", "seq"), 0, 0, tiled=True)
    y, gx, gc, gb = call(
        other_kernel,
        "other",
        [tall, tall, shape_of((GROUP, STATE), BF16), shape_of((GROUP, STATE), BF16)],
        [hbm, hbm, vmem, vmem],
        in_specs=[vmem] * 13 + [hbm, hbm],
        input_output_aliases={13: 0, 14: 1},
        scratch_shapes=out_scratch,
        cost=cost(4),
    )(low_back, high_back, yt, gxt, xt, gt, b, c, cum, gct, gbt, gci, gbi, y, gx)
    total = jnp.sum(sums, axis=(0, 1))
    return (
        y[None], gx[None], gb[None], gc[None], gdt[None],
        total[:HEADS], total[HEADS : 2 * HEADS],
    )


def solution(mesh):
    placed = (
        P("dp", "seq", None),
        P("dp", "seq", None),
        P("dp", "seq", None),
        P("dp", None, "seq"),
        P(),
        P(),
        P("dp", "seq", None),
    )
    return jax.shard_map(
        shards,
        mesh=mesh,
        in_specs=placed,
        out_specs=(
            P("dp", "seq", None),
            P("dp", "seq", None),
            P("dp", "seq", None),
            P("dp", "seq", None),
            P("dp", None, "seq"),
            P(),
            P(),
        ),
        check_vma=False,
    )
```

time: 707 us -> 145 us (0.21)
  waiting for transfers between devices: 397 us -> 14.5 us
  blocking collectives: 177 us -> 66.9 us
  other arithmetic: 65.5 us -> 1.19 us
  starting transfers between devices: 0.08 us -> 31.5 us
  matrix products: 27.8 us -> 0 us
  Pallas kernels: 0 us -> 16.4 us
  between operations: 14.5 us -> 0.87 us
  local copies, waits for them, and re-layouts: 21.1 us -> 12.8 us
    all_gather x2 -> x0, waiting for transfers between devices: 397 us -> none  [entering(): gathered = jax.tree.map(lambda a: lax.all_gather(a, axis), part)]
    psum x1 -> x0, blocking collectives: 140 us -> none  [shards(): lax.psum((alog_term, skip_term), ('dp', 'seq'))]
    all_to_all x0 -> x2, blocking collectives: none -> 66.9 us  [the longest x1 33.5 us: shards(): parts = lax.all_to_all(joined, 'seq', 0, 0, tiled=True)]
    add x32 -> x0, other arithmetic: 46.2 us -> none  [the longest x31 44.9 us: combine(): later[0][:, None, None] * earlier[1] + later[1]]
    all_gather x1 -> x0, blocking collectives: 37 us -> none  [entering(): gathered = jax.tree.map(lambda a: lax.all_gather(a, axis), part)]
    dot_general x12 -> x0, matrix products: 27.8 us -> none  [the longest x3 15.8 us: piece_out(): jnp.einsum('htu,uhp->thp', weights, x_heads, preferred_element_type=jnp.f...]
    all_to_all x0 -> x2, starting transfers between devices: none -> 17.7 us  [the longest x1 13.9 us: shards(): sums = lax.all_to_all(copies, ('dp', 'seq'), 0, 0, tiled=True)]
    pallas_call x0 -> x8, Pallas kernels: none -> 16.4 us  [the longest x1 5.45 us: shards(): call(inner_kernel, 'inner', [wide, wide, rows, rows, shape_of((GROUP, STA...]
  transfers between devices with their start and end apart: 2 -> 6, of which waited for: 2 -> 3; matrix products, arithmetic and copies ran while one was open for 4% -> 0% of each run, Pallas kernels for 0% -> 7%
where the time goes in v2:
time: 145 us; the launch traced here: 144 us
  blocking collectives  66.9 us (46%)
  starting transfers between devices  31.5 us (22%)
  Pallas kernels  16.4 us (11%)
  waiting for transfers between devices  14.5 us (10%)
  local copies, waits for them, and re-layouts  12.8 us (9%)
    all_to_all x1, blocking collectives, shards(): parts = lax.all_to_all(joined, 'seq', 0, 0, tiled=True)  33.5 us
    all_to_all x1, blocking collectives, shards(): mine = lax.all_to_all(scanned, 'seq', 0, 0, tiled=True)  33.3 us
    all_to_all x1, starting transfers between devices, shards(): sums = lax.all_to_all(copies, ('dp', 'seq'), 0, 0, tiled=True)  13.9 us
    unnamed x54, local copies, waits for them, and re-layouts  12.2 us
    ppermute x2, starting transfers between devices, swap(): lax.ppermute(high, 'seq', high_pairs)  8.42 us
    pallas_call x1, Pallas kernels, shards(): call(inner_kernel, 'inner', [wide, wide, rows, rows, shape_of((GROUP, STA...  5.45 us
    ppermute x2, starting transfers between devices, swap(): lax.ppermute(low, 'seq', low_pairs)  5.29 us
    all_to_all x1, waiting for transfers between devices, shards(): sums = lax.all_to_all(copies, ('dp', 'seq'), 0, 0, tiled=True)  5.12 us
  transfers between devices with their start and end apart: 6, of which 3 were waited for; matrix products, arithmetic and copies ran while one was open for 0% of the time, Pallas kernels for 7%

profile of v2, /device:TPU:1, one launch (start us, length us, event | category | flops | bytes accessed | tf_op | source)
XLA Modules:
  0.0 144.0 jit_solution(8614344781424671830)
XLA Ops:
  0.7 4.6 %states.1 = (f32[16,64,128]{2,1,0:T(8,128)}, f32[16,64,128]{2,1,0:T(8,128)}, f32[32,64,128]{2,1,0:T(8,128)}, f32[32,1,128]{2,1,0:T(1,128)}, bf16[2048,256]{1,0:T...) custom-call(bf16[256,2048]{1,0:T(8,128)(2,1)} %bitcast.29, bf16[256,2048]{1,0:T(8,128)(2,1)} %bitcast.11, ...), custom_call_target="tpu_custom_call" | custom-call | tf_op jit(solution)/shard_map/states/pallas_call | solution.py:443
  5.3 2.6 %collective-permute-start = (f32[16,64,128]{2,1,0:T(8,128)}, f32[16,64,128]{2,1,0:T(8,128)S(1)}, u32[]{:S(2)}, u32[]{:S(2)}) collective-permute-start(f32[16,64,128]{2,1,0:T(8,128)} %get-tuple-element.38.low_ref), channel_id=1, source_target_pairs={{0,1},{1,0},{2,3},{3,2},{4,5},{5,4},{6,7},{7,6},{8,9},{9,8},{10,11... | collective-permute-start | bytes 1572872 | tf_op jit(solution)/shard_map/ppermute | solution.py:429
  7.8 6.9 %collective-permute-start.1 = (f32[16,64,128]{2,1,0:T(8,128)}, f32[16,64,128]{2,1,0:T(8,128)S(1)}, u32[]{:S(2)}, u32[]{:S(2)}) collective-permute-start(f32[16,64,128]{2,1,0:T(8,128)} %get-tuple-element.39.high_ref), channel_id=1, source_target_pairs={{1,2},{2,1},{3,4},{4,3},{5,6},{6,5},{7,8},{8,7},{9,10},{10,9},{11,... | collective-permute-start | bytes 1572872 | tf_op jit(solution)/shard_map/ppermute | solution.py:429
  14.7 3.8 %all-to-all-start = ((f32[32,1,128]{2,1,0:T(1,128)}), f32[32,1,128]{2,1,0:T(1,128)S(1)}, u32[]{:S(2)}, u32[]{:S(2)}) async-start(f32[32,1,128]{2,1,0:T(1,128)} %get-tuple-element.40), calls=%async_computation | async-start | bytes 32768 | tf_op jit(solution)/shard_map/all_to_all | solution.py:460
  18.6 0.6 copy-done.26
  19.2 1.2 copy-done
  20.4 1.2 copy-done.2
  21.6 5.5 %inner.1 = (bf16[2048,256]{1,0:T(8,128)(2,1)S(1)}, bf16[2048,256]{1,0:T(8,128)(2,1)S(1)}, f32[32,256]{1,0:T(8,128)S(1)}, f32[32,256]{1,0:T(8,128)S(1)}, f32[256,128]{1,0:T(8,128)S(1)}, /*index=5*/f32[256,128]{1,0:T(8,128)S(1)}) custom-call(bf16[256,2048]{1,0:T(8,128)(2,1)S(1)} %bitcast.12, bf16[2048,256]{1,0:T(8,128)(2,1)S(1)} %copy-done, ...), custom_call_target="tpu_custom_call" | custom-call | flops 3000000000 | bytes 12582912 | tf_op jit(solution)/shard_map/inner/pallas_call | solution.py:461
  27.1 1.0 copy-done.4
  28.1 1.0 copy-done.7
  29.1 0.6 copy-done.17
  29.7 0.2 join.1
  30.0 33.5 %all_to_all.20.part_ref = f32[32,64,128]{2,1,0:T(8,128)S(1)} all-to-all(f32[32,64,128]{2,1,0:T(8,128)S(1)} %join.1), channel_id=1, replica_groups=mesh['dp'=8,'seq'=32] {'seq'}, dimensions={0} | all-to-all | bytes 2097152 | tf_op jit(solution)/shard_map/all_to_all | solution.py:471
  63.6 33.3 %all_to_all.21.mine_ref = f32[32,64,128]{2,1,0:T(8,128)S(1)} all-to-all(f32[32,64,128]{2,1,0:T(8,128)S(1)} %scan.1), channel_id=1, replica_groups=mesh['dp'=8,'seq'=32] {'seq'}, dimensions={0} | all-to-all | bytes 2097152 | tf_op jit(solution)/shard_map/all_to_all | solution.py:473
  97.2 2.7 %collective-permute-start.2 = (f32[16,64,128]{2,1,0:T(8,128)S(1)}, f32[16,64,128]{2,1,0:T(8,128)S(1)}, u32[]{:S(2)}, u32[]{:S(2)}) collective-permute-start(f32[16,64,128]{2,1,0:T(8,128)S(1)} %get-tuple-element.48), channel_id=1, source_target_pairs={{0,1},{1,0},{2,3},{3,2},{4,5},{5,4},{6,7},{7,6},{8,9},{9,8},{10,11... | collective-permute-start | bytes 1572872 | tf_op jit(solution)/shard_map/ppermute | solution.py:429
  100.0 1.6 %collective-permute-start.3 = (f32[16,64,128]{2,1,0:T(8,128)S(1)}, f32[16,64,128]{2,1,0:T(8,128)S(1)}, u32[]{:S(2)}, u32[]{:S(2)}) collective-permute-start(f32[16,64,128]{2,1,0:T(8,128)S(1)} %get-tuple-element.49), channel_id=1, source_target_pairs={{1,2},{2,1},{3,4},{4,3},{5,6},{6,5},{7,8},{8,7},{9,10},{10,9},{11,... | collective-permute-start | bytes 1572872 | tf_op jit(solution)/shard_map/ppermute | solution.py:429
  101.6 1.9 %own.1 = (bf16[256,2048]{1,0:T(8,128)(2,1)}, bf16[256,2048]{1,0:T(8,128)(2,1)}, f32[32,256]{1,0:T(8,128)S(1)}, f32[128,256]{1,0:T(8,128)S(1)}, f32[128,256]{1,0:T(8,128)S(1)}) custom-call(f32[32,64,128]{2,1,0:T(8,128)S(1)} %all_to_all.21.mine_ref, bf16[2048,256]{1,0:T(8,128)(2,1)S(1)} %copy-done.5, bf16[2048,256]{1,0:T(8,128)(2,1)S(1)} %copy-done.8, ...), custom_call_target="tpu_custom_call" | custom-call | flops 2000000000 | bytes 8388608 | tf_op jit(solution)/shard_map/own/pallas_call | solution.py:481
  103.5 4.6 %collective-permute-done.2.low_ref = f32[16,64,128]{2,1,0:T(8,128)S(1)} collective-permute-done((f32[16,64,128]{2,1,0:T(8,128)S(1)}, f32[16,64,128]{2,1,0:T(8,128)S(1)}, u32[]{:S(2)}, u32[]{:S(2)}) %collective-permute-start.2) | collective-permute-done | bytes 524320 | tf_op jit(solution)/shard_map/ppermute | solution.py:429
  108.1 4.7 %collective-permute-done.3.high_ref = f32[16,64,128]{2,1,0:T(8,128)S(1)} collective-permute-done((f32[16,64,128]{2,1,0:T(8,128)S(1)}, f32[16,64,128]{2,1,0:T(8,128)S(1)}, u32[]{:S(2)}, u32[]{:S(2)}) %collective-permute-start.3) | collective-permute-done | bytes 524320 | tf_op jit(solution)/shard_map/ppermute | solution.py:429
  112.8 0.7 copy-done.25
  113.5 1.7 %sums.1 = (f32[32,256]{1,0:T(8,128)}, f32[256,1,128]{2,1,0:T(1,128)S(1)}) custom-call(f32[32,64,128]{2,1,0:T(8,128)S(1)} %all_to_all.21.mine_ref, f32[16,64,128]{2,1,0:T(8,128)S(1)} %collective-permute-done.2.low_ref, f32[16,64,128]{2,1,0:T(8,128)S(1)} %collective-permute-done.3.high_ref, bf16[2048,256]{1,0:T(8,128)(2,1)S(1)} %copy-done.1, ...), custom_call_target="tpu_custom_call" | custom-call | tf_op jit(solution)/shard_map/sums/pallas_call | solution.py:490
  115.2 0.6 copy-done.24
  115.8 13.9 %all-to-all-start.3 = ((f32[256,1,128]{2,1,0:T(1,128)}), f32[256,1,128]{2,1,0:T(1,128)}, u32[]{:S(2)}, u32[]{:S(2)}) async-start(f32[256,1,128]{2,1,0:T(1,128)} %copy-done.24), calls=%async_computation.3 | async-start | bytes 262144 | tf_op jit(solution)/shard_map/all_to_all | solution.py:496
  129.7 1.2 copy-done.6
  131.0 1.2 copy-done.9
  132.2 0.9 copy-done.18
  133.1 0.9 copy-done.20
  134.0 0.9 copy-done.22
  134.9 2.2 %other.1 = (bf16[256,2048]{1,0:T(8,128)(2,1)}, bf16[256,2048]{1,0:T(8,128)(2,1)}, bf16[256,128]{1,0:T(8,128)(2,1)}, bf16[256,128]{1,0:T(8,128)(2,1)}) custom-call(f32[16,64,128]{2,1,0:T(8,128)S(1)} %collective-permute-done.2.low_ref, f32[16,64,128]{2,1,0:T(8,128)S(1)} %collective-permute-done.3.high_ref, ...), custom_call_target="tpu_custom_call", output_to_operand_aliasing={{0}: (13, {}), {1}: (14, {})} | custom-call | flops 2000000000 | bytes 8388608 | tf_op jit(solution)/shard_map/other/pallas_call | solution.py:497
  137.1 5.1 %all-to-all-done.3 = f32[256,1,128]{2,1,0:T(1,128)} async-done(((f32[256,1,128]{2,1,0:T(1,128)}), f32[256,1,128]{2,1,0:T(1,128)}, u32[]{:S(2)}, u32[]{:S(2)}) %all-to-all-start.3) | async-done | bytes 131104 | tf_op jit(solution)/shard_map/all_to_all | solution.py:496
  142.2 1.2 reduce_sum.9
  143.4 0.6 fusion
  (46 shorter events, 0.4 us)
Async XLA Ops:
  0.6 17.9 %copy-start.11 = (bf16[1,256,2048]{2,1,0:T(8,128)(2,1)S(1)}, bf16[1,256,2048]{2,1,0:T(8,128)(2,1)}, u32[]{:S(2)}) copy-start(bf16[1,256,2048]{2,1,0:T(8,128)(2,1)} %param.13) | copy-start | bytes 3145732
  0.6 17.9 %copy-start.12 = (bf16[1,256,128]{2,1,0:T(8,128)(2,1)S(1)}, bf16[1,256,128]{2,1,0:T(8,128)(2,1)}, u32[]{:S(2)}) copy-start(bf16[1,256,128]{2,1,0:T(8,128)(2,1)} %param.8) | copy-start | bytes 196612
  0.7 17.9 %copy-start.13 = (bf16[1,256,128]{2,1,0:T(8,128)(2,1)S(1)}, bf16[1,256,128]{2,1,0:T(8,128)(2,1)}, u32[]{:S(2)}) copy-start(bf16[1,256,128]{2,1,0:T(8,128)(2,1)} %param.9) | copy-start | bytes 196612
  5.3 13.3 %copy-start.14 = (f32[32,256]{1,0:T(8,128)S(1)}, f32[32,256]{1,0:T(8,128)}, u32[]{:S(2)}) copy-start(f32[32,256]{1,0:T(8,128)} %get-tuple-element.43.cum_ref) | copy-start | bytes 98308
  5.3 24.4 %collective-permute-start = (f32[16,64,128]{2,1,0:T(8,128)}, f32[16,64,128]{2,1,0:T(8,128)S(1)}, u32[]{:S(2)}, u32[]{:S(2)}) collective-permute-start(f32[16,64,128]{2,1,0:T(8,128)} %get-tuple-element.38.low_ref), channel_id=1, source_target_pairs={{0,1},{1,0},{2,3},{3,2},{4,5},{5,4},{6,7},{7,6},{8,9},{9,8},{10,11... | collective-permute-start | bytes 1572872 | tf_op jit(solution)/shard_map/ppermute | solution.py:429
  7.8 21.9 %collective-permute-start.1 = (f32[16,64,128]{2,1,0:T(8,128)}, f32[16,64,128]{2,1,0:T(8,128)S(1)}, u32[]{:S(2)}, u32[]{:S(2)}) collective-permute-start(f32[16,64,128]{2,1,0:T(8,128)} %get-tuple-element.39.high_ref), channel_id=1, source_target_pairs={{1,2},{2,1},{3,4},{4,3},{5,6},{6,5},{7,8},{8,7},{9,10},{10,9},{11,... | collective-permute-start | bytes 1572872 | tf_op jit(solution)/shard_map/ppermute | solution.py:429
  14.7 15.0 %all-to-all-start = ((f32[32,1,128]{2,1,0:T(1,128)}), f32[32,1,128]{2,1,0:T(1,128)S(1)}, u32[]{:S(2)}, u32[]{:S(2)}) async-start(f32[32,1,128]{2,1,0:T(1,128)} %get-tuple-element.40), calls=%async_computation | async-start | bytes 32768 | tf_op jit(solution)/shard_map/all_to_all | solution.py:460
  18.5 0.7 copy-start.26
  19.2 1.2 copy-start
  20.4 1.2 copy-start.2
  21.6 8.1 %copy-start.10 = (f32[32,64,128]{2,1,0:T(8,128)S(1)}, f32[32,64,128]{2,1,0:T(8,128)}, u32[]{:S(2)}) copy-start(f32[32,64,128]{2,1,0:T(8,128)} %get-tuple-element.37.keep_ref) | copy-start | bytes 3145732
  27.1 1.0 copy-start.4
  28.1 1.0 copy-start.7
  29.1 0.7 copy-start.17
  63.5 33.5 %copy-start.15 = (f32[16,64,128]{2,1,0:T(8,128)S(1)}, f32[16,64,128]{2,1,0:T(8,128)}, u32[]{:S(2)}) copy-start(f32[16,64,128]{2,1,0:T(8,128)} %get-tuple-element.38.low_ref) | copy-start | bytes 1572868
  63.5 33.5 %copy-start.16 = (f32[16,64,128]{2,1,0:T(8,128)S(1)}, f32[16,64,128]{2,1,0:T(8,128)}, u32[]{:S(2)}) copy-start(f32[16,64,128]{2,1,0:T(8,128)} %get-tuple-element.39.high_ref) | copy-start | bytes 1572868
  63.6 37.9 %copy-start.5 = (bf16[2048,256]{1,0:T(8,128)(2,1)S(1)}, bf16[2048,256]{1,0:T(8,128)(2,1)}, u32[]{:S(2)}) copy-start(bf16[2048,256]{1,0:T(8,128)(2,1)} %copy-done.4) | copy-start | bytes 3145732
  63.6 37.9 %copy-start.8 = (bf16[2048,256]{1,0:T(8,128)(2,1)S(1)}, bf16[2048,256]{1,0:T(8,128)(2,1)}, u32[]{:S(2)}) copy-start(bf16[2048,256]{1,0:T(8,128)(2,1)} %copy-done.7) | copy-start | bytes 3145732
  97.0 4.6 %copy-start.1 = (bf16[2048,256]{1,0:T(8,128)(2,1)S(1)}, bf16[2048,256]{1,0:T(8,128)(2,1)}, u32[]{:S(2)}) copy-start(bf16[2048,256]{1,0:T(8,128)(2,1)} %get-tuple-element.41.xt_ref) | copy-start | bytes 3145732
  97.0 4.6 %copy-start.3 = (bf16[2048,256]{1,0:T(8,128)(2,1)S(1)}, bf16[2048,256]{1,0:T(8,128)(2,1)}, u32[]{:S(2)}) copy-start(bf16[2048,256]{1,0:T(8,128)(2,1)} %get-tuple-element.42.gt_ref) | copy-start | bytes 3145732
  97.2 10.8 %collective-permute-start.2 = (f32[16,64,128]{2,1,0:T(8,128)S(1)}, f32[16,64,128]{2,1,0:T(8,128)S(1)}, u32[]{:S(2)}, u32[]{:S(2)}) collective-permute-start(f32[16,64,128]{2,1,0:T(8,128)S(1)} %get-tuple-element.48), channel_id=1, source_target_pairs={{0,1},{1,0},{2,3},{3,2},{4,5},{5,4},{6,7},{7,6},{8,9},{9,8},{10,11... | collective-permute-start | bytes 1572872 | tf_op jit(solution)/shard_map/ppermute | solution.py:429
  100.0 12.8 %collective-permute-start.3 = (f32[16,64,128]{2,1,0:T(8,128)S(1)}, f32[16,64,128]{2,1,0:T(8,128)S(1)}, u32[]{:S(2)}, u32[]{:S(2)}) collective-permute-start(f32[16,64,128]{2,1,0:T(8,128)S(1)} %get-tuple-element.49), channel_id=1, source_target_pairs={{1,2},{2,1},{3,4},{4,3},{5,6},{6,5},{7,8},{8,7},{9,10},{10,9},{11,... | collective-permute-start | bytes 1572872 | tf_op jit(solution)/shard_map/ppermute | solution.py:429
  101.5 11.3 %copy-start.23 = (f32[1,32,256]{2,1,0:T(8,128)S(1)}, f32[1,32,256]{2,1,0:T(8,128)}, u32[]{:S(2)}) copy-start(f32[1,32,256]{2,1,0:T(8,128)} %param.10) | copy-start | bytes 98308
  103.4 11.7 %copy-start.19 = (f32[128,256]{1,0:T(8,128)}, f32[128,256]{1,0:T(8,128)S(1)}, u32[]{:S(2)}) copy-start(f32[128,256]{1,0:T(8,128)S(1)} %get-tuple-element.52.gct_ref) | copy-start | bytes 393220
  103.4 11.7 %copy-start.21 = (f32[128,256]{1,0:T(8,128)}, f32[128,256]{1,0:T(8,128)S(1)}, u32[]{:S(2)}) copy-start(f32[128,256]{1,0:T(8,128)S(1)} %get-tuple-element.53.gbt_ref) | copy-start | bytes 393220
  112.8 0.7 copy-start.25
  115.8 26.4 %all-to-all-start.3 = ((f32[256,1,128]{2,1,0:T(1,128)}), f32[256,1,128]{2,1,0:T(1,128)}, u32[]{:S(2)}, u32[]{:S(2)}) async-start(f32[256,1,128]{2,1,0:T(1,128)} %copy-done.24), calls=%async_computation.3 | async-start | bytes 262144 | tf_op jit(solution)/shard_map/all_to_all | solution.py:496
  129.7 1.2 copy-start.6
  131.0 1.2 copy-start.9
  132.2 0.9 copy-start.18
  133.1 0.9 copy-start.20
  134.0 0.9 copy-start.22
  (1 other events, 0.6 us)

commit v3 on v2

--- a/solution.py
+++ b/solution.py
@@ -1,3 +1,5 @@
+import functools
+
 import jax
 import jax.numpy as jnp
 from jax import lax
@@ -19,6 +21,7 @@
 BF16 = jnp.bfloat16
 EXACT = lax.Precision.HIGHEST
 VMEM_LIMIT = 24 * 1024 * 1024
+LARGE_LIMIT = 60 * 1024 * 1024
 
 
 def dot(a, b, ca, cb, precision=None):
@@ -188,65 +191,93 @@
         out_high_ref[h] = high_ref[h] + high_gain[h : h + 1] * mine_ref[HALF + h]
 
 
-def inner_kernel(
-    g_ref, xt_ref, gt_ref, b_ref, c_ref, cum_ref, skip_ref,
-    y_ref, gx_ref, row_ref, skiprow_ref, gb_ref, gc_ref,
-    cb_s, acc_s,
-):
+def inner_kernel(offset, *refs):
+    (g_ref, xt_ref, gt_ref, b_ref, c_ref, cum_ref, skip_ref), refs = refs[:7], refs[7:]
+    (y_ref, gx_ref, row_ref, skiprow_ref, gb_ref, gc_ref, cb_s, acc_s) = refs[-8:]
+    place = pl.program_id(0)
+    step = place + offset
     half = GROUP // 2
-    cb_s[...] = dot(c_ref[...], b_ref[...], 1, 1)
-    acc_s[...] = jnp.zeros_like(acc_s)
+
+    @pl.when(place == 0)
+    def _():
+        cb_s[...] = dot(c_ref[...], b_ref[...], 1, 1)
+        acc_s[...] = jnp.zeros_like(acc_s)
+
     square = (half, half)
     lower = iota(square, 0) >= iota(square, 1)
     nothing = jnp.zeros((SIZE, GROUP), BF16)
-
-    def some_heads(step, carry):
-        cum = cum_ref[head_rows(step), :]
-        cum_t = cum.T
-        rows = []
-        skips = []
-        for j in range(STEP):
-            early, late = cum[j : j + 1, :half], cum[j : j + 1, half:]
-            start, end = cum_t[:half, j : j + 1], cum_t[half:, j : j + 1]
-            e00 = jnp.where(lower, jnp.exp(start - early), 0.0)
-            e10 = jnp.exp(end - early)
-            e11 = jnp.where(lower, jnp.exp(end - late), 0.0)
-            w00 = (cb_s[:half, :half] * e00).astype(BF16)
-            w10 = (cb_s[half:, :half] * e10).astype(BF16)
-            w11 = (cb_s[half:, half:] * e11).astype(BF16)
-            weights = jnp.concatenate(
-                [
-                    jnp.concatenate([w00, jnp.zeros(square, BF16)], axis=1),
-                    jnp.concatenate([w10, w11], axis=1),
-                ],
-                axis=0,
-            )
-            features = pl.ds(pl.multiple_of(step * WIDE + j * SIZE, SIZE), SIZE)
-            xt = xt_ref[features, :]
-            gt = gt_ref[features, :]
-            yt = dot(xt, weights, 1, 1)
-            gxt = dot(gt, weights, 1, 0)
-            pair = pl.ds(pl.multiple_of(step * WIDE + j // 2 * 2 * SIZE, 2 * SIZE), 2 * SIZE)
-            two = [xt, nothing] if j % 2 == 0 else [nothing, xt]
-            gw = dot(g_ref[:, pair], jnp.concatenate(two, axis=0), 1, 0)
-            acc_s[:half, :half] += gw[:half, :half] * e00
-            acc_s[half:, :half] += gw[half:, :half] * e10
-            acc_s[half:, half:] += gw[half:, half:] * e11
-            xf = xt.astype(F32)
-            gf = gt.astype(F32)
-            rows.append(jnp.sum(gf * yt - xf * gxt, axis=0, keepdims=True))
-            skips.append(jnp.sum(gf * xf, axis=0, keepdims=True))
-            skip = skip_ref[step * STEP + j]
-            y_ref[features, :] = (yt + skip * xf).astype(BF16)
-            gx_ref[features, :] = (gxt + skip * gf).astype(BF16)
-        row_ref[head_rows(step), :] = jnp.concatenate(rows, axis=0)
-        skiprow_ref[head_rows(step), :] = jnp.concatenate(skips, axis=0)
-        return carry
-
-    lax.fori_loop(0, GRID, some_heads, 0)
-    acc = acc_s[...].astype(BF16)
-    gc_ref[...] = dot(acc, b_ref[...], 1, 0)
-    gb_ref[...] = dot(acc, c_ref[...], 0, 0)
+    cum = cum_ref[head_rows(step), :]
+    cum_t = cum.T
+    rows = []
+    skips = []
+    for j in range(STEP):
+        low, high = j * SIZE, (j + 1) * SIZE
+        early, late = cum[j : j + 1, :half], cum[j : j + 1, half:]
+        start, end = cum_t[:half, j : j + 1], cum_t[half:, j : j + 1]
+        e00 = jnp.where(lower, jnp.exp(start - early), 0.0)
+        e10 = jnp.exp(end - early)
+        e11 = jnp.where(lower, jnp.exp(end - late), 0.0)
+        w00 = (cb_s[:half, :half] * e00).astype(BF16)
+        w10 = (cb_s[half:, :half] * e10).astype(BF16)
+        w11 = (cb_s[half:, half:] * e11).astype(BF16)
+        weights = jnp.concatenate(
+            [
+                jnp.concatenate([w00, jnp.zeros(square, BF16)], axis=1),
+                jnp.concatenate([w10, w11], axis=1),
+            ],
+            axis=0,
+        )
+        xt = xt_ref[low:high, :]
+        gt = gt_ref[low:high, :]
+        yt = dot(xt, weights, 1, 1)
+        gxt = dot(gt, weights, 1, 0)
+        pair = j // 2 * 2 * SIZE
+        two = [xt, nothing] if j % 2 == 0 else [nothing, xt]
+        gw = dot(g_ref[:, pair : pair + 2 * SIZE], jnp.concatenate(two, axis=0), 1, 0)
+        acc_s[:half, :half] += gw[:half, :half] * e00
+        acc_s[half:, :half] += gw[half:, :half] * e10
+        acc_s[half:, half:] += gw[half:, half:] * e11
+        xf = xt.astype(F32)
+        gf = gt.astype(F32)
+        rows.append(jnp.sum(gf * yt - xf * gxt, axis=0, keepdims=True))
+        skips.append(jnp.sum(gf * xf, axis=0, keepdims=True))
+        skip = skip_ref[step * STEP + j]
+        y_ref[low:high, :] = (yt + skip * xf).astype(BF16)
+        gx_ref[low:high, :] = (gxt + skip * gf).astype(BF16)
+    here = pl.ds(pl.multiple_of(place * STEP, STEP), STEP)
+    row_ref[here, :] = jnp.concatenate(rows, axis=0)
+    skiprow_ref[here, :] = jnp.concatenate(skips, axis=0)
+
+    @pl.when(place == HALF_STEPS - 1)
+    def _():
+        acc = acc_s[...].astype(BF16)
+        gc_ref[...] = dot(acc, b_ref[...], 1, 0)
+        gb_ref[...] = dot(acc, c_ref[...], 0, 0)
+
+
+def inner(offset, g, xt, gt, b, c, cum, skip, earlier=()):
+    wide_t = pl.BlockSpec((WIDE, GROUP), lambda i: (i + offset, 0))
+    wide_n = pl.BlockSpec((GROUP, WIDE), lambda i: (0, i + offset))
+    kept = lambda *shape: pl.BlockSpec(shape, lambda i: (0,) * len(shape))
+    narrow = kept(GROUP, STATE)
+    wide = shape_of((HEADS * SIZE, GROUP), BF16)
+    rows = shape_of((HALF, GROUP))
+    return call(
+        functools.partial(inner_kernel, offset),
+        "inner",
+        [wide, wide, rows, rows, shape_of((GROUP, STATE)), shape_of((GROUP, STATE))],
+        [wide_t, wide_t, kept(HALF, GROUP), kept(HALF, GROUP), narrow, narrow],
+        grid=(HALF_STEPS,),
+        in_specs=[
+            wide_n, wide_t, wide_t, narrow, narrow, kept(HEADS, GROUP),
+            pl.BlockSpec(memory_space=pltpu.SMEM),
+        ]
+        + [pl.BlockSpec(memory_space=pltpu.HBM)] * len(earlier),
+        input_output_aliases={7 + i: i for i in range(len(earlier))},
+        scratch_shapes=[pltpu.VMEM((GROUP, GROUP), F32), pltpu.VMEM((GROUP, GROUP), F32)],
+        cost=cost(4),
+        limit=LARGE_LIMIT,
+    )(g, xt, gt, b, c, cum, skip, *earlier)
 
 
 def halves(own):
@@ -339,8 +370,8 @@
 
 
 def sums_kernel(
-    mine_ref, low_ref, high_ref, xt_ref, gt_ref, b_ref, c_ref, cum_ref, row_ref, own_row_ref,
-    skiprow_ref, dt_ref, alog_ref,
+    mine_ref, low_ref, high_ref, xt_ref, gt_ref, b_ref, c_ref, cum_ref, low_row_ref,
+    high_row_ref, own_row_ref, low_skiprow_ref, high_skiprow_ref, dt_ref, alog_ref,
     gdt_ref, sums_ref,
     row_s,
 ):
@@ -363,20 +394,28 @@
     )
     overlap = jnp.sum(overlap, axis=1, keepdims=True) * jnp.exp(cum_ref[:, GROUP - 1 :])
     final = iota((HEADS, GROUP), 1) == GROUP - 1
-    row = row_ref[...] + own_row_ref[...] + row_s[...] + jnp.where(final, overlap, 0.0)
+    inner_row = jnp.concatenate([low_row_ref[...], high_row_ref[...]], axis=0)
+    row = inner_row + own_row_ref[...] + row_s[...] + jnp.where(final, overlap, 0.0)
     gdt = -jnp.exp(column(alog_ref[...])) * dot(row, triangle(), 1, 1, EXACT)
     gdt_ref[...] = gdt
     alog = jnp.sum(gdt * dt_ref[...], axis=1, keepdims=True)
-    skip = jnp.sum(skiprow_ref[...], axis=1, keepdims=True)
+    skiprow = jnp.concatenate([low_skiprow_ref[...], high_skiprow_ref[...]], axis=0)
+    skip = jnp.sum(skiprow, axis=1, keepdims=True)
     sums = jnp.concatenate(
         [as_row(alog), as_row(skip), jnp.zeros((1, STATE - 2 * HEADS), F32)], axis=1
     )
     sums_ref[...] = jnp.broadcast_to(sums[None], sums_ref.shape)
 
 
+def total_kernel(sums_ref, alog_ref, skip_ref):
+    total = jnp.sum(sums_ref[...], axis=0)
+    alog_ref[...] = total[:, :HEADS]
+    skip_ref[...] = total[:, HEADS : 2 * HEADS]
+
+
 def other_kernel(
     low_ref, high_ref, yt_ref, gxt_ref, xt_ref, gt_ref, b_ref, c_ref, cum_ref,
-    gct_ref, gbt_ref, gci_ref, gbi_ref, y_in, gx_in,
+    gct_ref, gbt_ref, low_gc_ref, high_gc_ref, low_gb_ref, high_gb_ref, y_in, gx_in,
     y_hbm, gx_hbm, gc_ref, gb_ref,
     out_s, sems,
 ):
@@ -395,8 +434,8 @@
             yt_ref, gxt_ref, y_hbm, gx_hbm, out_s, sems, gct, gbt,
         )
         copies += made
-    gc_ref[...] = (gci_ref[...] + gct.T).astype(BF16)
-    gb_ref[...] = (gbi_ref[...] + gbt.T).astype(BF16)
+    gc_ref[...] = (low_gc_ref[...] + high_gc_ref[...] + gct.T).astype(BF16)
+    gb_ref[...] = (low_gb_ref[...] + high_gb_ref[...] + gbt.T).astype(BF16)
     for made in copies:
         made.wait()
 
@@ -454,25 +493,21 @@
             pltpu.VMEM((1, HEADS), F32),
             pltpu.SemaphoreType.DMA((4 + 2 * GRID,)),
         ],
-        limit=60 * 1024 * 1024,
+        limit=LARGE_LIMIT,
     )(x, g, b, c, steps, alog)
     low_in, high_in = swap(low, high)
     gains = lax.all_to_all(gain, "seq", 0, 0, tiled=True)
-    yt, gxt, row, skiprow, gbi, gci = call(
-        inner_kernel,
-        "inner",
-        [wide, wide, rows, rows, shape_of((GROUP, STATE)), shape_of((GROUP, STATE))],
-        in_specs=[vmem] * 6 + [pl.BlockSpec(memory_space=pltpu.SMEM)],
-        scratch_shapes=[pltpu.VMEM((GROUP, GROUP), F32), pltpu.VMEM((GROUP, GROUP), F32)],
-        cost=cost(6),
-    )(g, xt, gt, b, c, cum, skip)
-    low_in, high_in, gains, row = lax.optimization_barrier((low_in, high_in, gains, row))
+    yt, gxt, low_row, low_skiprow, low_gb, low_gc = inner(0, g, xt, gt, b, c, cum, skip)
+    low_in, high_in, gains, yt, gxt = lax.optimization_barrier((low_in, high_in, gains, yt, gxt))
     joined = call(join_kernel, "join", all_heads)(keep, low_in, high_in, cum)
     parts = lax.all_to_all(joined, "seq", 0, 0, tiled=True)
     scanned = call(scan_kernel, "scan", all_heads)(parts, gains)
     mine = lax.all_to_all(scanned, "seq", 0, 0, tiled=True)
     low_out, high_out = call(pass_on_kernel, "pass_on", [half, half])(mine, low, high, cum)
     low_back, high_back = swap(low_out, high_out)
+    yt, gxt, high_row, high_skiprow, high_gb, high_gc = inner(
+        HALF_STEPS, g, xt, gt, b, c, cum, skip, (yt, gxt)
+    )
     out_scratch = [
         pltpu.VMEM((2 * HALF_STEPS, GROUP, WIDE), BF16),
         pltpu.SemaphoreType.DMA((2 * HALF_STEPS,)),
@@ -492,22 +527,30 @@
         "sums",
         [rows, shape_of((everyone, 1, STATE))],
         scratch_shapes=[pltpu.VMEM((HEADS, GROUP), F32)],
-    )(mine, low_back, high_back, xt, gt, b, c, cum, row, own_row, skiprow, steps, alog)
+    )(
+        mine, low_back, high_back, xt, gt, b, c, cum, low_row, high_row, own_row,
+        low_skiprow, high_skiprow, steps, alog,
+    )
     sums = lax.all_to_all(copies, ("dp", "seq"), 0, 0, tiled=True)
     y, gx, gc, gb = call(
         other_kernel,
         "other",
         [tall, tall, shape_of((GROUP, STATE), BF16), shape_of((GROUP, STATE), BF16)],
         [hbm, hbm, vmem, vmem],
-        in_specs=[vmem] * 13 + [hbm, hbm],
-        input_output_aliases={13: 0, 14: 1},
+        in_specs=[vmem] * 15 + [hbm, hbm],
+        input_output_aliases={15: 0, 16: 1},
         scratch_shapes=out_scratch,
         cost=cost(4),
-    )(low_back, high_back, yt, gxt, xt, gt, b, c, cum, gct, gbt, gci, gbi, y, gx)
-    total = jnp.sum(sums, axis=(0, 1))
+    )(
+        low_back, high_back, yt, gxt, xt, gt, b, c, cum, gct, gbt,
+        low_gc, high_gc, low_gb, high_gb, y, gx,
+    )
+    galog, gskip = call(
+        total_kernel, "total", [shape_of((1, HEADS)), shape_of((1, HEADS))]
+    )(sums)
     return (
         y[None], gx[None], gb[None], gc[None], gdt[None],
-        total[:HEADS], total[HEADS : 2 * HEADS],
+        galog[0], gskip[0],
     )
 
 

time: 145 us -> 138 us (0.952)
  Pallas kernels: 16.4 us -> 24.2 us
  blocking collectives: 66.9 us -> 59.6 us
  local copies, waits for them, and re-layouts: 12.8 us -> 8.05 us
  waiting for transfers between devices: 14.5 us -> 9.83 us
  starting transfers between devices: 31.5 us -> 34.4 us
    pallas_call x1 -> x3, Pallas kernels: 5.45 us -> 10.3 us  [the longest x2 9.42 us: inner(): call(functools.partial(inner_kernel, offset), 'inner', [wide, wide, rows,...]
    ppermute x2, waiting for transfers between devices: 4.75 us -> 0.01 us  [swap(): lax.ppermute(high, 'seq', high_pairs)]
    ppermute x2, waiting for transfers between devices: 4.59 us -> 0.01 us  [swap(): lax.ppermute(low, 'seq', low_pairs)]
    all_to_all x1, blocking collectives: 33.3 us -> 28.8 us  [shards(): mine = lax.all_to_all(scanned, 'seq', 0, 0, tiled=True)]
    all_to_all x1, waiting for transfers between devices: 0.01 us -> 4.35 us  [shards(): gains = lax.all_to_all(gain, 'seq', 0, 0, tiled=True)]
    unnamed x54 -> x56, local copies, waits for them, and re-layouts: 12.2 us -> 8.05 us
    all_to_all x1, blocking collectives: 33.5 us -> 30.8 us  [shards(): parts = lax.all_to_all(joined, 'seq', 0, 0, tiled=True)]
    ppermute x2, starting transfers between devices: 8.42 us -> 10.2 us  [swap(): lax.ppermute(high, 'seq', high_pairs)]
  transfers between devices with their start and end apart: 6 -> 6, of which waited for: 3 -> 2; matrix products, arithmetic and copies ran while one was open for 0% -> 0% of each run, Pallas kernels for 7% -> 11%
where the time goes in v3:
time: 138 us; the launch traced here: 137 us
  blocking collectives  59.6 us (43%)
  starting transfers between devices  34.4 us (25%)
  Pallas kernels  24.2 us (18%)
  waiting for transfers between devices  9.83 us (7%)
  local copies, waits for them, and re-layouts  8.05 us (6%)
    all_to_all x1, blocking collectives, shards(): parts = lax.all_to_all(joined, 'seq', 0, 0, tiled=True)  30.8 us
    all_to_all x1, blocking collectives, shards(): mine = lax.all_to_all(scanned, 'seq', 0, 0, tiled=True)  28.8 us
    all_to_all x1, starting transfers between devices, shards(): sums = lax.all_to_all(copies, ('dp', 'seq'), 0, 0, tiled=True)  13.6 us
    ppermute x2, starting transfers between devices, swap(): lax.ppermute(high, 'seq', high_pairs)  10.2 us
    pallas_call x2, Pallas kernels, inner(): call(functools.partial(inner_kernel, offset), 'inner', [wide, wide, rows,...  9.42 us
    unnamed x56, local copies, waits for them, and re-layouts  8.05 us
    ppermute x2, starting transfers between devices, swap(): lax.ppermute(low, 'seq', low_pairs)  6.7 us
    all_to_all x1, waiting for transfers between devices, shards(): sums = lax.all_to_all(copies, ('dp', 'seq'), 0, 0, tiled=True)  5.46 us
  transfers between devices with their start and end apart: 6, of which 2 were waited for; matrix products, arithmetic and copies ran while one was open for 0% of the time, Pallas kernels for 11%

profile of v3, /device:TPU:1, one launch (start us, length us, event | category | flops | bytes accessed | tf_op | source)
XLA Modules:
  0.0 137.0 jit_solution(7388238791928840156)
XLA Ops:
  0.6 4.5 %states.1 = (f32[16,64,128]{2,1,0:T(8,128)}, f32[16,64,128]{2,1,0:T(8,128)}, f32[32,64,128]{2,1,0:T(8,128)}, f32[32,1,128]{2,1,0:T(1,128)}, bf16[2048,256]{1,0:T...) custom-call(bf16[256,2048]{1,0:T(8,128)(2,1)} %bitcast.29, bf16[256,2048]{1,0:T(8,128)(2,1)} %bitcast.30, ...), custom_call_target="tpu_custom_call" | custom-call | tf_op jit(solution)/shard_map/states/pallas_call | solution.py:482
  5.2 2.6 %collective-permute-start = (f32[16,64,128]{2,1,0:T(8,128)}, f32[16,64,128]{2,1,0:T(8,128)S(1)}, u32[]{:S(2)}, u32[]{:S(2)}) collective-permute-start(f32[16,64,128]{2,1,0:T(8,128)} %get-tuple-element.47.low_ref), channel_id=1, source_target_pairs={{0,1},{1,0},{2,3},{3,2},{4,5},{5,4},{6,7},{7,6},{8,9},{9,8},{10,11... | collective-permute-start | bytes 1572872 | tf_op jit(solution)/shard_map/ppermute | solution.py:468
  7.7 6.9 %collective-permute-start.1 = (f32[16,64,128]{2,1,0:T(8,128)}, f32[16,64,128]{2,1,0:T(8,128)S(1)}, u32[]{:S(2)}, u32[]{:S(2)}) collective-permute-start(f32[16,64,128]{2,1,0:T(8,128)} %get-tuple-element.48.high_ref), channel_id=1, source_target_pairs={{1,2},{2,1},{3,4},{4,3},{5,6},{6,5},{7,8},{8,7},{9,10},{10,9},{11,... | collective-permute-start | bytes 1572872 | tf_op jit(solution)/shard_map/ppermute | solution.py:468
  14.6 3.8 %all-to-all-start = ((f32[32,1,128]{2,1,0:T(1,128)}), f32[32,1,128]{2,1,0:T(1,128)S(1)}, u32[]{:S(2)}, u32[]{:S(2)}) async-start(f32[32,1,128]{2,1,0:T(1,128)} %get-tuple-element.49), calls=%async_computation | async-start | bytes 32768 | tf_op jit(solution)/shard_map/all_to_all | solution.py:499
  18.4 0.0 copy-start.2
  18.4 0.0 copy-start.9
  18.4 4.8 %inner.2 = (bf16[2048,256]{1,0:T(8,128)(2,1)}, bf16[2048,256]{1,0:T(8,128)(2,1)}, f32[16,256]{1,0:T(8,128)}, f32[16,256]{1,0:T(8,128)}, f32[256,128]{1,0:T(8,128)}, /*index=5*/f32[256,128]{1,0:T(8,128)}) custom-call(bf16[256,2048]{1,0:T(8,128)(2,1)} %bitcast.31, bf16[2048,256]{1,0:T(8,128)(2,1)} %get-tuple-element.50.refs_1_.xt_ref, ...), custom_call_target="tpu_custom_call" | custom-call | flops 2000000000 | bytes 8388608 | tf_op jit(solution)/shard_map/inner/pallas_call | solution.py:265
  23.2 4.4 %all-to-all-done.gain_ref = f32[32,1,128]{2,1,0:T(1,128)S(1)} async-done(((f32[32,1,128]{2,1,0:T(1,128)}), f32[32,1,128]{2,1,0:T(1,128)S(1)}, u32[]{:S(2)}, u32[]{:S(2)}) %all-to-all-start) | async-done | bytes 16416 | tf_op jit(solution)/shard_map/all_to_all | solution.py:499
  27.6 0.2 join.1
  27.8 30.8 %all_to_all.20.part_ref = f32[32,64,128]{2,1,0:T(8,128)S(1)} all-to-all(f32[32,64,128]{2,1,0:T(8,128)S(1)} %join.1), channel_id=1, replica_groups=mesh['dp'=8,'seq'=32] {'seq'}, dimensions={0} | all-to-all | bytes 2097152 | tf_op jit(solution)/shard_map/all_to_all | solution.py:503
  58.6 0.1 scan.1
  58.7 28.8 %all_to_all.21.mine_ref = f32[32,64,128]{2,1,0:T(8,128)S(1)} all-to-all(f32[32,64,128]{2,1,0:T(8,128)S(1)} %scan.1), channel_id=1, replica_groups=mesh['dp'=8,'seq'=32] {'seq'}, dimensions={0} | all-to-all | bytes 2097152 | tf_op jit(solution)/shard_map/all_to_all | solution.py:505
  87.5 1.2 pass_on.1
  88.7 4.2 %collective-permute-start.2 = (f32[16,64,128]{2,1,0:T(8,128)}, f32[16,64,128]{2,1,0:T(8,128)S(1)}, u32[]{:S(2)}, u32[]{:S(2)}) collective-permute-start(f32[16,64,128]{2,1,0:T(8,128)} %get-tuple-element.58), channel_id=1, source_target_pairs={{0,1},{1,0},{2,3},{3,2},{4,5},{5,4},{6,7},{7,6},{8,9},{9,8},{10,11... | collective-permute-start | bytes 1572872 | tf_op jit(solution)/shard_map/ppermute | solution.py:468
  92.9 0.0 copy-start.10
  92.9 3.4 %collective-permute-start.3 = (f32[16,64,128]{2,1,0:T(8,128)}, f32[16,64,128]{2,1,0:T(8,128)}, u32[]{:S(2)}, u32[]{:S(2)}) collective-permute-start(f32[16,64,128]{2,1,0:T(8,128)} %get-tuple-element.59), channel_id=1, source_target_pairs={{1,2},{2,1},{3,4},{4,3},{5,6},{6,5},{7,8},{8,7},{9,10},{10,9},{11,... | collective-permute-start | bytes 1572872 | tf_op jit(solution)/shard_map/ppermute | solution.py:468
  96.2 4.7 %inner.3 = (bf16[2048,256]{1,0:T(8,128)(2,1)}, bf16[2048,256]{1,0:T(8,128)(2,1)}, f32[16,256]{1,0:T(8,128)}, f32[16,256]{1,0:T(8,128)}, f32[256,128]{1,0:T(8,128)}, /*index=5*/f32[256,128]{1,0:T(8,128)}) custom-call(bf16[256,2048]{1,0:T(8,128)(2,1)} %bitcast.32, ...), custom_call_target="tpu_custom_call", output_to_operand_aliasing={{0}: (7, {}), {1}: (8, {})} | custom-call | flops 2000000000 | bytes 8388608 | tf_op jit(solution)/shard_map/inner/pallas_call | solution.py:265
  101.0 1.2 copy-done.3
  102.2 1.2 copy-done.5
  103.4 1.9 %own.1 = (bf16[256,2048]{1,0:T(8,128)(2,1)}, bf16[256,2048]{1,0:T(8,128)(2,1)}, f32[32,256]{1,0:T(8,128)S(1)}, f32[128,256]{1,0:T(8,128)S(1)}, f32[128,256]{1,0:T(8,128)S(1)}) custom-call(f32[32,64,128]{2,1,0:T(8,128)S(1)} %all_to_all.21.mine_ref, bf16[2048,256]{1,0:T(8,128)(2,1)S(1)} %copy-done.3, bf16[2048,256]{1,0:T(8,128)(2,1)S(1)} %copy-done.5, ...), custom_call_target="tpu_custom_call" | custom-call | flops 2000000000 | bytes 8388608 | tf_op jit(solution)/shard_map/own/pallas_call | solution.py:516
  105.3 0.0 copy-start.27
  105.4 0.6 copy-done.27
  106.0 2.8 %sums.1 = (f32[32,256]{1,0:T(8,128)}, f32[256,1,128]{2,1,0:T(1,128)S(1)}) custom-call(f32[32,64,128]{2,1,0:T(8,128)S(1)} %all_to_all.21.mine_ref, f32[16,64,128]{2,1,0:T(8,128)S(1)} %collective-permute-done.2.low_ref, f32[16,64,128]{2,1,0:T(8,128)} %collective-permute-done.3.high_ref, bf16[2048,256]{1,0:T(8,128)(2,1)S(1)} %copy-done, ...), custom_call_target="tpu_custom_call" | custom-call | tf_op jit(solution)/shard_map/sums/pallas_call | solution.py:525
  108.8 0.7 copy-done.22
  109.5 13.6 %all-to-all-start.3 = ((f32[256,1,128]{2,1,0:T(1,128)}), f32[256,1,128]{2,1,0:T(1,128)S(1)}, u32[]{:S(2)}, u32[]{:S(2)}) async-start(f32[256,1,128]{2,1,0:T(1,128)} %copy-done.22), calls=%async_computation.3 | async-start | bytes 262144 | tf_op jit(solution)/shard_map/all_to_all | solution.py:534
  123.2 1.2 copy-done.4
  124.4 1.2 copy-done.6
  125.6 0.9 copy-done.18
  126.5 0.9 copy-done.20
  127.4 3.3 %other.1 = (bf16[256,2048]{1,0:T(8,128)(2,1)}, bf16[256,2048]{1,0:T(8,128)(2,1)}, bf16[256,128]{1,0:T(8,128)(2,1)}, bf16[256,128]{1,0:T(8,128)(2,1)}) custom-call(f32[16,64,128]{2,1,0:T(8,128)S(1)} %collective-permute-done.2.low_ref, f32[16,64,128]{2,1,0:T(8,128)} %collective-permute-done.3.high_ref, ...), custom_call_target="tpu_custom_call", output_to_operand_aliasing={{0}: (15, {}), {1}: (16, {})} | custom-call | flops 2000000000 | bytes 8388608 | tf_op jit(solution)/shard_map/other/pallas_call | solution.py:535
  130.7 5.5 %all-to-all-done.3.sums_ref = f32[256,1,128]{2,1,0:T(1,128)S(1)} async-done(((f32[256,1,128]{2,1,0:T(1,128)}), f32[256,1,128]{2,1,0:T(1,128)S(1)}, u32[]{:S(2)}, u32[]{:S(2)}) %all-to-all-start.3) | async-done | bytes 131104 | tf_op jit(solution)/shard_map/all_to_all | solution.py:534
  136.2 0.8 total.1
  (48 shorter events, 0.1 us)
Async XLA Ops:
  5.2 22.4 %collective-permute-start = (f32[16,64,128]{2,1,0:T(8,128)}, f32[16,64,128]{2,1,0:T(8,128)S(1)}, u32[]{:S(2)}, u32[]{:S(2)}) collective-permute-start(f32[16,64,128]{2,1,0:T(8,128)} %get-tuple-element.47.low_ref), channel_id=1, source_target_pairs={{0,1},{1,0},{2,3},{3,2},{4,5},{5,4},{6,7},{7,6},{8,9},{9,8},{10,11... | collective-permute-start | bytes 1572872 | tf_op jit(solution)/shard_map/ppermute | solution.py:468
  7.7 19.8 %collective-permute-start.1 = (f32[16,64,128]{2,1,0:T(8,128)}, f32[16,64,128]{2,1,0:T(8,128)S(1)}, u32[]{:S(2)}, u32[]{:S(2)}) collective-permute-start(f32[16,64,128]{2,1,0:T(8,128)} %get-tuple-element.48.high_ref), channel_id=1, source_target_pairs={{1,2},{2,1},{3,4},{4,3},{5,6},{6,5},{7,8},{8,7},{9,10},{10,9},{11,... | collective-permute-start | bytes 1572872 | tf_op jit(solution)/shard_map/ppermute | solution.py:468
  14.6 13.0 %all-to-all-start = ((f32[32,1,128]{2,1,0:T(1,128)}), f32[32,1,128]{2,1,0:T(1,128)S(1)}, u32[]{:S(2)}, u32[]{:S(2)}) async-start(f32[32,1,128]{2,1,0:T(1,128)} %get-tuple-element.49), calls=%async_computation | async-start | bytes 32768 | tf_op jit(solution)/shard_map/all_to_all | solution.py:499
  18.4 9.2 %copy-start.2 = (f32[32,64,128]{2,1,0:T(8,128)S(1)}, f32[32,64,128]{2,1,0:T(8,128)}, u32[]{:S(2)}) copy-start(f32[32,64,128]{2,1,0:T(8,128)} %get-tuple-element.46.keep_ref) | copy-start | bytes 3145732
  18.4 9.1 %copy-start.9 = (f32[32,256]{1,0:T(8,128)S(1)}, f32[32,256]{1,0:T(8,128)}, u32[]{:S(2)}) copy-start(f32[32,256]{1,0:T(8,128)} %get-tuple-element.52.refs_5_.cum_ref) | copy-start | bytes 98308
  58.7 28.8 %copy-start.11 = (f32[16,64,128]{2,1,0:T(8,128)S(1)}, f32[16,64,128]{2,1,0:T(8,128)}, u32[]{:S(2)}) copy-start(f32[16,64,128]{2,1,0:T(8,128)} %get-tuple-element.47.low_ref) | copy-start | bytes 1572868
  58.7 28.8 %copy-start.12 = (f32[16,64,128]{2,1,0:T(8,128)S(1)}, f32[16,64,128]{2,1,0:T(8,128)}, u32[]{:S(2)}) copy-start(f32[16,64,128]{2,1,0:T(8,128)} %get-tuple-element.48.high_ref) | copy-start | bytes 1572868
  88.7 16.6 %collective-permute-start.2 = (f32[16,64,128]{2,1,0:T(8,128)}, f32[16,64,128]{2,1,0:T(8,128)S(1)}, u32[]{:S(2)}, u32[]{:S(2)}) collective-permute-start(f32[16,64,128]{2,1,0:T(8,128)} %get-tuple-element.58), channel_id=1, source_target_pairs={{0,1},{1,0},{2,3},{3,2},{4,5},{5,4},{6,7},{7,6},{8,9},{9,8},{10,11... | collective-permute-start | bytes 1572872 | tf_op jit(solution)/shard_map/ppermute | solution.py:468
  92.8 8.1 %copy-start = (bf16[2048,256]{1,0:T(8,128)(2,1)S(1)}, bf16[2048,256]{1,0:T(8,128)(2,1)}, u32[]{:S(2)}) copy-start(bf16[2048,256]{1,0:T(8,128)(2,1)} %get-tuple-element.50.refs_1_.xt_ref) | copy-start | bytes 3145732
  92.8 8.1 %copy-start.1 = (bf16[2048,256]{1,0:T(8,128)(2,1)S(1)}, bf16[2048,256]{1,0:T(8,128)(2,1)}, u32[]{:S(2)}) copy-start(bf16[2048,256]{1,0:T(8,128)(2,1)} %get-tuple-element.51.refs_2_.gt_ref) | copy-start | bytes 3145732
  92.8 8.1 %copy-start.7 = (bf16[1,256,128]{2,1,0:T(8,128)(2,1)S(1)}, bf16[1,256,128]{2,1,0:T(8,128)(2,1)}, u32[]{:S(2)}) copy-start(bf16[1,256,128]{2,1,0:T(8,128)(2,1)} %param.8) | copy-start | bytes 196612
  92.8 8.1 %copy-start.8 = (bf16[1,256,128]{2,1,0:T(8,128)(2,1)S(1)}, bf16[1,256,128]{2,1,0:T(8,128)(2,1)}, u32[]{:S(2)}) copy-start(bf16[1,256,128]{2,1,0:T(8,128)(2,1)} %param.9) | copy-start | bytes 196612
  92.9 8.1 %copy-start.10 = (f32[32,256]{1,0:T(8,128)S(1)}, f32[32,256]{1,0:T(8,128)}, u32[]{:S(2)}) copy-start(f32[32,256]{1,0:T(8,128)} %get-tuple-element.52.refs_5_.cum_ref) | copy-start | bytes 98308
  92.9 12.5 %collective-permute-start.3 = (f32[16,64,128]{2,1,0:T(8,128)}, f32[16,64,128]{2,1,0:T(8,128)}, u32[]{:S(2)}, u32[]{:S(2)}) collective-permute-start(f32[16,64,128]{2,1,0:T(8,128)} %get-tuple-element.59), channel_id=1, source_target_pairs={{1,2},{2,1},{3,4},{4,3},{5,6},{6,5},{7,8},{8,7},{9,10},{10,9},{11,... | collective-permute-start | bytes 1572872 | tf_op jit(solution)/shard_map/ppermute | solution.py:468
  100.9 1.2 copy-start.3
  102.2 1.2 copy-start.5
  103.4 2.0 %copy-start.21 = (f32[1,32,256]{2,1,0:T(8,128)S(1)}, f32[1,32,256]{2,1,0:T(8,128)}, u32[]{:S(2)}) copy-start(f32[1,32,256]{2,1,0:T(8,128)} %param.10) | copy-start | bytes 98308
  103.4 2.0 %copy-start.23 = (f32[16,256]{1,0:T(8,128)S(1)}, f32[16,256]{1,0:T(8,128)}, u32[]{:S(2)}) copy-start(f32[16,256]{1,0:T(8,128)} %get-tuple-element.76.low_row_ref) | copy-start | bytes 49156
  103.4 2.0 %copy-start.24 = (f32[16,256]{1,0:T(8,128)S(1)}, f32[16,256]{1,0:T(8,128)}, u32[]{:S(2)}) copy-start(f32[16,256]{1,0:T(8,128)} %get-tuple-element.79.low_skiprow_ref) | copy-start | bytes 49156
  103.4 2.0 %copy-start.25 = (f32[16,256]{1,0:T(8,128)S(1)}, f32[16,256]{1,0:T(8,128)}, u32[]{:S(2)}) copy-start(f32[16,256]{1,0:T(8,128)} %get-tuple-element.77.high_row_ref) | copy-start | bytes 49156
  103.4 2.0 %copy-start.26 = (f32[16,256]{1,0:T(8,128)S(1)}, f32[16,256]{1,0:T(8,128)}, u32[]{:S(2)}) copy-start(f32[16,256]{1,0:T(8,128)} %get-tuple-element.80.high_skiprow_ref) | copy-start | bytes 49156
  105.3 3.5 %copy-start.17 = (f32[128,256]{1,0:T(8,128)}, f32[128,256]{1,0:T(8,128)S(1)}, u32[]{:S(2)}) copy-start(f32[128,256]{1,0:T(8,128)S(1)} %get-tuple-element.64.gct_ref) | copy-start | bytes 393220
  105.3 3.5 %copy-start.19 = (f32[128,256]{1,0:T(8,128)}, f32[128,256]{1,0:T(8,128)S(1)}, u32[]{:S(2)}) copy-start(f32[128,256]{1,0:T(8,128)S(1)} %get-tuple-element.65.gbt_ref) | copy-start | bytes 393220
  106.0 17.1 %copy-start.15 = (f32[256,128]{1,0:T(8,128)S(1)}, f32[256,128]{1,0:T(8,128)}, u32[]{:S(2)}) copy-start(f32[256,128]{1,0:T(8,128)} %get-tuple-element.69.high_gb_ref) | copy-start | bytes 393220
  106.0 17.1 %copy-start.16 = (f32[256,128]{1,0:T(8,128)S(1)}, f32[256,128]{1,0:T(8,128)}, u32[]{:S(2)}) copy-start(f32[256,128]{1,0:T(8,128)} %get-tuple-element.67.high_gc_ref) | copy-start | bytes 393220
  109.5 13.7 %copy-start.13 = (f32[256,128]{1,0:T(8,128)S(1)}, f32[256,128]{1,0:T(8,128)}, u32[]{:S(2)}) copy-start(f32[256,128]{1,0:T(8,128)} %get-tuple-element.68.low_gb_ref) | copy-start | bytes 393220
  109.5 13.7 %copy-start.14 = (f32[256,128]{1,0:T(8,128)S(1)}, f32[256,128]{1,0:T(8,128)}, u32[]{:S(2)}) copy-start(f32[256,128]{1,0:T(8,128)} %get-tuple-element.66.low_gc_ref) | copy-start | bytes 393220
  109.5 26.7 %all-to-all-start.3 = ((f32[256,1,128]{2,1,0:T(1,128)}), f32[256,1,128]{2,1,0:T(1,128)S(1)}, u32[]{:S(2)}, u32[]{:S(2)}) async-start(f32[256,1,128]{2,1,0:T(1,128)} %copy-done.22), calls=%async_computation.3 | async-start | bytes 262144 | tf_op jit(solution)/shard_map/all_to_all | solution.py:534
  123.2 1.2 copy-start.4
  124.4 1.2 copy-start.6
  125.6 0.9 copy-start.18
  126.5 0.9 copy-start.20
  (2 other events, 1.3 us)

commit v4 on v3

--- a/solution.py
+++ b/solution.py
@@ -20,7 +20,7 @@
 F32 = jnp.float32
 BF16 = jnp.bfloat16
 EXACT = lax.Precision.HIGHEST
-VMEM_LIMIT = 24 * 1024 * 1024
+VMEM_LIMIT = 16 * 1024 * 1024
 LARGE_LIMIT = 60 * 1024 * 1024
 
 
@@ -276,7 +276,7 @@
         input_output_aliases={7 + i: i for i in range(len(earlier))},
         scratch_shapes=[pltpu.VMEM((GROUP, GROUP), F32), pltpu.VMEM((GROUP, GROUP), F32)],
         cost=cost(4),
-        limit=LARGE_LIMIT,
+        limit=VMEM_LIMIT if earlier else LARGE_LIMIT,
     )(g, xt, gt, b, c, cum, skip, *earlier)
 
 
@@ -498,7 +498,7 @@
     low_in, high_in = swap(low, high)
     gains = lax.all_to_all(gain, "seq", 0, 0, tiled=True)
     yt, gxt, low_row, low_skiprow, low_gb, low_gc = inner(0, g, xt, gt, b, c, cum, skip)
-    low_in, high_in, gains, yt, gxt = lax.optimization_barrier((low_in, high_in, gains, yt, gxt))
+    low_in, high_in, yt, gxt = lax.optimization_barrier((low_in, high_in, yt, gxt))
     joined = call(join_kernel, "join", all_heads)(keep, low_in, high_in, cum)
     parts = lax.all_to_all(joined, "seq", 0, 0, tiled=True)
     scanned = call(scan_kernel, "scan", all_heads)(parts, gains)
@@ -541,6 +541,7 @@
         input_output_aliases={15: 0, 16: 1},
         scratch_shapes=out_scratch,
         cost=cost(4),
+        limit=LARGE_LIMIT,
     )(
         low_back, high_back, yt, gxt, xt, gt, b, c, cum, gct, gbt,
         low_gc, high_gc, low_gb, high_gb, y, gx,

time: 138 us -> 134 us (0.971)
  local copies, waits for them, and re-layouts: 8.05 us -> 2.02 us
  waiting for transfers between devices: 9.83 us -> 13.8 us
  Pallas kernels: 24.2 us -> 22.5 us
    unnamed x56 -> x48, local copies, waits for them, and re-layouts: 8.05 us -> 2.02 us
    ppermute x2, waiting for transfers between devices: 0.01 us -> 4.51 us  [swap(): lax.ppermute(high, 'seq', high_pairs)]
    all_to_all x1, waiting for transfers between devices: 4.35 us -> 1.2 us  [shards(): gains = lax.all_to_all(gain, 'seq', 0, 0, tiled=True)]
    all_to_all x1, waiting for transfers between devices: 5.46 us -> 8.05 us  [shards(): sums = lax.all_to_all(copies, ('dp', 'seq'), 0, 0, tiled=True)]
    pallas_call x1, Pallas kernels: 3.28 us -> 4.96 us  [shards(): call(other_kernel, 'other', [tall, tall, shape_of((GROUP, STATE), BF16),...]
    pallas_call x2, Pallas kernels: 9.42 us -> 7.89 us  [inner(): call(functools.partial(inner_kernel, offset), 'inner', [wide, wide, rows,...]
  transfers between devices with their start and end apart: 6 -> 6, of which waited for: 2 -> 4; matrix products, arithmetic and copies ran while one was open for 0% -> 0% of each run, Pallas kernels for 11% -> 11%
where the time goes in v4:
time: 134 us; the launch traced here: 133 us
  blocking collectives  59.8 us (45%)
  starting transfers between devices  34.3 us (26%)
  Pallas kernels  22.5 us (17%)
  waiting for transfers between devices  13.8 us (10%)
  local copies, waits for them, and re-layouts  2.02 us (2%)
    all_to_all x1, blocking collectives, shards(): parts = lax.all_to_all(joined, 'seq', 0, 0, tiled=True)  30.9 us
    all_to_all x1, blocking collectives, shards(): mine = lax.all_to_all(scanned, 'seq', 0, 0, tiled=True)  28.9 us
    all_to_all x1, starting transfers between devices, shards(): sums = lax.all_to_all(copies, ('dp', 'seq'), 0, 0, tiled=True)  13.5 us
    ppermute x2, starting transfers between devices, swap(): lax.ppermute(high, 'seq', high_pairs)  10.1 us
    all_to_all x1, waiting for transfers between devices, shards(): sums = lax.all_to_all(copies, ('dp', 'seq'), 0, 0, tiled=True)  8.05 us
    pallas_call x2, Pallas kernels, inner(): call(functools.partial(inner_kernel, offset), 'inner', [wide, wide, rows,...  7.89 us
    ppermute x2, starting transfers between devices, swap(): lax.ppermute(low, 'seq', low_pairs)  6.79 us
    pallas_call x1, Pallas kernels, shards(): call(other_kernel, 'other', [tall, tall, shape_of((GROUP, STATE), BF16),...  4.96 us
  transfers between devices with their start and end apart: 6, of which 4 were waited for; matrix products, arithmetic and copies ran while one was open for 0% of the time, Pallas kernels for 11%

profile of v4, /device:TPU:1, one launch (start us, length us, event | category | flops | bytes accessed | tf_op | source)
XLA Modules:
  0.0 133.4 jit_solution(9628717807225120392)
XLA Ops:
  0.6 4.5 %states.1 = (f32[16,64,128]{2,1,0:T(8,128)}, f32[16,64,128]{2,1,0:T(8,128)}, f32[32,64,128]{2,1,0:T(8,128)}, f32[32,1,128]{2,1,0:T(1,128)}, bf16[2048,256]{1,0:T...) custom-call(bf16[256,2048]{1,0:T(8,128)(2,1)} %bitcast.32, bf16[256,2048]{1,0:T(8,128)(2,1)} %bitcast.13, ...), custom_call_target="tpu_custom_call" | custom-call | tf_op jit(solution)/shard_map/states/pallas_call | solution.py:482
  5.2 2.6 %collective-permute-start = (f32[16,64,128]{2,1,0:T(8,128)}, f32[16,64,128]{2,1,0:T(8,128)S(1)}, u32[]{:S(2)}, u32[]{:S(2)}) collective-permute-start(f32[16,64,128]{2,1,0:T(8,128)} %get-tuple-element.46.low_ref), channel_id=1, source_target_pairs={{0,1},{1,0},{2,3},{3,2},{4,5},{5,4},{6,7},{7,6},{8,9},{9,8},{10,11... | collective-permute-start | bytes 1572872 | tf_op jit(solution)/shard_map/ppermute | solution.py:468
  7.7 6.9 %collective-permute-start.1 = (f32[16,64,128]{2,1,0:T(8,128)}, f32[16,64,128]{2,1,0:T(8,128)S(1)}, u32[]{:S(2)}, u32[]{:S(2)}) collective-permute-start(f32[16,64,128]{2,1,0:T(8,128)} %get-tuple-element.47.high_ref), channel_id=1, source_target_pairs={{1,2},{2,1},{3,4},{4,3},{5,6},{6,5},{7,8},{8,7},{9,10},{10,9},{11,... | collective-permute-start | bytes 1572872 | tf_op jit(solution)/shard_map/ppermute | solution.py:468
  14.6 3.8 %all-to-all-start.1 = ((f32[32,1,128]{2,1,0:T(1,128)}), f32[32,1,128]{2,1,0:T(1,128)S(1)}, u32[]{:S(2)}, u32[]{:S(2)}) async-start(f32[32,1,128]{2,1,0:T(1,128)} %get-tuple-element.55), calls=%async_computation.1 | async-start | bytes 32768 | tf_op jit(solution)/shard_map/all_to_all | solution.py:499
  18.4 0.0 copy-start.4
  18.4 4.8 %inner.2 = (bf16[2048,256]{1,0:T(8,128)(2,1)}, bf16[2048,256]{1,0:T(8,128)(2,1)}, f32[16,256]{1,0:T(8,128)}, f32[16,256]{1,0:T(8,128)}, f32[256,128]{1,0:T(8,128)}, /*index=5*/f32[256,128]{1,0:T(8,128)}) custom-call(bf16[256,2048]{1,0:T(8,128)(2,1)} %bitcast.14, bf16[2048,256]{1,0:T(8,128)(2,1)} %get-tuple-element.48.refs_1_.xt_ref, ...), custom_call_target="tpu_custom_call" | custom-call | flops 2000000000 | bytes 8388608 | tf_op jit(solution)/shard_map/inner/pallas_call | solution.py:265
  23.2 0.0 collective-permute-done.low_ref
  23.2 2.9 %collective-permute-done.1.high_ref = f32[16,64,128]{2,1,0:T(8,128)S(1)} collective-permute-done((f32[16,64,128]{2,1,0:T(8,128)}, f32[16,64,128]{2,1,0:T(8,128)S(1)}, u32[]{:S(2)}, u32[]{:S(2)}) %collective-permute-start.1) | collective-permute-done | bytes 524320 | tf_op jit(solution)/shard_map/ppermute | solution.py:468
  26.1 0.2 join.1
  26.3 1.2 all-to-all-done.1.gain_ref
  27.6 30.9 %all_to_all.20.part_ref = f32[32,64,128]{2,1,0:T(8,128)S(1)} all-to-all(f32[32,64,128]{2,1,0:T(8,128)S(1)} %join.1), channel_id=1, replica_groups=mesh['dp'=8,'seq'=32] {'seq'}, dimensions={0} | all-to-all | bytes 2097152 | tf_op jit(solution)/shard_map/all_to_all | solution.py:503
  58.5 0.1 scan.1
  58.6 0.0 copy-start.5
  58.6 0.0 copy-start.6
  58.6 28.9 %all_to_all.21.mine_ref = f32[32,64,128]{2,1,0:T(8,128)S(1)} all-to-all(f32[32,64,128]{2,1,0:T(8,128)S(1)} %scan.1), channel_id=1, replica_groups=mesh['dp'=8,'seq'=32] {'seq'}, dimensions={0} | all-to-all | bytes 2097152 | tf_op jit(solution)/shard_map/all_to_all | solution.py:505
  87.5 0.2 pass_on.1
  87.8 0.0 copy-start.23
  87.8 4.2 %collective-permute-start.2 = (f32[16,64,128]{2,1,0:T(8,128)S(1)}, f32[16,64,128]{2,1,0:T(8,128)S(1)}, u32[]{:S(2)}, u32[]{:S(2)}) collective-permute-start(f32[16,64,128]{2,1,0:T(8,128)S(1)} %get-tuple-element.56), channel_id=1, source_target_pairs={{0,1},{1,0},{2,3},{3,2},{4,5},{5,4},{6,7},{7,6},{8,9},{9,8},{10,11... | collective-permute-start | bytes 1572872 | tf_op jit(solution)/shard_map/ppermute | solution.py:468
  92.0 3.3 %collective-permute-start.3 = (f32[16,64,128]{2,1,0:T(8,128)S(1)}, f32[16,64,128]{2,1,0:T(8,128)S(1)}, u32[]{:S(2)}, u32[]{:S(2)}) collective-permute-start(f32[16,64,128]{2,1,0:T(8,128)S(1)} %get-tuple-element.57), channel_id=1, source_target_pairs={{1,2},{2,1},{3,4},{4,3},{5,6},{6,5},{7,8},{8,7},{9,10},{10,9},{11,... | collective-permute-start | bytes 1572872 | tf_op jit(solution)/shard_map/ppermute | solution.py:468
  95.4 3.1 %inner.3 = (bf16[2048,256]{1,0:T(8,128)(2,1)S(1)}, bf16[2048,256]{1,0:T(8,128)(2,1)S(1)}, f32[16,256]{1,0:T(8,128)S(1)}, f32[16,256]{1,0:T(8,128)S(1)}, f32[256,128]{1,0:T(8,128)S(1)}, /*index=5*/f32[256,128]{1,0:T(8,128)S(1)}) custom-call(bf16[256,2048]{1,0:T(8,128)(2,1)S(1)} %bitcast.15, ...), custom_call_target="tpu_custom_call", output_to_operand_aliasing={{0}: (7, {}), {1}: (8, {})} | custom-call | flops 2000000000 | bytes 8388608 | tf_op jit(solution)/shard_map/inner/pallas_call | solution.py:265
  98.5 0.6 copy-done.15
  99.2 0.6 copy-done.16
  99.8 0.0 copy-start.21
  99.8 1.9 %own.1 = (bf16[256,2048]{1,0:T(8,128)(2,1)}, bf16[256,2048]{1,0:T(8,128)(2,1)}, f32[32,256]{1,0:T(8,128)S(1)}, f32[128,256]{1,0:T(8,128)S(1)}, f32[128,256]{1,0:T(8,128)S(1)}) custom-call(f32[32,64,128]{2,1,0:T(8,128)S(1)} %all_to_all.21.mine_ref, bf16[2048,256]{1,0:T(8,128)(2,1)S(1)} %get-tuple-element.60.yt_ref, ...), custom_call_target="tpu_custom_call" | custom-call | flops 2000000000 | bytes 8388608 | tf_op jit(solution)/shard_map/own/pallas_call | solution.py:516
  101.8 0.0 collective-permute-done.2.low_ref
  101.8 1.6 %collective-permute-done.3.high_ref = f32[16,64,128]{2,1,0:T(8,128)S(1)} collective-permute-done((f32[16,64,128]{2,1,0:T(8,128)S(1)}, f32[16,64,128]{2,1,0:T(8,128)S(1)}, u32[]{:S(2)}, u32[]{:S(2)}) %collective-permute-start.3) | collective-permute-done | bytes 524320 | tf_op jit(solution)/shard_map/ppermute | solution.py:468
  103.4 0.6 copy-done.22
  104.0 1.9 %sums.1 = (f32[32,256]{1,0:T(8,128)}, f32[256,1,128]{2,1,0:T(1,128)}) custom-call(f32[32,64,128]{2,1,0:T(8,128)S(1)} %all_to_all.21.mine_ref, f32[16,64,128]{2,1,0:T(8,128)S(1)} %collective-permute-done.2.low_ref, f32[16,64,128]{2,1,0:T(8,128)S(1)} %collective-permute-done.3.high_ref, bf16[2048,256]{1,0:T(8,128)(2,1)S(1)} %copy-done, ...), custom_call_target="tpu_custom_call" | custom-call | tf_op jit(solution)/shard_map/sums/pallas_call | solution.py:525
  106.0 13.5 %all-to-all-start.3 = ((f32[256,1,128]{2,1,0:T(1,128)}), f32[256,1,128]{2,1,0:T(1,128)S(1)}, u32[]{:S(2)}, u32[]{:S(2)}) async-start(f32[256,1,128]{2,1,0:T(1,128)} %get-tuple-element.80), calls=%async_computation.3 | async-start | bytes 262144 | tf_op jit(solution)/shard_map/all_to_all | solution.py:534
  119.5 5.0 %other.1 = (bf16[256,2048]{1,0:T(8,128)(2,1)}, bf16[256,2048]{1,0:T(8,128)(2,1)}, bf16[256,128]{1,0:T(8,128)(2,1)}, bf16[256,128]{1,0:T(8,128)(2,1)}) custom-call(f32[16,64,128]{2,1,0:T(8,128)} %copy-done.2, f32[16,64,128]{2,1,0:T(8,128)} %copy-done.3, bf16[2048,256]{1,0:T(8,128)(2,1)} %copy-done.7, ...), custom_call_target="tpu_custom_call", output_to_operand_aliasing={{0}: (15, {}), {1}: (16, {})} | custom-call | flops 2000000000 | bytes 8388608 | tf_op jit(solution)/shard_map/other/pallas_call | solution.py:535
  124.5 8.1 %all-to-all-done.3.sums_ref = f32[256,1,128]{2,1,0:T(1,128)S(1)} async-done(((f32[256,1,128]{2,1,0:T(1,128)}), f32[256,1,128]{2,1,0:T(1,128)S(1)}, u32[]{:S(2)}, u32[]{:S(2)}) %all-to-all-start.3) | async-done | bytes 131104 | tf_op jit(solution)/shard_map/all_to_all | solution.py:534
  132.5 0.8 total.1
  (40 shorter events, 0.1 us)
Async XLA Ops:
  5.2 18.0 %collective-permute-start = (f32[16,64,128]{2,1,0:T(8,128)}, f32[16,64,128]{2,1,0:T(8,128)S(1)}, u32[]{:S(2)}, u32[]{:S(2)}) collective-permute-start(f32[16,64,128]{2,1,0:T(8,128)} %get-tuple-element.46.low_ref), channel_id=1, source_target_pairs={{0,1},{1,0},{2,3},{3,2},{4,5},{5,4},{6,7},{7,6},{8,9},{9,8},{10,11... | collective-permute-start | bytes 1572872 | tf_op jit(solution)/shard_map/ppermute | solution.py:468
  7.7 18.4 %collective-permute-start.1 = (f32[16,64,128]{2,1,0:T(8,128)}, f32[16,64,128]{2,1,0:T(8,128)S(1)}, u32[]{:S(2)}, u32[]{:S(2)}) collective-permute-start(f32[16,64,128]{2,1,0:T(8,128)} %get-tuple-element.47.high_ref), channel_id=1, source_target_pairs={{1,2},{2,1},{3,4},{4,3},{5,6},{6,5},{7,8},{8,7},{9,10},{10,9},{11,... | collective-permute-start | bytes 1572872 | tf_op jit(solution)/shard_map/ppermute | solution.py:468
  14.6 13.0 %all-to-all-start.1 = ((f32[32,1,128]{2,1,0:T(1,128)}), f32[32,1,128]{2,1,0:T(1,128)S(1)}, u32[]{:S(2)}, u32[]{:S(2)}) async-start(f32[32,1,128]{2,1,0:T(1,128)} %get-tuple-element.55), calls=%async_computation.1 | async-start | bytes 32768 | tf_op jit(solution)/shard_map/all_to_all | solution.py:499
  18.4 7.7 %copy-start.4 = (f32[32,64,128]{2,1,0:T(8,128)S(1)}, f32[32,64,128]{2,1,0:T(8,128)}, u32[]{:S(2)}) copy-start(f32[32,64,128]{2,1,0:T(8,128)} %get-tuple-element.45.keep_ref) | copy-start | bytes 3145732
  18.4 7.7 %copy-start.12 = (f32[32,256]{1,0:T(8,128)S(1)}, f32[32,256]{1,0:T(8,128)}, u32[]{:S(2)}) copy-start(f32[32,256]{1,0:T(8,128)} %get-tuple-element.50.refs_5_.cum_ref) | copy-start | bytes 98308
  27.5 60.0 %copy-start.14 = (f32[16,64,128]{2,1,0:T(8,128)S(1)}, f32[16,64,128]{2,1,0:T(8,128)}, u32[]{:S(2)}) copy-start(f32[16,64,128]{2,1,0:T(8,128)} %get-tuple-element.47.high_ref) | copy-start | bytes 1572868
  58.5 29.1 %copy-start.13 = (f32[16,64,128]{2,1,0:T(8,128)S(1)}, f32[16,64,128]{2,1,0:T(8,128)}, u32[]{:S(2)}) copy-start(f32[16,64,128]{2,1,0:T(8,128)} %get-tuple-element.46.low_ref) | copy-start | bytes 1572868
  58.5 36.8 %copy-start.8 = (bf16[2048,256]{1,0:T(8,128)(2,1)S(1)}, bf16[2048,256]{1,0:T(8,128)(2,1)}, u32[]{:S(2)}) copy-start(bf16[2048,256]{1,0:T(8,128)(2,1)} %get-tuple-element.59.refs_8_) | copy-start | bytes 3145732
  58.5 36.8 %copy-start.10 = (bf16[1,256,128]{2,1,0:T(8,128)(2,1)S(1)}, bf16[1,256,128]{2,1,0:T(8,128)(2,1)}, u32[]{:S(2)}) copy-start(bf16[1,256,128]{2,1,0:T(8,128)(2,1)} %param.8) | copy-start | bytes 196612
  58.5 36.8 %copy-start.11 = (bf16[1,256,128]{2,1,0:T(8,128)(2,1)S(1)}, bf16[1,256,128]{2,1,0:T(8,128)(2,1)}, u32[]{:S(2)}) copy-start(bf16[1,256,128]{2,1,0:T(8,128)(2,1)} %param.9) | copy-start | bytes 196612
  58.6 36.7 %copy-start.5 = (bf16[1,256,2048]{2,1,0:T(8,128)(2,1)S(1)}, bf16[1,256,2048]{2,1,0:T(8,128)(2,1)}, u32[]{:S(2)}) copy-start(bf16[1,256,2048]{2,1,0:T(8,128)(2,1)} %param.13) | copy-start | bytes 3145732
  58.6 36.7 %copy-start.6 = (bf16[2048,256]{1,0:T(8,128)(2,1)S(1)}, bf16[2048,256]{1,0:T(8,128)(2,1)}, u32[]{:S(2)}) copy-start(bf16[2048,256]{1,0:T(8,128)(2,1)} %get-tuple-element.58.refs_7_) | copy-start | bytes 3145732
  87.5 7.8 %copy-start = (bf16[2048,256]{1,0:T(8,128)(2,1)S(1)}, bf16[2048,256]{1,0:T(8,128)(2,1)}, u32[]{:S(2)}) copy-start(bf16[2048,256]{1,0:T(8,128)(2,1)} %get-tuple-element.48.refs_1_.xt_ref) | copy-start | bytes 3145732
  87.5 7.8 %copy-start.1 = (bf16[2048,256]{1,0:T(8,128)(2,1)S(1)}, bf16[2048,256]{1,0:T(8,128)(2,1)}, u32[]{:S(2)}) copy-start(bf16[2048,256]{1,0:T(8,128)(2,1)} %get-tuple-element.49.refs_2_.gt_ref) | copy-start | bytes 3145732
  87.8 7.6 %copy-start.23 = (f32[32]{0:T(128)S(1)}, f32[32]{0:T(128)}, u32[]{:S(2)}) copy-start(f32[32]{0:T(128)} %refs_6_.3) | copy-start | bytes 388
  87.8 14.0 %collective-permute-start.2 = (f32[16,64,128]{2,1,0:T(8,128)S(1)}, f32[16,64,128]{2,1,0:T(8,128)S(1)}, u32[]{:S(2)}, u32[]{:S(2)}) collective-permute-start(f32[16,64,128]{2,1,0:T(8,128)S(1)} %get-tuple-element.56), channel_id=1, source_target_pairs={{0,1},{1,0},{2,3},{3,2},{4,5},{5,4},{6,7},{7,6},{8,9},{9,8},{10,11... | collective-permute-start | bytes 1572872 | tf_op jit(solution)/shard_map/ppermute | solution.py:468
  92.0 11.4 %collective-permute-start.3 = (f32[16,64,128]{2,1,0:T(8,128)S(1)}, f32[16,64,128]{2,1,0:T(8,128)S(1)}, u32[]{:S(2)}, u32[]{:S(2)}) collective-permute-start(f32[16,64,128]{2,1,0:T(8,128)S(1)} %get-tuple-element.57), channel_id=1, source_target_pairs={{1,2},{2,1},{3,4},{4,3},{5,6},{6,5},{7,8},{8,7},{9,10},{10,9},{11,... | collective-permute-start | bytes 1572872 | tf_op jit(solution)/shard_map/ppermute | solution.py:468
  98.5 0.7 copy-start.15
  99.2 0.7 copy-start.16
  99.8 1.9 %copy-start.7 = (bf16[2048,256]{1,0:T(8,128)(2,1)}, bf16[2048,256]{1,0:T(8,128)(2,1)S(1)}, u32[]{:S(2)}) copy-start(bf16[2048,256]{1,0:T(8,128)(2,1)S(1)} %get-tuple-element.60.yt_ref) | copy-start | bytes 3145732
  99.8 1.9 %copy-start.9 = (bf16[2048,256]{1,0:T(8,128)(2,1)}, bf16[2048,256]{1,0:T(8,128)(2,1)S(1)}, u32[]{:S(2)}) copy-start(bf16[2048,256]{1,0:T(8,128)(2,1)S(1)} %get-tuple-element.61.gxt_ref) | copy-start | bytes 3145732
  99.8 3.6 %copy-start.19 = (f32[1,32,256]{2,1,0:T(8,128)S(1)}, f32[1,32,256]{2,1,0:T(8,128)}, u32[]{:S(2)}) copy-start(f32[1,32,256]{2,1,0:T(8,128)} %param.10) | copy-start | bytes 98308
  99.8 3.6 %copy-start.20 = (f32[16,256]{1,0:T(8,128)S(1)}, f32[16,256]{1,0:T(8,128)}, u32[]{:S(2)}) copy-start(f32[16,256]{1,0:T(8,128)} %get-tuple-element.74.low_row_ref) | copy-start | bytes 49156
  99.8 3.6 %copy-start.21 = (f32[16,256]{1,0:T(8,128)S(1)}, f32[16,256]{1,0:T(8,128)}, u32[]{:S(2)}) copy-start(f32[16,256]{1,0:T(8,128)} %get-tuple-element.77.low_skiprow_ref) | copy-start | bytes 49156
  101.7 4.2 %copy-start.17 = (f32[128,256]{1,0:T(8,128)}, f32[128,256]{1,0:T(8,128)S(1)}, u32[]{:S(2)}) copy-start(f32[128,256]{1,0:T(8,128)S(1)} %get-tuple-element.62.gct_ref) | copy-start | bytes 393220
  101.7 4.2 %copy-start.18 = (f32[128,256]{1,0:T(8,128)}, f32[128,256]{1,0:T(8,128)S(1)}, u32[]{:S(2)}) copy-start(f32[128,256]{1,0:T(8,128)S(1)} %get-tuple-element.63.gbt_ref) | copy-start | bytes 393220
  101.8 4.2 %copy-start.2 = (f32[16,64,128]{2,1,0:T(8,128)}, f32[16,64,128]{2,1,0:T(8,128)S(1)}, u32[]{:S(2)}) copy-start(f32[16,64,128]{2,1,0:T(8,128)S(1)} %collective-permute-done.2.low_ref) | copy-start | bytes 1572868
  103.4 2.6 %copy-start.3 = (f32[16,64,128]{2,1,0:T(8,128)}, f32[16,64,128]{2,1,0:T(8,128)S(1)}, u32[]{:S(2)}) copy-start(f32[16,64,128]{2,1,0:T(8,128)S(1)} %collective-permute-done.3.high_ref) | copy-start | bytes 1572868
  103.4 0.7 copy-start.22
  106.0 26.6 %all-to-all-start.3 = ((f32[256,1,128]{2,1,0:T(1,128)}), f32[256,1,128]{2,1,0:T(1,128)S(1)}, u32[]{:S(2)}, u32[]{:S(2)}) async-start(f32[256,1,128]{2,1,0:T(1,128)} %get-tuple-element.80), calls=%async_computation.3 | async-start | bytes 262144 | tf_op jit(solution)/shard_map/all_to_all | solution.py:534

commit v5 on v4

--- a/solution.py
+++ b/solution.py
@@ -1,5 +1,3 @@
-import functools
-
 import jax
 import jax.numpy as jnp
 from jax import lax
@@ -16,6 +14,7 @@
 GRID = HEADS // STEP
 HALF = HEADS // 2
 HALF_STEPS = GRID // 2
+ROWS = SIZE + 1
 
 F32 = jnp.float32
 BF16 = jnp.bfloat16
@@ -84,47 +83,46 @@
 
 def states_kernel(
     x_hbm, g_hbm, b_hbm, c_hbm, dt_hbm, alog_hbm,
-    low_ref, high_ref, keep_ref, gain_ref, xt_ref, gt_ref, cum_ref,
-    x_s, g_s, b_s, c_s, dt_s, alog_s, sems,
+    low_hbm, high_hbm, keep_hbm, xt_hbm, gt_hbm, cum_ref, rate_ref,
+    x_s, g_s, b_s, c_s, dt_s, alog_s, send_s, keep_s, xt_s, gt_s, sems, out_sems,
 ):
-    def copy(source, target, slot):
-        made = pltpu.make_async_copy(source, target, sems.at[slot])
+    def copy(source, target, sem):
+        made = pltpu.make_async_copy(source, target, sem)
         made.start()
         return made
 
-    alog_copy = copy(alog_hbm, alog_s, 0)
-    dt_copy = copy(dt_hbm, dt_s, 1)
-    b_copy = copy(b_hbm, b_s, 2)
-    c_copy = copy(c_hbm, c_s, 3)
+    alog_copy = copy(alog_hbm, alog_s, sems.at[0])
+    dt_copy = copy(dt_hbm, dt_s, sems.at[1])
+    b_copy = copy(b_hbm, b_s, sems.at[2])
+    c_copy = copy(c_hbm, c_s, sems.at[3])
     inputs = []
     for i in range(GRID):
         lanes = pl.ds(i * WIDE, WIDE)
         inputs.append(
             (
-                copy(x_hbm.at[:, lanes], x_s.at[i], 4 + 2 * i),
-                copy(g_hbm.at[:, lanes], g_s.at[i], 5 + 2 * i),
+                copy(x_hbm.at[:, lanes], x_s.at[i], sems.at[4 + 2 * i]),
+                copy(g_hbm.at[:, lanes], g_s.at[i], sems.at[5 + 2 * i]),
             )
         )
     alog_copy.wait()
     dt_copy.wait()
     rate = jnp.exp(column(alog_s[...]))
+    rate_ref[...] = jnp.broadcast_to(rate, (HEADS, STATE))
     cum_all = dot(-rate * dt_s[...], triangle(), 1, 0, EXACT)
     cum_ref[...] = cum_all
     b_copy.wait()
     c_copy.wait()
+    outputs = []
     for i in range(GRID):
         for made in inputs[i]:
             made.wait()
         cum = cum_all[i * STEP : (i + 1) * STEP]
-        last = cum[:, GROUP - 1 :]
-        to_end = jnp.exp(last - cum)
+        to_end = jnp.exp(cum[:, GROUP - 1 :] - cum)
         from_start = jnp.exp(cum)
-        gain = jnp.exp(last)
         xt = x_s[i].T
         gt = g_s[i].T
-        rows = pl.ds(i * WIDE, WIDE)
-        xt_ref[rows, :] = xt
-        gt_ref[rows, :] = gt
+        xt_s[i] = xt
+        gt_s[i] = gt
         scaled = (xt.astype(F32) * spread(to_end)).astype(BF16)
         raised = (gt.astype(F32) * spread(from_start)).astype(BF16)
         state = dot(scaled, b_s[...], 1, 0)
@@ -132,28 +130,48 @@
         first = keeps_adjoint(i)
         send = jnp.where(first, state, adjoint) * unpaired(i)
         keep = jnp.where(first, adjoint, state)
-        send_ref = low_ref if i < HALF_STEPS else high_ref
-        base = i % HALF_STEPS * STEP
-        for j in range(STEP):
-            part = slice(j * SIZE, (j + 1) * SIZE)
-            send_ref[base + j] = send[part]
-            keep_ref[i * STEP + j] = keep[part]
-            gain_ref[i * STEP + j] = jnp.broadcast_to(gain[j : j + 1], (1, STATE))
+        send_s[i] = send.reshape(STEP, SIZE, STATE)
+        keep_s[i] = keep.reshape(STEP, SIZE, STATE)
+        send_hbm = low_hbm if i < HALF_STEPS else high_hbm
+        rows = pl.ds(i * WIDE, WIDE)
+        for k, (source, target) in enumerate(
+            (
+                (send_s, send_hbm.at[pl.ds(i % HALF_STEPS * STEP, STEP)]),
+                (keep_s, keep_hbm.at[pl.ds(i * STEP, STEP)]),
+                (xt_s, xt_hbm.at[rows]),
+                (gt_s, gt_hbm.at[rows]),
+            )
+        ):
+            outputs.append(copy(source.at[i], target, out_sems.at[4 * i + k]))
+    for made in outputs:
+        made.wait()
+
+
+def head_part(h):
+    return slice(h * ROWS, h * ROWS + SIZE), slice(h * ROWS + SIZE, (h + 1) * ROWS)
 
 
 def join_kernel(keep_ref, low_ref, high_ref, cum_ref, out_ref):
     gain = jnp.exp(cum_ref[:, GROUP - 1 :])
     for h in range(HEADS):
         other = low_ref[h] if h < HALF else high_ref[h - HALF]
-        out_ref[h] = keep_ref[h] + gain[h : h + 1] * other
-
-
-def scan_kernel(part_ref, gain_ref, out_ref):
-    count = part_ref.shape[0]
+        matrix, decay = head_part(h)
+        out_ref[matrix, :] = keep_ref[h] + gain[h : h + 1] * other
+        out_ref[decay, :] = jnp.broadcast_to(gain[h : h + 1], (1, STATE))
+
+
+def scan_kernel(part_ref, out_ref):
+    count = out_ref.shape[0]
     low = lax.axis_index("seq") < HALF
 
+    def matrix(k):
+        return part_ref[head_part(k)[0], :]
+
+    def gain(k):
+        return part_ref[head_part(k)[1], :]
+
     def pair(first, second, carried, mine):
-        return gain_ref[first] * gain_ref[second] * carried + part_ref[mine]
+        return gain(first) * gain(second) * carried + matrix(mine)
 
     nothing = jnp.zeros((SIZE, STATE), F32)
 
@@ -170,12 +188,12 @@
 
     @pl.when(jnp.logical_not(low))
     def _():
-        state = part_ref[0]
+        state = matrix(0)
         for k in range(1, count - 1, 2):
             out_ref[k] = state
             state = pair(k, k + 1, state, k + 1)
         out_ref[count - 1] = state
-        adjoint = part_ref[count - 1]
+        adjoint = matrix(count - 1)
         for k in reversed(range(1, count - 1, 2)):
             out_ref[k + 1] = adjoint
             adjoint = pair(k, k + 1, adjoint, k)
@@ -191,14 +209,15 @@
         out_high_ref[h] = high_ref[h] + high_gain[h : h + 1] * mine_ref[HALF + h]
 
 
-def inner_kernel(offset, *refs):
-    (g_ref, xt_ref, gt_ref, b_ref, c_ref, cum_ref, skip_ref), refs = refs[:7], refs[7:]
-    (y_ref, gx_ref, row_ref, skiprow_ref, gb_ref, gc_ref, cb_s, acc_s) = refs[-8:]
-    place = pl.program_id(0)
-    step = place + offset
+def inner_kernel(
+    g_ref, xt_ref, gt_ref, b_ref, c_ref, cum_ref, skip_ref,
+    y_ref, gx_ref, row_ref, skiprow_ref, gb_ref, gc_ref,
+    cb_s, acc_s,
+):
+    step = pl.program_id(0)
     half = GROUP // 2
 
-    @pl.when(place == 0)
+    @pl.when(step == 0)
     def _():
         cb_s[...] = dot(c_ref[...], b_ref[...], 1, 1)
         acc_s[...] = jnp.zeros_like(acc_s)
@@ -244,40 +263,37 @@
         skip = skip_ref[step * STEP + j]
         y_ref[low:high, :] = (yt + skip * xf).astype(BF16)
         gx_ref[low:high, :] = (gxt + skip * gf).astype(BF16)
-    here = pl.ds(pl.multiple_of(place * STEP, STEP), STEP)
-    row_ref[here, :] = jnp.concatenate(rows, axis=0)
-    skiprow_ref[here, :] = jnp.concatenate(skips, axis=0)
-
-    @pl.when(place == HALF_STEPS - 1)
+    row_ref[head_rows(step), :] = jnp.concatenate(rows, axis=0)
+    skiprow_ref[head_rows(step), :] = jnp.concatenate(skips, axis=0)
+
+    @pl.when(step == GRID - 1)
     def _():
         acc = acc_s[...].astype(BF16)
         gc_ref[...] = dot(acc, b_ref[...], 1, 0)
         gb_ref[...] = dot(acc, c_ref[...], 0, 0)
 
 
-def inner(offset, g, xt, gt, b, c, cum, skip, earlier=()):
-    wide_t = pl.BlockSpec((WIDE, GROUP), lambda i: (i + offset, 0))
-    wide_n = pl.BlockSpec((GROUP, WIDE), lambda i: (0, i + offset))
-    kept = lambda *shape: pl.BlockSpec(shape, lambda i: (0,) * len(shape))
-    narrow = kept(GROUP, STATE)
+def inner(g, xt, gt, b, c, cum, skip):
+    wide_t = pl.BlockSpec((WIDE, GROUP), lambda i: (i, 0))
+    wide_n = pl.BlockSpec((GROUP, WIDE), lambda i: (0, i))
+    narrow = pl.BlockSpec((GROUP, STATE), lambda i: (0, 0))
+    heads = pl.BlockSpec((HEADS, GROUP), lambda i: (0, 0))
     wide = shape_of((HEADS * SIZE, GROUP), BF16)
-    rows = shape_of((HALF, GROUP))
+    rows = shape_of((HEADS, GROUP))
     return call(
-        functools.partial(inner_kernel, offset),
+        inner_kernel,
         "inner",
         [wide, wide, rows, rows, shape_of((GROUP, STATE)), shape_of((GROUP, STATE))],
-        [wide_t, wide_t, kept(HALF, GROUP), kept(HALF, GROUP), narrow, narrow],
-        grid=(HALF_STEPS,),
+        [wide_t, wide_t, heads, heads, narrow, narrow],
+        grid=(GRID,),
         in_specs=[
-            wide_n, wide_t, wide_t, narrow, narrow, kept(HEADS, GROUP),
+            wide_n, wide_t, wide_t, narrow, narrow, heads,
             pl.BlockSpec(memory_space=pltpu.SMEM),
-        ]
-        + [pl.BlockSpec(memory_space=pltpu.HBM)] * len(earlier),
-        input_output_aliases={7 + i: i for i in range(len(earlier))},
+        ],
         scratch_shapes=[pltpu.VMEM((GROUP, GROUP), F32), pltpu.VMEM((GROUP, GROUP), F32)],
-        cost=cost(4),
-        limit=VMEM_LIMIT if earlier else LARGE_LIMIT,
-    )(g, xt, gt, b, c, cum, skip, *earlier)
+        cost=cost(7),
+        limit=LARGE_LIMIT,
+    )(g, xt, gt, b, c, cum, skip)
 
 
 def halves(own):
@@ -370,8 +386,8 @@
 
 
 def sums_kernel(
-    mine_ref, low_ref, high_ref, xt_ref, gt_ref, b_ref, c_ref, cum_ref, low_row_ref,
-    high_row_ref, own_row_ref, low_skiprow_ref, high_skiprow_ref, dt_ref, alog_ref,
+    mine_ref, low_ref, high_ref, xt_ref, gt_ref, b_ref, c_ref, cum_ref, inner_row_ref,
+    own_row_ref, skiprow_ref, dt_ref, rate_ref,
     gdt_ref, sums_ref,
     row_s,
 ):
@@ -394,13 +410,11 @@
     )
     overlap = jnp.sum(overlap, axis=1, keepdims=True) * jnp.exp(cum_ref[:, GROUP - 1 :])
     final = iota((HEADS, GROUP), 1) == GROUP - 1
-    inner_row = jnp.concatenate([low_row_ref[...], high_row_ref[...]], axis=0)
-    row = inner_row + own_row_ref[...] + row_s[...] + jnp.where(final, overlap, 0.0)
-    gdt = -jnp.exp(column(alog_ref[...])) * dot(row, triangle(), 1, 1, EXACT)
+    row = inner_row_ref[...] + own_row_ref[...] + row_s[...] + jnp.where(final, overlap, 0.0)
+    gdt = -rate_ref[:, :1] * dot(row, triangle(), 1, 1, EXACT)
     gdt_ref[...] = gdt
     alog = jnp.sum(gdt * dt_ref[...], axis=1, keepdims=True)
-    skiprow = jnp.concatenate([low_skiprow_ref[...], high_skiprow_ref[...]], axis=0)
-    skip = jnp.sum(skiprow, axis=1, keepdims=True)
+    skip = jnp.sum(skiprow_ref[...], axis=1, keepdims=True)
     sums = jnp.concatenate(
         [as_row(alog), as_row(skip), jnp.zeros((1, STATE - 2 * HEADS), F32)], axis=1
     )
@@ -415,7 +429,7 @@
 
 def other_kernel(
     low_ref, high_ref, yt_ref, gxt_ref, xt_ref, gt_ref, b_ref, c_ref, cum_ref,
-    gct_ref, gbt_ref, low_gc_ref, high_gc_ref, low_gb_ref, high_gb_ref, y_in, gx_in,
+    gct_ref, gbt_ref, gci_ref, gbi_ref, y_in, gx_in,
     y_hbm, gx_hbm, gc_ref, gb_ref,
     out_s, sems,
 ):
@@ -434,8 +448,8 @@
             yt_ref, gxt_ref, y_hbm, gx_hbm, out_s, sems, gct, gbt,
         )
         copies += made
-    gc_ref[...] = (low_gc_ref[...] + high_gc_ref[...] + gct.T).astype(BF16)
-    gb_ref[...] = (low_gb_ref[...] + high_gb_ref[...] + gbt.T).astype(BF16)
+    gc_ref[...] = (gci_ref[...] + gct.T).astype(BF16)
+    gb_ref[...] = (gbi_ref[...] + gbt.T).astype(BF16)
     for made in copies:
         made.wait()
 
@@ -479,10 +493,12 @@
     wide = shape_of((feat, GROUP), BF16)
     tall = shape_of((GROUP, feat), BF16)
     rows = shape_of((HEADS, GROUP))
-    low, high, keep, gain, xt, gt, cum = call(
+    vector = shape_of((HEADS, STATE))
+    low, high, keep, xt, gt, cum, rate = call(
         states_kernel,
         "states",
-        [half, half, all_heads, shape_of((HEADS, 1, STATE)), wide, wide, rows],
+        [half, half, all_heads, wide, wide, rows, vector],
+        [hbm] * 5 + [vmem] * 2,
         in_specs=[hbm] * 6,
         scratch_shapes=[
             pltpu.VMEM((GRID, GROUP, WIDE), BF16),
@@ -491,23 +507,24 @@
             pltpu.VMEM((GROUP, STATE), BF16),
             pltpu.VMEM((HEADS, GROUP), F32),
             pltpu.VMEM((1, HEADS), F32),
+            pltpu.VMEM((GRID, STEP, SIZE, STATE), F32),
+            pltpu.VMEM((GRID, STEP, SIZE, STATE), F32),
+            pltpu.VMEM((GRID, WIDE, GROUP), BF16),
+            pltpu.VMEM((GRID, WIDE, GROUP), BF16),
             pltpu.SemaphoreType.DMA((4 + 2 * GRID,)),
+            pltpu.SemaphoreType.DMA((4 * GRID,)),
         ],
         limit=LARGE_LIMIT,
     )(x, g, b, c, steps, alog)
     low_in, high_in = swap(low, high)
-    gains = lax.all_to_all(gain, "seq", 0, 0, tiled=True)
-    yt, gxt, low_row, low_skiprow, low_gb, low_gc = inner(0, g, xt, gt, b, c, cum, skip)
+    yt, gxt, row, skiprow, gbi, gci = inner(g, xt, gt, b, c, cum, skip)
     low_in, high_in, yt, gxt = lax.optimization_barrier((low_in, high_in, yt, gxt))
-    joined = call(join_kernel, "join", all_heads)(keep, low_in, high_in, cum)
-    parts = lax.all_to_all(joined, "seq", 0, 0, tiled=True)
-    scanned = call(scan_kernel, "scan", all_heads)(parts, gains)
+    joined = call(join_kernel, "join", shape_of((HEADS * ROWS, STATE)))(keep, low_in, high_in, cum)
+    parts = lax.all_to_all(joined.reshape(HEADS, ROWS, 1, STATE), "seq", 0, 0, tiled=True)
+    scanned = call(scan_kernel, "scan", all_heads)(parts.reshape(HEADS * ROWS, STATE))
     mine = lax.all_to_all(scanned, "seq", 0, 0, tiled=True)
     low_out, high_out = call(pass_on_kernel, "pass_on", [half, half])(mine, low, high, cum)
     low_back, high_back = swap(low_out, high_out)
-    yt, gxt, high_row, high_skiprow, high_gb, high_gc = inner(
-        HALF_STEPS, g, xt, gt, b, c, cum, skip, (yt, gxt)
-    )
     out_scratch = [
         pltpu.VMEM((2 * HALF_STEPS, GROUP, WIDE), BF16),
         pltpu.SemaphoreType.DMA((2 * HALF_STEPS,)),
@@ -528,8 +545,7 @@
         [rows, shape_of((everyone, 1, STATE))],
         scratch_shapes=[pltpu.VMEM((HEADS, GROUP), F32)],
     )(
-        mine, low_back, high_back, xt, gt, b, c, cum, low_row, high_row, own_row,
-        low_skiprow, high_skiprow, steps, alog,
+        mine, low_back, high_back, xt, gt, b, c, cum, row, own_row, skiprow, steps, rate,
     )
     sums = lax.all_to_all(copies, ("dp", "seq"), 0, 0, tiled=True)
     y, gx, gc, gb = call(
@@ -537,14 +553,14 @@
         "other",
         [tall, tall, shape_of((GROUP, STATE), BF16), shape_of((GROUP, STATE), BF16)],
         [hbm, hbm, vmem, vmem],
-        in_specs=[vmem] * 15 + [hbm, hbm],
-        input_output_aliases={15: 0, 16: 1},
+        in_specs=[vmem] * 13 + [hbm, hbm],
+        input_output_aliases={13: 0, 14: 1},
         scratch_shapes=out_scratch,
         cost=cost(4),
         limit=LARGE_LIMIT,
     )(
         low_back, high_back, yt, gxt, xt, gt, b, c, cum, gct, gbt,
-        low_gc, high_gc, low_gb, high_gb, y, gx,
+        gci, gbi, y, gx,
     )
     galog, gskip = call(
         total_kernel, "total", [shape_of((1, HEADS)), shape_of((1, HEADS))]

time: 134 us -> 136 us (1.015)
  waiting for transfers between devices: 13.8 us -> 21.8 us
  starting transfers between devices: 34.3 us -> 26.7 us
  blocking collectives: 59.8 us -> 64.2 us
  local copies, waits for them, and re-layouts: 2.02 us -> 0.07 us
    ppermute x2, waiting for transfers between devices: 4.51 us -> 9.18 us  [swap(): lax.ppermute(high, 'seq', high_pairs)]
    ppermute x2, waiting for transfers between devices: 0.01 us -> 4.49 us  [swap(): lax.ppermute(low, 'seq', low_pairs)]
    all_to_all x1 -> x0, starting transfers between devices: 3.83 us -> none  [shards(): gains = lax.all_to_all(gain, 'seq', 0, 0, tiled=True)]
    all_to_all x1, blocking collectives: 30.9 us -> 33.6 us  [shards(): lax.all_to_all(joined.reshape(HEADS, ROWS, 1, STATE), 'seq', 0, 0, tiled=...]
    unnamed x48 -> x36, local copies, waits for them, and re-layouts: 2.02 us -> 0.07 us
    all_to_all x1, blocking collectives: 28.9 us -> 30.6 us  [shards(): mine = lax.all_to_all(scanned, 'seq', 0, 0, tiled=True)]
    ppermute x2, starting transfers between devices: 10.1 us -> 8.51 us  [swap(): lax.ppermute(high, 'seq', high_pairs)]
    ppermute x2, starting transfers between devices: 6.79 us -> 5.29 us  [swap(): lax.ppermute(low, 'seq', low_pairs)]
  transfers between devices with their start and end apart: 6 -> 5, of which waited for: 4 -> 4; matrix products, arithmetic and copies ran while one was open for 0% -> 0% of each run, Pallas kernels for 11% -> 10%
where the time goes in v5:
time: 136 us; the launch traced here: 135 us
  blocking collectives  64.2 us (47%)
  starting transfers between devices  26.7 us (20%)
  Pallas kernels  21.8 us (16%)
  waiting for transfers between devices  21.8 us (16%)
    all_to_all x1, blocking collectives, shards(): lax.all_to_all(joined.reshape(HEADS, ROWS, 1, STATE), 'seq', 0, 0, tiled=...  33.6 us
    all_to_all x1, blocking collectives, shards(): mine = lax.all_to_all(scanned, 'seq', 0, 0, tiled=True)  30.6 us
    all_to_all x1, starting transfers between devices, shards(): sums = lax.all_to_all(copies, ('dp', 'seq'), 0, 0, tiled=True)  12.9 us
    ppermute x2, waiting for transfers between devices, swap(): lax.ppermute(high, 'seq', high_pairs)  9.18 us
    ppermute x2, starting transfers between devices, swap(): lax.ppermute(high, 'seq', high_pairs)  8.51 us
    all_to_all x1, waiting for transfers between devices, shards(): sums = lax.all_to_all(copies, ('dp', 'seq'), 0, 0, tiled=True)  8.17 us
    pallas_call x1, Pallas kernels, inner(): call(inner_kernel, 'inner', [wide, wide, rows, rows, shape_of((GROUP, STA...  7.19 us
    ppermute x2, starting transfers between devices, swap(): lax.ppermute(low, 'seq', low_pairs)  5.29 us
  transfers between devices with their start and end apart: 5, of which 4 were waited for; matrix products, arithmetic and copies ran while one was open for 0% of the time, Pallas kernels for 10%

profile of v5, /device:TPU:1, one launch (start us, length us, event | category | flops | bytes accessed | tf_op | source)
XLA Modules:
  0.0 135.4 jit_solution(16079429246118938238)
XLA Ops:
  0.6 4.5 %states.1 = (f32[16,64,128]{2,1,0:T(8,128)}, f32[16,64,128]{2,1,0:T(8,128)}, f32[32,64,128]{2,1,0:T(8,128)}, bf16[2048,256]{1,0:T(8,128)(2,1)}, bf16[2048,256]{1...) custom-call(bf16[256,2048]{1,0:T(8,128)(2,1)} %bitcast.31, bf16[256,2048]{1,0:T(8,128)(2,1)} %bitcast.32, ...), custom_call_target="tpu_custom_call" | custom-call | tf_op jit(solution)/shard_map/states/pallas_call | solution.py:497
  5.2 2.6 %collective-permute-start = (f32[16,64,128]{2,1,0:T(8,128)}, f32[16,64,128]{2,1,0:T(8,128)S(1)}, u32[]{:S(2)}, u32[]{:S(2)}) collective-permute-start(f32[16,64,128]{2,1,0:T(8,128)} %get-tuple-element.40.low_ref), channel_id=1, source_target_pairs={{0,1},{1,0},{2,3},{3,2},{4,5},{5,4},{6,7},{7,6},{8,9},{9,8},{10,11... | collective-permute-start | bytes 1572872 | tf_op jit(solution)/shard_map/ppermute | solution.py:482
  7.7 6.9 %collective-permute-start.1 = (f32[16,64,128]{2,1,0:T(8,128)}, f32[16,64,128]{2,1,0:T(8,128)S(1)}, u32[]{:S(2)}, u32[]{:S(2)}) collective-permute-start(f32[16,64,128]{2,1,0:T(8,128)} %get-tuple-element.41.high_ref), channel_id=1, source_target_pairs={{1,2},{2,1},{3,4},{4,3},{5,6},{6,5},{7,8},{8,7},{9,10},{10,9},{11,... | collective-permute-start | bytes 1572872 | tf_op jit(solution)/shard_map/ppermute | solution.py:482
  14.6 7.2 %inner.1 = (bf16[2048,256]{1,0:T(8,128)(2,1)}, bf16[2048,256]{1,0:T(8,128)(2,1)}, f32[32,256]{1,0:T(8,128)}, f32[32,256]{1,0:T(8,128)}, f32[256,128]{1,0:T(8,128)}, /*index=5*/f32[256,128]{1,0:T(8,128)}) custom-call(bf16[256,2048]{1,0:T(8,128)(2,1)} %bitcast.33, bf16[2048,256]{1,0:T(8,128)(2,1)} %get-tuple-element.42.xt_ref, ...), custom_call_target="tpu_custom_call" | custom-call | flops 3500000000 | bytes 14680064 | tf_op jit(solution)/shard_map/inner/pallas_call | solution.py:283
  21.8 0.0 collective-permute-done.low_ref
  21.8 4.3 %collective-permute-done.1.high_ref = f32[16,64,128]{2,1,0:T(8,128)S(1)} collective-permute-done((f32[16,64,128]{2,1,0:T(8,128)}, f32[16,64,128]{2,1,0:T(8,128)S(1)}, u32[]{:S(2)}, u32[]{:S(2)}) %collective-permute-start.1) | collective-permute-done | bytes 524320 | tf_op jit(solution)/shard_map/ppermute | solution.py:482
  26.1 0.0 copy-done.6
  26.1 0.0 copy-done.9
  26.1 0.2 join.1
  26.4 33.6 %all_to_all.15 = f32[32,65,1,128]{3,2,1,0:T(1,128)S(1)} all-to-all(f32[32,65,1,128]{3,2,1,0:T(1,128)S(1)} %bitcast.15), channel_id=1, replica_groups=mesh['dp'=8,'seq'=32] {'seq'}, dimensions={0} | all-to-all | bytes 2129920 | tf_op jit(solution)/shard_map/all_to_all | solution.py:523
  60.0 0.1 scan.1
  60.1 0.0 copy-start.4
  60.1 0.0 copy-start.5
  60.1 30.6 %all_to_all.16.mine_ref = f32[32,64,128]{2,1,0:T(8,128)S(1)} all-to-all(f32[32,64,128]{2,1,0:T(8,128)S(1)} %scan.1), channel_id=1, replica_groups=mesh['dp'=8,'seq'=32] {'seq'}, dimensions={0} | all-to-all | bytes 2097152 | tf_op jit(solution)/shard_map/all_to_all | solution.py:525
  90.7 0.0 copy-done.10
  90.7 0.0 copy-done.11
  90.7 0.2 pass_on.1
  91.0 2.7 %collective-permute-start.2 = (f32[16,64,128]{2,1,0:T(8,128)S(1)}, f32[16,64,128]{2,1,0:T(8,128)S(1)}, u32[]{:S(2)}, u32[]{:S(2)}) collective-permute-start(f32[16,64,128]{2,1,0:T(8,128)S(1)} %get-tuple-element.49), channel_id=1, source_target_pairs={{0,1},{1,0},{2,3},{3,2},{4,5},{5,4},{6,7},{7,6},{8,9},{9,8},{10,11... | collective-permute-start | bytes 1572872 | tf_op jit(solution)/shard_map/ppermute | solution.py:482
  93.7 1.7 %collective-permute-start.3 = (f32[16,64,128]{2,1,0:T(8,128)S(1)}, f32[16,64,128]{2,1,0:T(8,128)S(1)}, u32[]{:S(2)}, u32[]{:S(2)}) collective-permute-start(f32[16,64,128]{2,1,0:T(8,128)S(1)} %get-tuple-element.50), channel_id=1, source_target_pairs={{1,2},{2,1},{3,4},{4,3},{5,6},{6,5},{7,8},{8,7},{9,10},{10,9},{11,... | collective-permute-start | bytes 1572872 | tf_op jit(solution)/shard_map/ppermute | solution.py:482
  95.4 0.0 copy-done.7
  95.4 0.0 copy-done.8
  95.4 1.9 %own.1 = (bf16[256,2048]{1,0:T(8,128)(2,1)}, bf16[256,2048]{1,0:T(8,128)(2,1)}, f32[32,256]{1,0:T(8,128)S(1)}, f32[128,256]{1,0:T(8,128)S(1)}, f32[128,256]{1,0:T(8,128)S(1)}) custom-call(f32[32,64,128]{2,1,0:T(8,128)S(1)} %all_to_all.16.mine_ref, bf16[2048,256]{1,0:T(8,128)(2,1)S(1)} %copy-done.4, bf16[2048,256]{1,0:T(8,128)(2,1)S(1)} %copy-done.5, ...), custom_call_target="tpu_custom_call" | custom-call | flops 2000000000 | bytes 8388608 | tf_op jit(solution)/shard_map/own/pallas_call | solution.py:533
  97.3 4.5 %collective-permute-done.2.low_ref = f32[16,64,128]{2,1,0:T(8,128)S(1)} collective-permute-done((f32[16,64,128]{2,1,0:T(8,128)S(1)}, f32[16,64,128]{2,1,0:T(8,128)S(1)}, u32[]{:S(2)}, u32[]{:S(2)}) %collective-permute-start.2) | collective-permute-done | bytes 524320 | tf_op jit(solution)/shard_map/ppermute | solution.py:482
  101.8 4.8 %collective-permute-done.3.high_ref = f32[16,64,128]{2,1,0:T(8,128)S(1)} collective-permute-done((f32[16,64,128]{2,1,0:T(8,128)S(1)}, f32[16,64,128]{2,1,0:T(8,128)S(1)}, u32[]{:S(2)}, u32[]{:S(2)}) %collective-permute-start.3) | collective-permute-done | bytes 524320 | tf_op jit(solution)/shard_map/ppermute | solution.py:482
  106.6 0.0 copy-done.14
  106.6 0.0 copy-done.16
  106.7 1.9 %sums.1 = (f32[32,256]{1,0:T(8,128)}, f32[256,1,128]{2,1,0:T(1,128)}) custom-call(f32[32,64,128]{2,1,0:T(8,128)S(1)} %all_to_all.16.mine_ref, f32[16,64,128]{2,1,0:T(8,128)S(1)} %collective-permute-done.2.low_ref, f32[16,64,128]{2,1,0:T(8,128)S(1)} %collective-permute-done.3.high_ref, bf16[2048,256]{1,0:T(8,128)(2,1)S(1)} %copy-done, ...), custom_call_target="tpu_custom_call" | custom-call | tf_op jit(solution)/shard_map/sums/pallas_call | solution.py:542
  108.6 0.0 copy-done.13
  108.6 12.9 %all-to-all-start.2 = ((f32[256,1,128]{2,1,0:T(1,128)}), f32[256,1,128]{2,1,0:T(1,128)S(1)}, u32[]{:S(2)}, u32[]{:S(2)}) async-start(f32[256,1,128]{2,1,0:T(1,128)} %get-tuple-element.68), calls=%async_computation.2 | async-start | bytes 262144 | tf_op jit(solution)/shard_map/all_to_all | solution.py:550
  121.5 4.9 %other.1 = (bf16[256,2048]{1,0:T(8,128)(2,1)}, bf16[256,2048]{1,0:T(8,128)(2,1)}, bf16[256,128]{1,0:T(8,128)(2,1)}, bf16[256,128]{1,0:T(8,128)(2,1)}) custom-call(f32[16,64,128]{2,1,0:T(8,128)} %copy-done.2, f32[16,64,128]{2,1,0:T(8,128)} %copy-done.3, bf16[2048,256]{1,0:T(8,128)(2,1)} %get-tuple-element.51.yt_ref, ...), custom_call_target="tpu_custom_call", output_to_operand_aliasing={{0}: (13, {}), {1}: (14, {})} | custom-call | flops 2000000000 | bytes 8388608 | tf_op jit(solution)/shard_map/other/pallas_call | solution.py:551
  126.3 8.2 %all-to-all-done.2.sums_ref = f32[256,1,128]{2,1,0:T(1,128)S(1)} async-done(((f32[256,1,128]{2,1,0:T(1,128)}), f32[256,1,128]{2,1,0:T(1,128)S(1)}, u32[]{:S(2)}, u32[]{:S(2)}) %all-to-all-start.2) | async-done | bytes 131104 | tf_op jit(solution)/shard_map/all_to_all | solution.py:550
  134.5 0.8 total.1
  (25 shorter events, 0.0 us)
Async XLA Ops:
  5.2 16.6 %collective-permute-start = (f32[16,64,128]{2,1,0:T(8,128)}, f32[16,64,128]{2,1,0:T(8,128)S(1)}, u32[]{:S(2)}, u32[]{:S(2)}) collective-permute-start(f32[16,64,128]{2,1,0:T(8,128)} %get-tuple-element.40.low_ref), channel_id=1, source_target_pairs={{0,1},{1,0},{2,3},{3,2},{4,5},{5,4},{6,7},{7,6},{8,9},{9,8},{10,11... | collective-permute-start | bytes 1572872 | tf_op jit(solution)/shard_map/ppermute | solution.py:482
  7.7 18.4 %collective-permute-start.1 = (f32[16,64,128]{2,1,0:T(8,128)}, f32[16,64,128]{2,1,0:T(8,128)S(1)}, u32[]{:S(2)}, u32[]{:S(2)}) collective-permute-start(f32[16,64,128]{2,1,0:T(8,128)} %get-tuple-element.41.high_ref), channel_id=1, source_target_pairs={{1,2},{2,1},{3,4},{4,3},{5,6},{6,5},{7,8},{8,7},{9,10},{10,9},{11,... | collective-permute-start | bytes 1572872 | tf_op jit(solution)/shard_map/ppermute | solution.py:482
  14.6 11.5 %copy-start.6 = (f32[32,64,128]{2,1,0:T(8,128)S(1)}, f32[32,64,128]{2,1,0:T(8,128)}, u32[]{:S(2)}) copy-start(f32[32,64,128]{2,1,0:T(8,128)} %get-tuple-element.39.keep_ref) | copy-start | bytes 3145732
  14.6 11.5 %copy-start.9 = (f32[32,256]{1,0:T(8,128)S(1)}, f32[32,256]{1,0:T(8,128)}, u32[]{:S(2)}) copy-start(f32[32,256]{1,0:T(8,128)} %get-tuple-element.44.cum_ref) | copy-start | bytes 98308
  60.0 30.8 %copy-start.10 = (f32[16,64,128]{2,1,0:T(8,128)S(1)}, f32[16,64,128]{2,1,0:T(8,128)}, u32[]{:S(2)}) copy-start(f32[16,64,128]{2,1,0:T(8,128)} %get-tuple-element.40.low_ref) | copy-start | bytes 1572868
  60.0 30.8 %copy-start.11 = (f32[16,64,128]{2,1,0:T(8,128)S(1)}, f32[16,64,128]{2,1,0:T(8,128)}, u32[]{:S(2)}) copy-start(f32[16,64,128]{2,1,0:T(8,128)} %get-tuple-element.41.high_ref) | copy-start | bytes 1572868
  60.0 35.4 %copy-start.7 = (bf16[1,256,128]{2,1,0:T(8,128)(2,1)S(1)}, bf16[1,256,128]{2,1,0:T(8,128)(2,1)}, u32[]{:S(2)}) copy-start(bf16[1,256,128]{2,1,0:T(8,128)(2,1)} %param.8) | copy-start | bytes 196612
  60.0 35.4 %copy-start.8 = (bf16[1,256,128]{2,1,0:T(8,128)(2,1)S(1)}, bf16[1,256,128]{2,1,0:T(8,128)(2,1)}, u32[]{:S(2)}) copy-start(bf16[1,256,128]{2,1,0:T(8,128)(2,1)} %param.9) | copy-start | bytes 196612
  60.1 35.3 %copy-start.4 = (bf16[2048,256]{1,0:T(8,128)(2,1)S(1)}, bf16[2048,256]{1,0:T(8,128)(2,1)}, u32[]{:S(2)}) copy-start(bf16[2048,256]{1,0:T(8,128)(2,1)} %get-tuple-element.51.yt_ref) | copy-start | bytes 3145732
  60.1 35.3 %copy-start.5 = (bf16[2048,256]{1,0:T(8,128)(2,1)S(1)}, bf16[2048,256]{1,0:T(8,128)(2,1)}, u32[]{:S(2)}) copy-start(bf16[2048,256]{1,0:T(8,128)(2,1)} %get-tuple-element.52.gxt_ref) | copy-start | bytes 3145732
  90.7 4.7 %copy-start = (bf16[2048,256]{1,0:T(8,128)(2,1)S(1)}, bf16[2048,256]{1,0:T(8,128)(2,1)}, u32[]{:S(2)}) copy-start(bf16[2048,256]{1,0:T(8,128)(2,1)} %get-tuple-element.42.xt_ref) | copy-start | bytes 3145732
  90.7 4.7 %copy-start.1 = (bf16[2048,256]{1,0:T(8,128)(2,1)S(1)}, bf16[2048,256]{1,0:T(8,128)(2,1)}, u32[]{:S(2)}) copy-start(bf16[2048,256]{1,0:T(8,128)(2,1)} %get-tuple-element.43.gt_ref) | copy-start | bytes 3145732
  91.0 10.8 %collective-permute-start.2 = (f32[16,64,128]{2,1,0:T(8,128)S(1)}, f32[16,64,128]{2,1,0:T(8,128)S(1)}, u32[]{:S(2)}, u32[]{:S(2)}) collective-permute-start(f32[16,64,128]{2,1,0:T(8,128)S(1)} %get-tuple-element.49), channel_id=1, source_target_pairs={{0,1},{1,0},{2,3},{3,2},{4,5},{5,4},{6,7},{7,6},{8,9},{9,8},{10,11... | collective-permute-start | bytes 1572872 | tf_op jit(solution)/shard_map/ppermute | solution.py:482
  93.7 12.9 %copy-start.14 = (f32[1,32,256]{2,1,0:T(8,128)S(1)}, f32[1,32,256]{2,1,0:T(8,128)}, u32[]{:S(2)}) copy-start(f32[1,32,256]{2,1,0:T(8,128)} %param.10) | copy-start | bytes 98308
  93.7 12.9 %copy-start.15 = (f32[32,256]{1,0:T(8,128)S(1)}, f32[32,256]{1,0:T(8,128)}, u32[]{:S(2)}) copy-start(f32[32,256]{1,0:T(8,128)} %get-tuple-element.63.inner_row_ref) | copy-start | bytes 98308
  93.7 12.9 %copy-start.16 = (f32[32,256]{1,0:T(8,128)S(1)}, f32[32,256]{1,0:T(8,128)}, u32[]{:S(2)}) copy-start(f32[32,256]{1,0:T(8,128)} %get-tuple-element.65.skiprow_ref) | copy-start | bytes 98308
  93.7 12.9 %copy-start.17 = (f32[32,128]{1,0:T(8,128)S(1)}, f32[32,128]{1,0:T(8,128)}, u32[]{:S(2)}) copy-start(f32[32,128]{1,0:T(8,128)} %get-tuple-element.66.rate_ref) | copy-start | bytes 49156
  93.7 12.9 %collective-permute-start.3 = (f32[16,64,128]{2,1,0:T(8,128)S(1)}, f32[16,64,128]{2,1,0:T(8,128)S(1)}, u32[]{:S(2)}, u32[]{:S(2)}) collective-permute-start(f32[16,64,128]{2,1,0:T(8,128)S(1)} %get-tuple-element.50), channel_id=1, source_target_pairs={{1,2},{2,1},{3,4},{4,3},{5,6},{6,5},{7,8},{8,7},{9,10},{10,9},{11,... | collective-permute-start | bytes 1572872 | tf_op jit(solution)/shard_map/ppermute | solution.py:482
  97.3 11.3 %copy-start.12 = (f32[128,256]{1,0:T(8,128)}, f32[128,256]{1,0:T(8,128)S(1)}, u32[]{:S(2)}) copy-start(f32[128,256]{1,0:T(8,128)S(1)} %get-tuple-element.53.gct_ref) | copy-start | bytes 393220
  97.3 11.3 %copy-start.13 = (f32[128,256]{1,0:T(8,128)}, f32[128,256]{1,0:T(8,128)S(1)}, u32[]{:S(2)}) copy-start(f32[128,256]{1,0:T(8,128)S(1)} %get-tuple-element.54.gbt_ref) | copy-start | bytes 393220
  101.8 6.8 %copy-start.2 = (f32[16,64,128]{2,1,0:T(8,128)}, f32[16,64,128]{2,1,0:T(8,128)S(1)}, u32[]{:S(2)}) copy-start(f32[16,64,128]{2,1,0:T(8,128)S(1)} %collective-permute-done.2.low_ref) | copy-start | bytes 1572868
  106.6 1.9 %copy-start.3 = (f32[16,64,128]{2,1,0:T(8,128)}, f32[16,64,128]{2,1,0:T(8,128)S(1)}, u32[]{:S(2)}) copy-start(f32[16,64,128]{2,1,0:T(8,128)S(1)} %collective-permute-done.3.high_ref) | copy-start | bytes 1572868
  108.6 25.9 %all-to-all-start.2 = ((f32[256,1,128]{2,1,0:T(1,128)}), f32[256,1,128]{2,1,0:T(1,128)S(1)}, u32[]{:S(2)}, u32[]{:S(2)}) async-start(f32[256,1,128]{2,1,0:T(1,128)} %get-tuple-element.68), calls=%async_computation.2 | async-start | bytes 262144 | tf_op jit(solution)/shard_map/all_to_all | solution.py:550

commit v6 on v5

--- a/solution.py
+++ b/solution.py
@@ -81,29 +81,57 @@
     return jnp.where(edge & (step >= HALF_STEPS), 0.0, 1.0).astype(F32)
 
 
-def states_kernel(
+def start_copy(source, target, sem):
+    made = pltpu.make_async_copy(source, target, sem)
+    made.start()
+    return made
+
+
+def start_either(first, one, other, sem):
+    @pl.when(first)
+    def _():
+        start_copy(*one, sem)
+
+    @pl.when(jnp.logical_not(first))
+    def _():
+        start_copy(*other, sem)
+
+    return pltpu.make_async_copy(*one, sem)
+
+
+def fetch_chunks(x_hbm, g_hbm, in_s, sems, sending):
+    chunks = []
+    for i in range(GRID):
+        is_state = keeps_adjoint(i) == sending
+        lanes = pl.ds(i * WIDE, WIDE)
+        target = in_s.at[i]
+        made = start_either(
+            is_state, (x_hbm.at[:, lanes], target), (g_hbm.at[:, lanes], target), sems.at[i]
+        )
+        chunks.append((is_state, made))
+    return chunks
+
+
+def chunk_matrix(i, is_state, cum_all, in_s, t_s, b_ref, c_ref):
+    cum = cum_all[i * STEP : (i + 1) * STEP]
+    weights = jnp.exp(jnp.where(is_state, cum[:, GROUP - 1 :] - cum, cum))
+    turned = in_s[i].T
+    t_s[i] = turned
+    scaled = (turned.astype(F32) * spread(weights)).astype(BF16)
+    matrix = dot(scaled, jnp.where(is_state, b_ref[...], c_ref[...]), 1, 0)
+    return matrix.reshape(STEP, SIZE, STATE)
+
+
+def send_kernel(
     x_hbm, g_hbm, b_hbm, c_hbm, dt_hbm, alog_hbm,
-    low_hbm, high_hbm, keep_hbm, xt_hbm, gt_hbm, cum_ref, rate_ref,
-    x_s, g_s, b_s, c_s, dt_s, alog_s, send_s, keep_s, xt_s, gt_s, sems, out_sems,
+    low_hbm, high_hbm, xt_hbm, gt_hbm, cum_ref, rate_ref,
+    in_s, b_s, c_s, dt_s, alog_s, send_s, t_s, sems, out_sems,
 ):
-    def copy(source, target, sem):
-        made = pltpu.make_async_copy(source, target, sem)
-        made.start()
-        return made
-
-    alog_copy = copy(alog_hbm, alog_s, sems.at[0])
-    dt_copy = copy(dt_hbm, dt_s, sems.at[1])
-    b_copy = copy(b_hbm, b_s, sems.at[2])
-    c_copy = copy(c_hbm, c_s, sems.at[3])
-    inputs = []
-    for i in range(GRID):
-        lanes = pl.ds(i * WIDE, WIDE)
-        inputs.append(
-            (
-                copy(x_hbm.at[:, lanes], x_s.at[i], sems.at[4 + 2 * i]),
-                copy(g_hbm.at[:, lanes], g_s.at[i], sems.at[5 + 2 * i]),
-            )
-        )
+    alog_copy = start_copy(alog_hbm, alog_s, sems.at[GRID])
+    dt_copy = start_copy(dt_hbm, dt_s, sems.at[GRID + 1])
+    b_copy = start_copy(b_hbm, b_s, sems.at[GRID + 2])
+    c_copy = start_copy(c_hbm, c_s, sems.at[GRID + 3])
+    chunks = fetch_chunks(x_hbm, g_hbm, in_s, sems, True)
     alog_copy.wait()
     dt_copy.wait()
     rate = jnp.exp(column(alog_s[...]))
@@ -113,36 +141,46 @@
     b_copy.wait()
     c_copy.wait()
     outputs = []
-    for i in range(GRID):
-        for made in inputs[i]:
-            made.wait()
-        cum = cum_all[i * STEP : (i + 1) * STEP]
-        to_end = jnp.exp(cum[:, GROUP - 1 :] - cum)
-        from_start = jnp.exp(cum)
-        xt = x_s[i].T
-        gt = g_s[i].T
-        xt_s[i] = xt
-        gt_s[i] = gt
-        scaled = (xt.astype(F32) * spread(to_end)).astype(BF16)
-        raised = (gt.astype(F32) * spread(from_start)).astype(BF16)
-        state = dot(scaled, b_s[...], 1, 0)
-        adjoint = dot(raised, c_s[...], 1, 0)
-        first = keeps_adjoint(i)
-        send = jnp.where(first, state, adjoint) * unpaired(i)
-        keep = jnp.where(first, adjoint, state)
-        send_s[i] = send.reshape(STEP, SIZE, STATE)
-        keep_s[i] = keep.reshape(STEP, SIZE, STATE)
+    for i, (is_state, made) in enumerate(chunks):
+        made.wait()
+        send_s[i] = chunk_matrix(i, is_state, cum_all, in_s, t_s, b_s, c_s) * unpaired(i)
         send_hbm = low_hbm if i < HALF_STEPS else high_hbm
         rows = pl.ds(i * WIDE, WIDE)
-        for k, (source, target) in enumerate(
-            (
-                (send_s, send_hbm.at[pl.ds(i % HALF_STEPS * STEP, STEP)]),
-                (keep_s, keep_hbm.at[pl.ds(i * STEP, STEP)]),
-                (xt_s, xt_hbm.at[rows]),
-                (gt_s, gt_hbm.at[rows]),
+        outputs.append(
+            start_copy(
+                send_s.at[i], send_hbm.at[pl.ds(i % HALF_STEPS * STEP, STEP)], out_sems.at[2 * i]
             )
-        ):
-            outputs.append(copy(source.at[i], target, out_sems.at[4 * i + k]))
+        )
+        outputs.append(
+            start_either(
+                is_state, (t_s.at[i], xt_hbm.at[rows]), (t_s.at[i], gt_hbm.at[rows]),
+                out_sems.at[2 * i + 1],
+            )
+        )
+    for made in outputs:
+        made.wait()
+
+
+def keep_kernel(
+    x_hbm, g_hbm, b_ref, c_ref, cum_ref, xt_in, gt_in,
+    keep_hbm, xt_hbm, gt_hbm,
+    in_s, keep_s, t_s, sems, out_sems,
+):
+    cum_all = cum_ref[...]
+    outputs = []
+    for i, (is_state, made) in enumerate(fetch_chunks(x_hbm, g_hbm, in_s, sems, False)):
+        made.wait()
+        keep_s[i] = chunk_matrix(i, is_state, cum_all, in_s, t_s, b_ref, c_ref)
+        rows = pl.ds(i * WIDE, WIDE)
+        outputs.append(
+            start_copy(keep_s.at[i], keep_hbm.at[pl.ds(i * STEP, STEP)], out_sems.at[2 * i])
+        )
+        outputs.append(
+            start_either(
+                is_state, (t_s.at[i], xt_hbm.at[rows]), (t_s.at[i], gt_hbm.at[rows]),
+                out_sems.at[2 * i + 1],
+            )
+        )
     for made in outputs:
         made.wait()
 
@@ -357,9 +395,27 @@
     return gct, gbt, copies
 
 
+def partner_weights(mine_ref, xt_ref, gt_ref, b_ref, c_ref, cum_ref, out_ref):
+    _, state_first, adjoint_first = halves(False)
+    for i in range(HALF_STEPS):
+        for step, data_ref, rhs_ref, is_state in (
+            (state_first + i, gt_ref, c_ref, True),
+            (adjoint_first + i, xt_ref, b_ref, False),
+        ):
+            cum = cum_ref[head_rows(step), :]
+            last = cum[:, GROUP - 1 :]
+            lag = cum if is_state else last - cum
+            data = data_ref[feature_rows(step), :].astype(F32) * spread(lag * jnp.exp(lag))
+            made = dot(data.astype(BF16), rhs_ref[...], 1, 0).reshape(STEP, SIZE, STATE)
+            gain = last * jnp.exp(last)
+            here = pl.multiple_of(step * STEP, STEP)
+            for j in range(STEP):
+                out_ref[here + j] = made[j] + gain[j : j + 1] * mine_ref[here + j]
+
+
 def own_kernel(
-    mine_ref, yt_ref, gxt_ref, xt_ref, gt_ref, b_ref, c_ref, cum_ref,
-    y_hbm, gx_hbm, row_ref, gct_ref, gbt_ref,
+    mine_ref, yt_ref, gxt_ref, xt_ref, gt_ref, b_ref, c_ref, cum_ref, inner_row_ref, skiprow_ref,
+    y_hbm, gx_hbm, row_ref, gct_ref, gbt_ref, weights_ref, base_ref,
     out_s, sems,
 ):
     _, state_first, adjoint_first = halves(True)
@@ -381,40 +437,26 @@
         copies += made
     gct_ref[...] = gct
     gbt_ref[...] = gbt
+    partner_weights(mine_ref, xt_ref, gt_ref, b_ref, c_ref, cum_ref, weights_ref)
+    alog = (inner_row_ref[...] + row_ref[...]) * cum_ref[...]
+    alog = jnp.sum(alog, axis=1, keepdims=True)
+    skip = jnp.sum(skiprow_ref[...], axis=1, keepdims=True)
+    lane = iota((HEADS, STATE), 1)
+    base_ref[...] = jnp.where(lane == 0, alog, jnp.where(lane == 1, skip, 0.0))
     for made in copies:
         made.wait()
 
 
-def sums_kernel(
-    mine_ref, low_ref, high_ref, xt_ref, gt_ref, b_ref, c_ref, cum_ref, inner_row_ref,
-    own_row_ref, skiprow_ref, dt_ref, rate_ref,
-    gdt_ref, sums_ref,
-    row_s,
-):
-    state_low, state_first, adjoint_first = halves(False)
-    for i in range(HALF_STEPS):
-        state = take_half(low_ref, high_ref, state_low, i)
-        adjoint = take_half(high_ref, low_ref, state_low, i)
-        row_s[head_rows(state_first + i), :] = carried_rows(
-            state, gt_ref, c_ref, cum_ref, state_first + i
-        )[-1]
-        row_s[head_rows(adjoint_first + i), :] = scaled_rows(
-            adjoint, xt_ref, b_ref, cum_ref, adjoint_first + i
-        )[-1]
-    overlap = jnp.concatenate(
+def sums_kernel(weights_ref, low_ref, high_ref, base_ref, sums_ref):
+    product = jnp.concatenate(
         [
-            jnp.sum(mine_ref[:HALF] * low_ref[...], axis=1),
-            jnp.sum(mine_ref[HALF:] * high_ref[...], axis=1),
+            jnp.sum(weights_ref[:HALF] * low_ref[...], axis=1),
+            jnp.sum(weights_ref[HALF:] * high_ref[...], axis=1),
         ],
         axis=0,
     )
-    overlap = jnp.sum(overlap, axis=1, keepdims=True) * jnp.exp(cum_ref[:, GROUP - 1 :])
-    final = iota((HEADS, GROUP), 1) == GROUP - 1
-    row = inner_row_ref[...] + own_row_ref[...] + row_s[...] + jnp.where(final, overlap, 0.0)
-    gdt = -rate_ref[:, :1] * dot(row, triangle(), 1, 1, EXACT)
-    gdt_ref[...] = gdt
-    alog = jnp.sum(gdt * dt_ref[...], axis=1, keepdims=True)
-    skip = jnp.sum(skiprow_ref[...], axis=1, keepdims=True)
+    alog = base_ref[:, :1] + jnp.sum(product, axis=1, keepdims=True)
+    skip = base_ref[:, 1:2]
     sums = jnp.concatenate(
         [as_row(alog), as_row(skip), jnp.zeros((1, STATE - 2 * HEADS), F32)], axis=1
     )
@@ -429,9 +471,9 @@
 
 def other_kernel(
     low_ref, high_ref, yt_ref, gxt_ref, xt_ref, gt_ref, b_ref, c_ref, cum_ref,
-    gct_ref, gbt_ref, gci_ref, gbi_ref, y_in, gx_in,
-    y_hbm, gx_hbm, gc_ref, gb_ref,
-    out_s, sems,
+    gct_ref, gbt_ref, gci_ref, gbi_ref, mine_ref, inner_row_ref, own_row_ref, rate_ref, y_in, gx_in,
+    y_hbm, gx_hbm, gc_ref, gb_ref, gdt_ref,
+    out_s, row_s, sems,
 ):
     state_low, state_first, adjoint_first = halves(False)
     gct = gct_ref[...]
@@ -441,8 +483,10 @@
         state_step, adjoint_step = state_first + i, adjoint_first + i
         state = take_half(low_ref, high_ref, state_low, i)
         adjoint = take_half(high_ref, low_ref, state_low, i)
-        raw, gf, from_start, _ = carried_rows(state, gt_ref, c_ref, cum_ref, state_step)
-        back, xf, to_end, _ = scaled_rows(adjoint, xt_ref, b_ref, cum_ref, adjoint_step)
+        raw, gf, from_start, row = carried_rows(state, gt_ref, c_ref, cum_ref, state_step)
+        row_s[head_rows(state_step), :] = row
+        back, xf, to_end, row = scaled_rows(adjoint, xt_ref, b_ref, cum_ref, adjoint_step)
+        row_s[head_rows(adjoint_step), :] = row
         gct, gbt, made = give_out(
             i, state_step, adjoint_step, state, adjoint, (raw, gf, from_start, back, xf, to_end),
             yt_ref, gxt_ref, y_hbm, gx_hbm, out_s, sems, gct, gbt,
@@ -450,6 +494,17 @@
         copies += made
     gc_ref[...] = (gci_ref[...] + gct.T).astype(BF16)
     gb_ref[...] = (gbi_ref[...] + gbt.T).astype(BF16)
+    overlap = jnp.concatenate(
+        [
+            jnp.sum(mine_ref[:HALF] * low_ref[...], axis=1),
+            jnp.sum(mine_ref[HALF:] * high_ref[...], axis=1),
+        ],
+        axis=0,
+    )
+    overlap = jnp.sum(overlap, axis=1, keepdims=True) * jnp.exp(cum_ref[:, GROUP - 1 :])
+    final = iota((HEADS, GROUP), 1) == GROUP - 1
+    row = inner_row_ref[...] + own_row_ref[...] + row_s[...] + jnp.where(final, overlap, 0.0)
+    gdt_ref[...] = -rate_ref[:, :1] * dot(row, triangle(), 1, 1, EXACT)
     for made in copies:
         made.wait()
 
@@ -494,29 +549,46 @@
     tall = shape_of((GROUP, feat), BF16)
     rows = shape_of((HEADS, GROUP))
     vector = shape_of((HEADS, STATE))
-    low, high, keep, xt, gt, cum, rate = call(
-        states_kernel,
-        "states",
-        [half, half, all_heads, wide, wide, rows, vector],
-        [hbm] * 5 + [vmem] * 2,
+    chunk = pltpu.VMEM((GRID, GROUP, WIDE), BF16)
+    turned = pltpu.VMEM((GRID, WIDE, GROUP), BF16)
+    matrices = pltpu.VMEM((GRID, STEP, SIZE, STATE), F32)
+    low, high, xt, gt, cum, rate = call(
+        send_kernel,
+        "send",
+        [half, half, wide, wide, rows, vector],
+        [hbm] * 4 + [vmem] * 2,
         in_specs=[hbm] * 6,
         scratch_shapes=[
-            pltpu.VMEM((GRID, GROUP, WIDE), BF16),
-            pltpu.VMEM((GRID, GROUP, WIDE), BF16),
+            chunk,
             pltpu.VMEM((GROUP, STATE), BF16),
             pltpu.VMEM((GROUP, STATE), BF16),
             pltpu.VMEM((HEADS, GROUP), F32),
             pltpu.VMEM((1, HEADS), F32),
-            pltpu.VMEM((GRID, STEP, SIZE, STATE), F32),
-            pltpu.VMEM((GRID, STEP, SIZE, STATE), F32),
-            pltpu.VMEM((GRID, WIDE, GROUP), BF16),
-            pltpu.VMEM((GRID, WIDE, GROUP), BF16),
-            pltpu.SemaphoreType.DMA((4 + 2 * GRID,)),
-            pltpu.SemaphoreType.DMA((4 * GRID,)),
+            matrices,
+            turned,
+            pltpu.SemaphoreType.DMA((GRID + 4,)),
+            pltpu.SemaphoreType.DMA((2 * GRID,)),
         ],
         limit=LARGE_LIMIT,
     )(x, g, b, c, steps, alog)
     low_in, high_in = swap(low, high)
+    keep, xt, gt = call(
+        keep_kernel,
+        "keep",
+        [all_heads, wide, wide],
+        [hbm] * 3,
+        in_specs=[hbm, hbm, vmem, vmem, vmem, hbm, hbm],
+        input_output_aliases={5: 1, 6: 2},
+        scratch_shapes=[
+            chunk,
+            matrices,
+            turned,
+            pltpu.SemaphoreType.DMA((GRID,)),
+            pltpu.SemaphoreType.DMA((2 * GRID,)),
+        ],
+        cost=cost(3),
+        limit=LARGE_LIMIT,
+    )(x, g, b, c, cum, xt, gt)
     yt, gxt, row, skiprow, gbi, gci = inner(g, xt, gt, b, c, cum, skip)
     low_in, high_in, yt, gxt = lax.optimization_barrier((low_in, high_in, yt, gxt))
     joined = call(join_kernel, "join", shape_of((HEADS * ROWS, STATE)))(keep, low_in, high_in, cum)
@@ -525,42 +597,38 @@
     mine = lax.all_to_all(scanned, "seq", 0, 0, tiled=True)
     low_out, high_out = call(pass_on_kernel, "pass_on", [half, half])(mine, low, high, cum)
     low_back, high_back = swap(low_out, high_out)
-    out_scratch = [
-        pltpu.VMEM((2 * HALF_STEPS, GROUP, WIDE), BF16),
-        pltpu.SemaphoreType.DMA((2 * HALF_STEPS,)),
-    ]
+    out_scratch = pltpu.VMEM((2 * HALF_STEPS, GROUP, WIDE), BF16)
     part = shape_of((STATE, GROUP))
-    y, gx, own_row, gct, gbt = call(
+    y, gx, own_row, gct, gbt, weights, base = call(
         own_kernel,
         "own",
-        [tall, tall, rows, part, part],
-        [hbm, hbm, vmem, vmem, vmem],
-        scratch_shapes=out_scratch,
+        [tall, tall, rows, part, part, all_heads, vector],
+        [hbm, hbm] + [vmem] * 5,
+        scratch_shapes=[out_scratch, pltpu.SemaphoreType.DMA((2 * HALF_STEPS,))],
         cost=cost(4),
-    )(mine, yt, gxt, xt, gt, b, c, cum)
+    )(mine, yt, gxt, xt, gt, b, c, cum, row, skiprow)
     everyone = lax.axis_size("dp") * lax.axis_size("seq")
-    gdt, copies = call(
-        sums_kernel,
-        "sums",
-        [rows, shape_of((everyone, 1, STATE))],
-        scratch_shapes=[pltpu.VMEM((HEADS, GROUP), F32)],
-    )(
-        mine, low_back, high_back, xt, gt, b, c, cum, row, own_row, skiprow, steps, rate,
+    copies = call(sums_kernel, "sums", shape_of((everyone, 1, STATE)))(
+        weights, low_back, high_back, base
     )
     sums = lax.all_to_all(copies, ("dp", "seq"), 0, 0, tiled=True)
-    y, gx, gc, gb = call(
+    y, gx, gc, gb, gdt = call(
         other_kernel,
         "other",
-        [tall, tall, shape_of((GROUP, STATE), BF16), shape_of((GROUP, STATE), BF16)],
-        [hbm, hbm, vmem, vmem],
-        in_specs=[vmem] * 13 + [hbm, hbm],
-        input_output_aliases={13: 0, 14: 1},
-        scratch_shapes=out_scratch,
+        [tall, tall, shape_of((GROUP, STATE), BF16), shape_of((GROUP, STATE), BF16), rows],
+        [hbm, hbm, vmem, vmem, vmem],
+        in_specs=[vmem] * 17 + [hbm, hbm],
+        input_output_aliases={17: 0, 18: 1},
+        scratch_shapes=[
+            out_scratch,
+            pltpu.VMEM((HEADS, GROUP), F32),
+            pltpu.SemaphoreType.DMA((2 * HALF_STEPS,)),
+        ],
         cost=cost(4),
         limit=LARGE_LIMIT,
     )(
         low_back, high_back, yt, gxt, xt, gt, b, c, cum, gct, gbt,
-        gci, gbi, y, gx,
+        gci, gbi, mine, row, own_row, rate, y, gx,
     )
     galog, gskip = call(
         total_kernel, "total", [shape_of((1, HEADS)), shape_of((1, HEADS))]

time: 136 us -> 134 us (0.985)
  waiting for transfers between devices: 21.8 us -> 14.6 us
  Pallas kernels: 21.8 us -> 25.6 us
  local copies, waits for them, and re-layouts: 0.07 us -> 1.98 us
    ppermute x2, waiting for transfers between devices: 9.18 us -> 5 us  [swap(): lax.ppermute(high, 'seq', high_pairs)]
    pallas_call x3 -> x4, Pallas kernels: 8.31 us -> 11.2 us  [the longest x1 4.05 us: shards(): call(keep_kernel, 'keep', [all_heads, wide, wide], [hbm] * 3, in_specs=[h...]
    ppermute x2, waiting for transfers between devices: 4.49 us -> 2.36 us  [swap(): lax.ppermute(low, 'seq', low_pairs)]
    unnamed x36, local copies, waits for them, and re-layouts: 0.07 us -> 1.98 us
  transfers between devices with their start and end apart: 5 -> 5, of which waited for: 4 -> 4; matrix products, arithmetic and copies ran while one was open for 0% -> 0% of each run, Pallas kernels for 10% -> 14%
where the time goes in v6:
time: 134 us
  blocking collectives  64.2 us (48%)
  starting transfers between devices  26.6 us (20%)
  Pallas kernels  25.6 us (19%)
  waiting for transfers between devices  14.6 us (11%)
  local copies, waits for them, and re-layouts  1.98 us (1%)
    all_to_all x1, blocking collectives, shards(): lax.all_to_all(joined.reshape(HEADS, ROWS, 1, STATE), 'seq', 0, 0, tiled=...  33.6 us
    all_to_all x1, blocking collectives, shards(): mine = lax.all_to_all(scanned, 'seq', 0, 0, tiled=True)  30.6 us
    all_to_all x1, starting transfers between devices, shards(): sums = lax.all_to_all(copies, ('dp', 'seq'), 0, 0, tiled=True)  12.9 us
    ppermute x2, starting transfers between devices, swap(): lax.ppermute(high, 'seq', high_pairs)  8.45 us
    all_to_all x1, waiting for transfers between devices, shards(): sums = lax.all_to_all(copies, ('dp', 'seq'), 0, 0, tiled=True)  7.27 us
    pallas_call x1, Pallas kernels, inner(): call(inner_kernel, 'inner', [wide, wide, rows, rows, shape_of((GROUP, STA...  7.19 us
    pallas_call x1, Pallas kernels, shards(): call(other_kernel, 'other', [tall, tall, shape_of((GROUP, STATE), BF16),...  5.75 us
    ppermute x2, starting transfers between devices, swap(): lax.ppermute(low, 'seq', low_pairs)  5.28 us
  transfers between devices with their start and end apart: 5, of which 4 were waited for; matrix products, arithmetic and copies ran while one was open for 0% of the time, Pallas kernels for 14%

profile of v6, /device:TPU:1, one launch (start us, length us, event | category | flops | bytes accessed | tf_op | source)
XLA Modules:
  0.0 133.8 jit_solution(17149999640241794500)
XLA Ops:
  0.6 4.0 %send.1 = (f32[16,64,128]{2,1,0:T(8,128)}, f32[16,64,128]{2,1,0:T(8,128)}, bf16[2048,256]{1,0:T(8,128)(2,1)}, bf16[2048,256]{1,0:T(8,128)(2,1)}, f32[32,256]{1,0:T(8,128)}, /*index=5*/f32[32,128]{1,0:T(8,128)}) custom-call(bf16[256,2048]{1,0:T(8,128)(2,1)} %bitcast.29, bf16[256,2048]{1,0:T(8,128)(2,1)} %bitcast.31, bf16[256,128]{1,0:T(8,128)(2,1)} %bitcast.17, ...), custom_call_target="tpu_custom_call" | custom-call | tf_op jit(solution)/shard_map/send/pallas_call | solution.py:555
  4.7 2.5 %collective-permute-start = (f32[16,64,128]{2,1,0:T(8,128)}, f32[16,64,128]{2,1,0:T(8,128)S(1)}, u32[]{:S(2)}, u32[]{:S(2)}) collective-permute-start(f32[16,64,128]{2,1,0:T(8,128)} %get-tuple-element.46.low_ref), channel_id=1, source_target_pairs={{0,1},{1,0},{2,3},{3,2},{4,5},{5,4},{6,7},{7,6},{8,9},{9,8},{10,11... | collective-permute-start | bytes 1572872 | tf_op jit(solution)/shard_map/ppermute | solution.py:537
  7.2 6.9 %collective-permute-start.1 = (f32[16,64,128]{2,1,0:T(8,128)}, f32[16,64,128]{2,1,0:T(8,128)S(1)}, u32[]{:S(2)}, u32[]{:S(2)}) collective-permute-start(f32[16,64,128]{2,1,0:T(8,128)} %get-tuple-element.47.high_ref), channel_id=1, source_target_pairs={{1,2},{2,1},{3,4},{4,3},{5,6},{6,5},{7,8},{8,7},{9,10},{10,9},{11,... | collective-permute-start | bytes 1572872 | tf_op jit(solution)/shard_map/ppermute | solution.py:537
  14.1 4.1 %keep.1 = (f32[32,64,128]{2,1,0:T(8,128)}, bf16[2048,256]{1,0:T(8,128)(2,1)}, bf16[2048,256]{1,0:T(8,128)(2,1)}) custom-call(bf16[256,2048]{1,0:T(8,128)(2,1)} %bitcast.30, bf16[256,2048]{1,0:T(8,128)(2,1)} %bitcast.32, bf16[256,128]{1,0:T(8,128)(2,1)} %bitcast.18, bf16[256,128]{1,0:T(8,128)(2,1)} %bitcast.23, ...), custom_call_target="tpu_custom_call", output_to_operand_aliasing={{1}: (5, {}), {2}: (6, {})} | custom-call | flops 1500000000 | bytes 6291456 | tf_op jit(solution)/shard_map/keep/pallas_call | solution.py:575
  18.2 0.0 copy-start.5
  18.2 0.0 copy-start.10
  18.2 7.2 %inner.1 = (bf16[2048,256]{1,0:T(8,128)(2,1)}, bf16[2048,256]{1,0:T(8,128)(2,1)}, f32[32,256]{1,0:T(8,128)}, f32[32,256]{1,0:T(8,128)}, f32[256,128]{1,0:T(8,128)}, /*index=5*/f32[256,128]{1,0:T(8,128)}) custom-call(bf16[256,2048]{1,0:T(8,128)(2,1)} %bitcast.33, bf16[2048,256]{1,0:T(8,128)(2,1)} %get-tuple-element.48.xt_ref, ...), custom_call_target="tpu_custom_call" | custom-call | flops 3500000000 | bytes 14680064 | tf_op jit(solution)/shard_map/inner/pallas_call | solution.py:321
  25.4 0.0 collective-permute-done.low_ref
  25.4 0.3 collective-permute-done.1.high_ref
  25.6 0.0 copy-done.5
  25.6 0.0 copy-done.10
  25.6 0.2 join.1
  25.9 33.6 %all_to_all.15 = f32[32,65,1,128]{3,2,1,0:T(1,128)S(1)} all-to-all(f32[32,65,1,128]{3,2,1,0:T(1,128)S(1)} %bitcast.15), channel_id=1, replica_groups=mesh['dp'=8,'seq'=32] {'seq'}, dimensions={0} | all-to-all | bytes 2129920 | tf_op jit(solution)/shard_map/all_to_all | solution.py:595
  59.5 0.0 copy-start.17
  59.5 0.1 scan.1
  59.6 30.6 %all_to_all.16.mine_ref = f32[32,64,128]{2,1,0:T(8,128)S(1)} all-to-all(f32[32,64,128]{2,1,0:T(8,128)S(1)} %scan.1), channel_id=1, replica_groups=mesh['dp'=8,'seq'=32] {'seq'}, dimensions={0} | all-to-all | bytes 2097152 | tf_op jit(solution)/shard_map/all_to_all | solution.py:597
  90.2 0.0 copy-start.4
  90.2 0.0 copy-start.15
  90.3 0.2 pass_on.1
  90.5 2.7 %collective-permute-start.2 = (f32[16,64,128]{2,1,0:T(8,128)S(1)}, f32[16,64,128]{2,1,0:T(8,128)S(1)}, u32[]{:S(2)}, u32[]{:S(2)}) collective-permute-start(f32[16,64,128]{2,1,0:T(8,128)S(1)} %get-tuple-element.54), channel_id=1, source_target_pairs={{0,1},{1,0},{2,3},{3,2},{4,5},{5,4},{6,7},{7,6},{8,9},{9,8},{10,11... | collective-permute-start | bytes 1572872 | tf_op jit(solution)/shard_map/ppermute | solution.py:537
  93.2 1.6 %collective-permute-start.3 = (f32[16,64,128]{2,1,0:T(8,128)S(1)}, f32[16,64,128]{2,1,0:T(8,128)S(1)}, u32[]{:S(2)}, u32[]{:S(2)}) collective-permute-start(f32[16,64,128]{2,1,0:T(8,128)S(1)} %get-tuple-element.55), channel_id=1, source_target_pairs={{1,2},{2,1},{3,4},{4,3},{5,6},{6,5},{7,8},{8,7},{9,10},{10,9},{11,... | collective-permute-start | bytes 1572872 | tf_op jit(solution)/shard_map/ppermute | solution.py:537
  94.9 2.1 %own.1 = (bf16[256,2048]{1,0:T(8,128)(2,1)}, bf16[256,2048]{1,0:T(8,128)(2,1)}, f32[32,256]{1,0:T(8,128)S(1)}, f32[128,256]{1,0:T(8,128)S(1)}, f32[128,256]{1,0:...) custom-call(f32[32,64,128]{2,1,0:T(8,128)S(1)} %all_to_all.16.mine_ref, bf16[2048,256]{1,0:T(8,128)(2,1)S(1)} %copy-done.3, ...), custom_call_target="tpu_custom_call" | custom-call | flops 2000000000 | bytes 8388608 | tf_op jit(solution)/shard_map/own/pallas_call | solution.py:602
  97.0 0.6 copy-done.13
  97.7 0.7 copy-done.14
  98.3 0.6 copy-done.16
  98.9 2.4 %collective-permute-done.2.low_ref = f32[16,64,128]{2,1,0:T(8,128)S(1)} collective-permute-done((f32[16,64,128]{2,1,0:T(8,128)S(1)}, f32[16,64,128]{2,1,0:T(8,128)S(1)}, u32[]{:S(2)}, u32[]{:S(2)}) %collective-permute-start.2) | collective-permute-done | bytes 524320 | tf_op jit(solution)/shard_map/ppermute | solution.py:537
  101.3 4.7 %collective-permute-done.3.high_ref = f32[16,64,128]{2,1,0:T(8,128)S(1)} collective-permute-done((f32[16,64,128]{2,1,0:T(8,128)S(1)}, f32[16,64,128]{2,1,0:T(8,128)S(1)}, u32[]{:S(2)}, u32[]{:S(2)}) %collective-permute-start.3) | collective-permute-done | bytes 524320 | tf_op jit(solution)/shard_map/ppermute | solution.py:537
  106.1 1.0 sums.1
  107.1 12.9 %all-to-all-start.2 = ((f32[256,1,128]{2,1,0:T(1,128)}), f32[256,1,128]{2,1,0:T(1,128)S(1)}, u32[]{:S(2)}, u32[]{:S(2)}) async-start(f32[256,1,128]{2,1,0:T(1,128)} %sums.1), calls=%async_computation.2 | async-start | bytes 262144 | tf_op jit(solution)/shard_map/all_to_all | solution.py:614
  119.9 5.7 %other.1 = (bf16[256,2048]{1,0:T(8,128)(2,1)}, bf16[256,2048]{1,0:T(8,128)(2,1)}, bf16[256,128]{1,0:T(8,128)(2,1)}, bf16[256,128]{1,0:T(8,128)(2,1)}, f32[32,256]{1,0:T(8,128)}) custom-call(f32[16,64,128]{2,1,0:T(8,128)} %copy-done.1, f32[16,64,128]{2,1,0:T(8,128)} %copy-done.2, ...), custom_call_target="tpu_custom_call", output_to_operand_aliasing={{0}: (17, {}), {1}: (18, {})} | custom-call | flops 2000000000 | bytes 8388608 | tf_op jit(solution)/shard_map/other/pallas_call | solution.py:615
  125.7 7.3 %all-to-all-done.2.sums_ref = f32[256,1,128]{2,1,0:T(1,128)S(1)} async-done(((f32[256,1,128]{2,1,0:T(1,128)}), f32[256,1,128]{2,1,0:T(1,128)S(1)}, u32[]{:S(2)}, u32[]{:S(2)}) %all-to-all-start.2) | async-done | bytes 131104 | tf_op jit(solution)/shard_map/all_to_all | solution.py:614
  133.0 0.8 total.1
  (26 shorter events, 0.0 us)
Async XLA Ops:
  4.7 20.7 %collective-permute-start = (f32[16,64,128]{2,1,0:T(8,128)}, f32[16,64,128]{2,1,0:T(8,128)S(1)}, u32[]{:S(2)}, u32[]{:S(2)}) collective-permute-start(f32[16,64,128]{2,1,0:T(8,128)} %get-tuple-element.46.low_ref), channel_id=1, source_target_pairs={{0,1},{1,0},{2,3},{3,2},{4,5},{5,4},{6,7},{7,6},{8,9},{9,8},{10,11... | collective-permute-start | bytes 1572872 | tf_op jit(solution)/shard_map/ppermute | solution.py:537
  7.2 18.4 %collective-permute-start.1 = (f32[16,64,128]{2,1,0:T(8,128)}, f32[16,64,128]{2,1,0:T(8,128)S(1)}, u32[]{:S(2)}, u32[]{:S(2)}) collective-permute-start(f32[16,64,128]{2,1,0:T(8,128)} %get-tuple-element.47.high_ref), channel_id=1, source_target_pairs={{1,2},{2,1},{3,4},{4,3},{5,6},{6,5},{7,8},{8,7},{9,10},{10,9},{11,... | collective-permute-start | bytes 1572872 | tf_op jit(solution)/shard_map/ppermute | solution.py:537
  18.2 7.5 %copy-start.5 = (f32[32,64,128]{2,1,0:T(8,128)S(1)}, f32[32,64,128]{2,1,0:T(8,128)}, u32[]{:S(2)}) copy-start(f32[32,64,128]{2,1,0:T(8,128)} %get-tuple-element.45.keep_ref) | copy-start | bytes 3145732
  18.2 7.5 %copy-start.10 = (f32[32,256]{1,0:T(8,128)S(1)}, f32[32,256]{1,0:T(8,128)}, u32[]{:S(2)}) copy-start(f32[32,256]{1,0:T(8,128)} %get-tuple-element.42.cum_ref) | copy-start | bytes 98308
  59.5 30.8 %copy-start.8 = (f32[16,64,128]{2,1,0:T(8,128)S(1)}, f32[16,64,128]{2,1,0:T(8,128)}, u32[]{:S(2)}) copy-start(f32[16,64,128]{2,1,0:T(8,128)} %get-tuple-element.46.low_ref) | copy-start | bytes 1572868
  59.5 30.8 %copy-start.9 = (f32[16,64,128]{2,1,0:T(8,128)S(1)}, f32[16,64,128]{2,1,0:T(8,128)}, u32[]{:S(2)}) copy-start(f32[16,64,128]{2,1,0:T(8,128)} %get-tuple-element.47.high_ref) | copy-start | bytes 1572868
  59.5 35.3 %copy-start.11 = (bf16[1,256,128]{2,1,0:T(8,128)(2,1)S(1)}, bf16[1,256,128]{2,1,0:T(8,128)(2,1)}, u32[]{:S(2)}) copy-start(bf16[1,256,128]{2,1,0:T(8,128)(2,1)} %param.8) | copy-start | bytes 196612
  59.5 35.3 %copy-start.12 = (bf16[1,256,128]{2,1,0:T(8,128)(2,1)S(1)}, bf16[1,256,128]{2,1,0:T(8,128)(2,1)}, u32[]{:S(2)}) copy-start(bf16[1,256,128]{2,1,0:T(8,128)(2,1)} %param.9) | copy-start | bytes 196612
  59.5 35.3 %copy-start.17 = (f32[32,256]{1,0:T(8,128)S(1)}, f32[32,256]{1,0:T(8,128)}, u32[]{:S(2)}) copy-start(f32[32,256]{1,0:T(8,128)} %get-tuple-element.59.skiprow_ref) | copy-start | bytes 98308
  59.6 35.2 %copy-start.6 = (bf16[2048,256]{1,0:T(8,128)(2,1)S(1)}, bf16[2048,256]{1,0:T(8,128)(2,1)}, u32[]{:S(2)}) copy-start(bf16[2048,256]{1,0:T(8,128)(2,1)} %get-tuple-element.48.xt_ref) | copy-start | bytes 3145732
  59.6 35.2 %copy-start.7 = (bf16[2048,256]{1,0:T(8,128)(2,1)S(1)}, bf16[2048,256]{1,0:T(8,128)(2,1)}, u32[]{:S(2)}) copy-start(bf16[2048,256]{1,0:T(8,128)(2,1)} %get-tuple-element.49.gt_ref) | copy-start | bytes 3145732
  90.2 4.6 %copy-start = (f32[32,64,128]{2,1,0:T(8,128)}, f32[32,64,128]{2,1,0:T(8,128)S(1)}, u32[]{:S(2)}) copy-start(f32[32,64,128]{2,1,0:T(8,128)S(1)} %all_to_all.16.mine_ref) | copy-start | bytes 3145732
  90.2 4.6 %copy-start.3 = (bf16[2048,256]{1,0:T(8,128)(2,1)S(1)}, bf16[2048,256]{1,0:T(8,128)(2,1)}, u32[]{:S(2)}) copy-start(bf16[2048,256]{1,0:T(8,128)(2,1)} %get-tuple-element.56.yt_ref) | copy-start | bytes 3145732
  90.2 4.6 %copy-start.4 = (bf16[2048,256]{1,0:T(8,128)(2,1)S(1)}, bf16[2048,256]{1,0:T(8,128)(2,1)}, u32[]{:S(2)}) copy-start(bf16[2048,256]{1,0:T(8,128)(2,1)} %get-tuple-element.57.gxt_ref) | copy-start | bytes 3145732
  90.2 4.6 %copy-start.15 = (f32[32,256]{1,0:T(8,128)S(1)}, f32[32,256]{1,0:T(8,128)}, u32[]{:S(2)}) copy-start(f32[32,256]{1,0:T(8,128)} %get-tuple-element.58.inner_row_ref) | copy-start | bytes 98308
  90.5 10.8 %collective-permute-start.2 = (f32[16,64,128]{2,1,0:T(8,128)S(1)}, f32[16,64,128]{2,1,0:T(8,128)S(1)}, u32[]{:S(2)}, u32[]{:S(2)}) collective-permute-start(f32[16,64,128]{2,1,0:T(8,128)S(1)} %get-tuple-element.54), channel_id=1, source_target_pairs={{0,1},{1,0},{2,3},{3,2},{4,5},{5,4},{6,7},{7,6},{8,9},{9,8},{10,11... | collective-permute-start | bytes 1572872 | tf_op jit(solution)/shard_map/ppermute | solution.py:537
  93.2 12.8 %collective-permute-start.3 = (f32[16,64,128]{2,1,0:T(8,128)S(1)}, f32[16,64,128]{2,1,0:T(8,128)S(1)}, u32[]{:S(2)}, u32[]{:S(2)}) collective-permute-start(f32[16,64,128]{2,1,0:T(8,128)S(1)} %get-tuple-element.55), channel_id=1, source_target_pairs={{1,2},{2,1},{3,4},{4,3},{5,6},{6,5},{7,8},{8,7},{9,10},{10,9},{11,... | collective-permute-start | bytes 1572872 | tf_op jit(solution)/shard_map/ppermute | solution.py:537
  97.0 0.6 copy-start.13
  97.7 0.7 copy-start.14
  98.3 0.6 copy-start.16
  101.3 5.8 %copy-start.1 = (f32[16,64,128]{2,1,0:T(8,128)}, f32[16,64,128]{2,1,0:T(8,128)S(1)}, u32[]{:S(2)}) copy-start(f32[16,64,128]{2,1,0:T(8,128)S(1)} %collective-permute-done.2.low_ref) | copy-start | bytes 1572868
  106.1 1.0 copy-start.2
  107.1 25.9 %all-to-all-start.2 = ((f32[256,1,128]{2,1,0:T(1,128)}), f32[256,1,128]{2,1,0:T(1,128)S(1)}, u32[]{:S(2)}, u32[]{:S(2)}) async-start(f32[256,1,128]{2,1,0:T(1,128)} %sums.1), calls=%async_computation.2 | async-start | bytes 262144 | tf_op jit(solution)/shard_map/all_to_all | solution.py:614

commit v7 on v4

--- a/solution.py
+++ b/solution.py
@@ -341,9 +341,28 @@
     return gct, gbt, copies
 
 
+def partner_weights(mine_ref, xt_ref, gt_ref, b_ref, c_ref, cum_ref, out_ref):
+    _, state_first, adjoint_first = halves(False)
+    for i in range(HALF_STEPS):
+        for step, data_ref, rhs_ref, is_state in (
+            (state_first + i, gt_ref, c_ref, True),
+            (adjoint_first + i, xt_ref, b_ref, False),
+        ):
+            cum = cum_ref[head_rows(step), :]
+            last = cum[:, GROUP - 1 :]
+            lag = cum if is_state else last - cum
+            data = data_ref[feature_rows(step), :].astype(F32) * spread(lag * jnp.exp(lag))
+            made = dot(data.astype(BF16), rhs_ref[...], 1, 0).reshape(STEP, SIZE, STATE)
+            gain = last * jnp.exp(last)
+            here = pl.multiple_of(step * STEP, STEP)
+            for j in range(STEP):
+                out_ref[here + j] = made[j] + gain[j : j + 1] * mine_ref[here + j]
+
+
 def own_kernel(
     mine_ref, yt_ref, gxt_ref, xt_ref, gt_ref, b_ref, c_ref, cum_ref,
-    y_hbm, gx_hbm, row_ref, gct_ref, gbt_ref,
+    low_row_ref, high_row_ref, low_skiprow_ref, high_skiprow_ref,
+    y_hbm, gx_hbm, row_ref, gct_ref, gbt_ref, weights_ref, base_ref,
     out_s, sems,
 ):
     _, state_first, adjoint_first = halves(True)
@@ -365,42 +384,28 @@
         copies += made
     gct_ref[...] = gct
     gbt_ref[...] = gbt
+    partner_weights(mine_ref, xt_ref, gt_ref, b_ref, c_ref, cum_ref, weights_ref)
+    row = row_ref[...] + jnp.concatenate([low_row_ref[...], high_row_ref[...]], axis=0)
+    alog = jnp.sum(row * cum_ref[...], axis=1, keepdims=True)
+    skiprow = jnp.concatenate([low_skiprow_ref[...], high_skiprow_ref[...]], axis=0)
+    skip = jnp.sum(skiprow, axis=1, keepdims=True)
+    lane = iota((HEADS, STATE), 1)
+    base_ref[...] = jnp.where(lane == 0, alog, jnp.where(lane == 1, skip, 0.0))
+    row_ref[...] = row
     for made in copies:
         made.wait()
 
 
-def sums_kernel(
-    mine_ref, low_ref, high_ref, xt_ref, gt_ref, b_ref, c_ref, cum_ref, low_row_ref,
-    high_row_ref, own_row_ref, low_skiprow_ref, high_skiprow_ref, dt_ref, alog_ref,
-    gdt_ref, sums_ref,
-    row_s,
-):
-    state_low, state_first, adjoint_first = halves(False)
-    for i in range(HALF_STEPS):
-        state = take_half(low_ref, high_ref, state_low, i)
-        adjoint = take_half(high_ref, low_ref, state_low, i)
-        row_s[head_rows(state_first + i), :] = carried_rows(
-            state, gt_ref, c_ref, cum_ref, state_first + i
-        )[-1]
-        row_s[head_rows(adjoint_first + i), :] = scaled_rows(
-            adjoint, xt_ref, b_ref, cum_ref, adjoint_first + i
-        )[-1]
-    overlap = jnp.concatenate(
+def sums_kernel(weights_ref, low_ref, high_ref, base_ref, sums_ref):
+    product = jnp.concatenate(
         [
-            jnp.sum(mine_ref[:HALF] * low_ref[...], axis=1),
-            jnp.sum(mine_ref[HALF:] * high_ref[...], axis=1),
+            jnp.sum(weights_ref[:HALF] * low_ref[...], axis=1),
+            jnp.sum(weights_ref[HALF:] * high_ref[...], axis=1),
         ],
         axis=0,
     )
-    overlap = jnp.sum(overlap, axis=1, keepdims=True) * jnp.exp(cum_ref[:, GROUP - 1 :])
-    final = iota((HEADS, GROUP), 1) == GROUP - 1
-    inner_row = jnp.concatenate([low_row_ref[...], high_row_ref[...]], axis=0)
-    row = inner_row + own_row_ref[...] + row_s[...] + jnp.where(final, overlap, 0.0)
-    gdt = -jnp.exp(column(alog_ref[...])) * dot(row, triangle(), 1, 1, EXACT)
-    gdt_ref[...] = gdt
-    alog = jnp.sum(gdt * dt_ref[...], axis=1, keepdims=True)
-    skiprow = jnp.concatenate([low_skiprow_ref[...], high_skiprow_ref[...]], axis=0)
-    skip = jnp.sum(skiprow, axis=1, keepdims=True)
+    alog = base_ref[:, :1] + jnp.sum(product, axis=1, keepdims=True)
+    skip = base_ref[:, 1:2]
     sums = jnp.concatenate(
         [as_row(alog), as_row(skip), jnp.zeros((1, STATE - 2 * HEADS), F32)], axis=1
     )
@@ -415,9 +420,10 @@
 
 def other_kernel(
     low_ref, high_ref, yt_ref, gxt_ref, xt_ref, gt_ref, b_ref, c_ref, cum_ref,
-    gct_ref, gbt_ref, low_gc_ref, high_gc_ref, low_gb_ref, high_gb_ref, y_in, gx_in,
-    y_hbm, gx_hbm, gc_ref, gb_ref,
-    out_s, sems,
+    gct_ref, gbt_ref, low_gc_ref, high_gc_ref, low_gb_ref, high_gb_ref,
+    mine_ref, row_ref, alog_ref, y_in, gx_in,
+    y_hbm, gx_hbm, gc_ref, gb_ref, gdt_ref,
+    out_s, row_s, sems,
 ):
     state_low, state_first, adjoint_first = halves(False)
     gct = gct_ref[...]
@@ -427,8 +433,10 @@
         state_step, adjoint_step = state_first + i, adjoint_first + i
         state = take_half(low_ref, high_ref, state_low, i)
         adjoint = take_half(high_ref, low_ref, state_low, i)
-        raw, gf, from_start, _ = carried_rows(state, gt_ref, c_ref, cum_ref, state_step)
-        back, xf, to_end, _ = scaled_rows(adjoint, xt_ref, b_ref, cum_ref, adjoint_step)
+        raw, gf, from_start, row = carried_rows(state, gt_ref, c_ref, cum_ref, state_step)
+        row_s[head_rows(state_step), :] = row
+        back, xf, to_end, row = scaled_rows(adjoint, xt_ref, b_ref, cum_ref, adjoint_step)
+        row_s[head_rows(adjoint_step), :] = row
         gct, gbt, made = give_out(
             i, state_step, adjoint_step, state, adjoint, (raw, gf, from_start, back, xf, to_end),
             yt_ref, gxt_ref, y_hbm, gx_hbm, out_s, sems, gct, gbt,
@@ -436,6 +444,17 @@
         copies += made
     gc_ref[...] = (low_gc_ref[...] + high_gc_ref[...] + gct.T).astype(BF16)
     gb_ref[...] = (low_gb_ref[...] + high_gb_ref[...] + gbt.T).astype(BF16)
+    overlap = jnp.concatenate(
+        [
+            jnp.sum(mine_ref[:HALF] * low_ref[...], axis=1),
+            jnp.sum(mine_ref[HALF:] * high_ref[...], axis=1),
+        ],
+        axis=0,
+    )
+    overlap = jnp.sum(overlap, axis=1, keepdims=True) * jnp.exp(cum_ref[:, GROUP - 1 :])
+    final = iota((HEADS, GROUP), 1) == GROUP - 1
+    row = row_ref[...] + row_s[...] + jnp.where(final, overlap, 0.0)
+    gdt_ref[...] = -jnp.exp(column(alog_ref[...])) * dot(row, triangle(), 1, 1, EXACT)
     for made in copies:
         made.wait()
 
@@ -513,38 +532,32 @@
         pltpu.SemaphoreType.DMA((2 * HALF_STEPS,)),
     ]
     part = shape_of((STATE, GROUP))
-    y, gx, own_row, gct, gbt = call(
+    y, gx, row, gct, gbt, weights, base = call(
         own_kernel,
         "own",
-        [tall, tall, rows, part, part],
-        [hbm, hbm, vmem, vmem, vmem],
+        [tall, tall, rows, part, part, all_heads, shape_of((HEADS, STATE))],
+        [hbm, hbm] + [vmem] * 5,
         scratch_shapes=out_scratch,
         cost=cost(4),
-    )(mine, yt, gxt, xt, gt, b, c, cum)
+    )(mine, yt, gxt, xt, gt, b, c, cum, low_row, high_row, low_skiprow, high_skiprow)
     everyone = lax.axis_size("dp") * lax.axis_size("seq")
-    gdt, copies = call(
-        sums_kernel,
-        "sums",
-        [rows, shape_of((everyone, 1, STATE))],
-        scratch_shapes=[pltpu.VMEM((HEADS, GROUP), F32)],
-    )(
-        mine, low_back, high_back, xt, gt, b, c, cum, low_row, high_row, own_row,
-        low_skiprow, high_skiprow, steps, alog,
+    copies = call(sums_kernel, "sums", shape_of((everyone, 1, STATE)))(
+        weights, low_back, high_back, base
     )
     sums = lax.all_to_all(copies, ("dp", "seq"), 0, 0, tiled=True)
-    y, gx, gc, gb = call(
+    y, gx, gc, gb, gdt = call(
         other_kernel,
         "other",
-        [tall, tall, shape_of((GROUP, STATE), BF16), shape_of((GROUP, STATE), BF16)],
-        [hbm, hbm, vmem, vmem],
-        in_specs=[vmem] * 15 + [hbm, hbm],
-        input_output_aliases={15: 0, 16: 1},
-        scratch_shapes=out_scratch,
+        [tall, tall, shape_of((GROUP, STATE), BF16), shape_of((GROUP, STATE), BF16), rows],
+        [hbm, hbm, vmem, vmem, vmem],
+        in_specs=[vmem] * 18 + [hbm, hbm],
+        input_output_aliases={18: 0, 19: 1},
+        scratch_shapes=[out_scratch[0], pltpu.VMEM((HEADS, GROUP), F32), out_scratch[1]],
         cost=cost(4),
         limit=LARGE_LIMIT,
     )(
         low_back, high_back, yt, gxt, xt, gt, b, c, cum, gct, gbt,
-        low_gc, high_gc, low_gb, high_gb, y, gx,
+        low_gc, high_gc, low_gb, high_gb, mine, row, alog, y, gx,
     )
     galog, gskip = call(
         total_kernel, "total", [shape_of((1, HEADS)), shape_of((1, HEADS))]

time: 134 us -> 132 us (0.985)
  waiting for transfers between devices: 13.8 us -> 11.3 us
    ppermute x2, waiting for transfers between devices: 4.51 us -> 2.92 us  [swap(): lax.ppermute(high, 'seq', high_pairs)]
  transfers between devices with their start and end apart: 6 -> 6, of which waited for: 4 -> 3; matrix products, arithmetic and copies ran while one was open for 0% -> 0% of each run, Pallas kernels for 11% -> 12%
where the time goes in v7:
time: 132 us
  blocking collectives  59.8 us (45%)
  starting transfers between devices  33.7 us (26%)
  Pallas kernels  22.8 us (17%)
  waiting for transfers between devices  11.3 us (9%)
  local copies, waits for them, and re-layouts  3.29 us (2%)
    all_to_all x1, blocking collectives, shards(): parts = lax.all_to_all(joined, 'seq', 0, 0, tiled=True)  30.9 us
    all_to_all x1, blocking collectives, shards(): mine = lax.all_to_all(scanned, 'seq', 0, 0, tiled=True)  28.9 us
    all_to_all x1, starting transfers between devices, shards(): sums = lax.all_to_all(copies, ('dp', 'seq'), 0, 0, tiled=True)  12.9 us
    ppermute x2, starting transfers between devices, swap(): lax.ppermute(high, 'seq', high_pairs)  10.1 us
    pallas_call x2, Pallas kernels, inner(): call(functools.partial(inner_kernel, offset), 'inner', [wide, wide, rows,...  7.88 us
    all_to_all x1, waiting for transfers between devices, shards(): sums = lax.all_to_all(copies, ('dp', 'seq'), 0, 0, tiled=True)  7.16 us
    ppermute x2, starting transfers between devices, swap(): lax.ppermute(low, 'seq', low_pairs)  6.79 us
    pallas_call x1, Pallas kernels, shards(): call(other_kernel, 'other', [tall, tall, shape_of((GROUP, STATE), BF16),...  5.87 us
  transfers between devices with their start and end apart: 6, of which 3 were waited for; matrix products, arithmetic and copies ran while one was open for 0% of the time, Pallas kernels for 12%

profile of v7, /device:TPU:1, one launch (start us, length us, event | category | flops | bytes accessed | tf_op | source)
XLA Modules:
  0.0 131.8 jit_solution(346403745703897242)
XLA Ops:
  0.6 4.5 %states.1 = (f32[16,64,128]{2,1,0:T(8,128)}, f32[16,64,128]{2,1,0:T(8,128)}, f32[32,64,128]{2,1,0:T(8,128)}, f32[32,1,128]{2,1,0:T(1,128)}, bf16[2048,256]{1,0:T...) custom-call(bf16[256,2048]{1,0:T(8,128)(2,1)} %bitcast.28, bf16[256,2048]{1,0:T(8,128)(2,1)} %bitcast.13, ...), custom_call_target="tpu_custom_call" | custom-call | tf_op jit(solution)/shard_map/states/pallas_call | solution.py:501
  5.2 2.6 %collective-permute-start = (f32[16,64,128]{2,1,0:T(8,128)}, f32[16,64,128]{2,1,0:T(8,128)S(1)}, u32[]{:S(2)}, u32[]{:S(2)}) collective-permute-start(f32[16,64,128]{2,1,0:T(8,128)} %get-tuple-element.47.low_ref), channel_id=1, source_target_pairs={{0,1},{1,0},{2,3},{3,2},{4,5},{5,4},{6,7},{7,6},{8,9},{9,8},{10,11... | collective-permute-start | bytes 1572872 | tf_op jit(solution)/shard_map/ppermute | solution.py:487
  7.7 6.9 %collective-permute-start.1 = (f32[16,64,128]{2,1,0:T(8,128)}, f32[16,64,128]{2,1,0:T(8,128)S(1)}, u32[]{:S(2)}, u32[]{:S(2)}) collective-permute-start(f32[16,64,128]{2,1,0:T(8,128)} %get-tuple-element.48.high_ref), channel_id=1, source_target_pairs={{1,2},{2,1},{3,4},{4,3},{5,6},{6,5},{7,8},{8,7},{9,10},{10,9},{11,... | collective-permute-start | bytes 1572872 | tf_op jit(solution)/shard_map/ppermute | solution.py:487
  14.6 3.8 %all-to-all-start.1 = ((f32[32,1,128]{2,1,0:T(1,128)}), f32[32,1,128]{2,1,0:T(1,128)S(1)}, u32[]{:S(2)}, u32[]{:S(2)}) async-start(f32[32,1,128]{2,1,0:T(1,128)} %get-tuple-element.56), calls=%async_computation.1 | async-start | bytes 32768 | tf_op jit(solution)/shard_map/all_to_all | solution.py:518
  18.4 0.0 copy-start.9
  18.4 4.7 %inner.2 = (bf16[2048,256]{1,0:T(8,128)(2,1)}, bf16[2048,256]{1,0:T(8,128)(2,1)}, f32[16,256]{1,0:T(8,128)}, f32[16,256]{1,0:T(8,128)}, f32[256,128]{1,0:T(8,128)}, /*index=5*/f32[256,128]{1,0:T(8,128)}) custom-call(bf16[256,2048]{1,0:T(8,128)(2,1)} %bitcast.14, bf16[2048,256]{1,0:T(8,128)(2,1)} %get-tuple-element.49.refs_1_.xt_ref, ...), custom_call_target="tpu_custom_call" | custom-call | flops 2000000000 | bytes 8388608 | tf_op jit(solution)/shard_map/inner/pallas_call | solution.py:265
  23.2 0.0 collective-permute-done.low_ref
  23.2 2.9 %collective-permute-done.1.high_ref = f32[16,64,128]{2,1,0:T(8,128)S(1)} collective-permute-done((f32[16,64,128]{2,1,0:T(8,128)}, f32[16,64,128]{2,1,0:T(8,128)S(1)}, u32[]{:S(2)}, u32[]{:S(2)}) %collective-permute-start.1) | collective-permute-done | bytes 524320 | tf_op jit(solution)/shard_map/ppermute | solution.py:487
  26.1 0.2 join.1
  26.3 1.2 all-to-all-done.1.gain_ref
  27.6 30.9 %all_to_all.20.part_ref = f32[32,64,128]{2,1,0:T(8,128)S(1)} all-to-all(f32[32,64,128]{2,1,0:T(8,128)S(1)} %join.1), channel_id=1, replica_groups=mesh['dp'=8,'seq'=32] {'seq'}, dimensions={0} | all-to-all | bytes 2097152 | tf_op jit(solution)/shard_map/all_to_all | solution.py:522
  58.5 0.1 scan.1
  58.6 0.0 copy-start.5
  58.6 28.9 %all_to_all.21.mine_ref = f32[32,64,128]{2,1,0:T(8,128)S(1)} all-to-all(f32[32,64,128]{2,1,0:T(8,128)S(1)} %scan.1), channel_id=1, replica_groups=mesh['dp'=8,'seq'=32] {'seq'}, dimensions={0} | all-to-all | bytes 2097152 | tf_op jit(solution)/shard_map/all_to_all | solution.py:524
  87.5 0.2 pass_on.1
  87.8 0.0 copy-start.21
  87.8 4.2 %collective-permute-start.2 = (f32[16,64,128]{2,1,0:T(8,128)S(1)}, f32[16,64,128]{2,1,0:T(8,128)S(1)}, u32[]{:S(2)}, u32[]{:S(2)}) collective-permute-start(f32[16,64,128]{2,1,0:T(8,128)S(1)} %get-tuple-element.57), channel_id=1, source_target_pairs={{0,1},{1,0},{2,3},{3,2},{4,5},{5,4},{6,7},{7,6},{8,9},{9,8},{10,11... | collective-permute-start | bytes 1572872 | tf_op jit(solution)/shard_map/ppermute | solution.py:487
  92.0 3.3 %collective-permute-start.3 = (f32[16,64,128]{2,1,0:T(8,128)S(1)}, f32[16,64,128]{2,1,0:T(8,128)S(1)}, u32[]{:S(2)}, u32[]{:S(2)}) collective-permute-start(f32[16,64,128]{2,1,0:T(8,128)S(1)} %get-tuple-element.58), channel_id=1, source_target_pairs={{1,2},{2,1},{3,4},{4,3},{5,6},{6,5},{7,8},{8,7},{9,10},{10,9},{11,... | collective-permute-start | bytes 1572872 | tf_op jit(solution)/shard_map/ppermute | solution.py:487
  95.4 3.1 %inner.3 = (bf16[2048,256]{1,0:T(8,128)(2,1)S(1)}, bf16[2048,256]{1,0:T(8,128)(2,1)S(1)}, f32[16,256]{1,0:T(8,128)S(1)}, f32[16,256]{1,0:T(8,128)S(1)}, f32[256,128]{1,0:T(8,128)S(1)}, /*index=5*/f32[256,128]{1,0:T(8,128)S(1)}) custom-call(bf16[256,2048]{1,0:T(8,128)(2,1)S(1)} %bitcast.15, ...), custom_call_target="tpu_custom_call", output_to_operand_aliasing={{0}: (7, {}), {1}: (8, {})} | custom-call | flops 2000000000 | bytes 8388608 | tf_op jit(solution)/shard_map/inner/pallas_call | solution.py:265
  98.5 0.6 copy-done.16
  99.1 0.6 copy-done.17
  99.8 2.1 %own.1 = (bf16[256,2048]{1,0:T(8,128)(2,1)}, bf16[256,2048]{1,0:T(8,128)(2,1)}, f32[32,256]{1,0:T(8,128)S(1)}, f32[128,256]{1,0:T(8,128)S(1)}, f32[128,256]{1,0:...) custom-call(f32[32,64,128]{2,1,0:T(8,128)S(1)} %all_to_all.21.mine_ref, ...), custom_call_target="tpu_custom_call" | custom-call | flops 2000000000 | bytes 8388608 | tf_op jit(solution)/shard_map/own/pallas_call | solution.py:535
  102.0 0.7 copy-done.18
  102.7 0.6 copy-done.19
  103.3 0.6 copy-done.20
  103.9 0.0 collective-permute-done.2.low_ref
  103.9 0.0 collective-permute-done.3.high_ref
  103.9 1.0 sums.1
  105.0 12.9 %all-to-all-start.3 = ((f32[256,1,128]{2,1,0:T(1,128)}), f32[256,1,128]{2,1,0:T(1,128)S(1)}, u32[]{:S(2)}, u32[]{:S(2)}) async-start(f32[256,1,128]{2,1,0:T(1,128)} %sums.1), calls=%async_computation.3 | async-start | bytes 262144 | tf_op jit(solution)/shard_map/all_to_all | solution.py:547
  117.9 5.9 %other.1 = (bf16[256,2048]{1,0:T(8,128)(2,1)}, bf16[256,2048]{1,0:T(8,128)(2,1)}, bf16[256,128]{1,0:T(8,128)(2,1)}, bf16[256,128]{1,0:T(8,128)(2,1)}, f32[32,256]{1,0:T(8,128)}) custom-call(f32[16,64,128]{2,1,0:T(8,128)} %copy-done.1, f32[16,64,128]{2,1,0:T(8,128)} %copy-done.2, ...), custom_call_target="tpu_custom_call", output_to_operand_aliasing={{0}: (18, {}), {1}: (19, {})} | custom-call | flops 2000000000 | bytes 8388608 | tf_op jit(solution)/shard_map/other/pallas_call | solution.py:548
  123.8 7.2 %all-to-all-done.3.sums_ref = f32[256,1,128]{2,1,0:T(1,128)S(1)} async-done(((f32[256,1,128]{2,1,0:T(1,128)}), f32[256,1,128]{2,1,0:T(1,128)S(1)}, u32[]{:S(2)}, u32[]{:S(2)}) %all-to-all-start.3) | async-done | bytes 131104 | tf_op jit(solution)/shard_map/all_to_all | solution.py:547
  130.9 0.8 total.1
  (40 shorter events, 0.1 us)
Async XLA Ops:
  5.2 18.0 %collective-permute-start = (f32[16,64,128]{2,1,0:T(8,128)}, f32[16,64,128]{2,1,0:T(8,128)S(1)}, u32[]{:S(2)}, u32[]{:S(2)}) collective-permute-start(f32[16,64,128]{2,1,0:T(8,128)} %get-tuple-element.47.low_ref), channel_id=1, source_target_pairs={{0,1},{1,0},{2,3},{3,2},{4,5},{5,4},{6,7},{7,6},{8,9},{9,8},{10,11... | collective-permute-start | bytes 1572872 | tf_op jit(solution)/shard_map/ppermute | solution.py:487
  7.7 18.4 %collective-permute-start.1 = (f32[16,64,128]{2,1,0:T(8,128)}, f32[16,64,128]{2,1,0:T(8,128)S(1)}, u32[]{:S(2)}, u32[]{:S(2)}) collective-permute-start(f32[16,64,128]{2,1,0:T(8,128)} %get-tuple-element.48.high_ref), channel_id=1, source_target_pairs={{1,2},{2,1},{3,4},{4,3},{5,6},{6,5},{7,8},{8,7},{9,10},{10,9},{11,... | collective-permute-start | bytes 1572872 | tf_op jit(solution)/shard_map/ppermute | solution.py:487
  14.6 13.0 %all-to-all-start.1 = ((f32[32,1,128]{2,1,0:T(1,128)}), f32[32,1,128]{2,1,0:T(1,128)S(1)}, u32[]{:S(2)}, u32[]{:S(2)}) async-start(f32[32,1,128]{2,1,0:T(1,128)} %get-tuple-element.56), calls=%async_computation.1 | async-start | bytes 32768 | tf_op jit(solution)/shard_map/all_to_all | solution.py:518
  18.4 7.7 %copy-start.9 = (f32[32,64,128]{2,1,0:T(8,128)S(1)}, f32[32,64,128]{2,1,0:T(8,128)}, u32[]{:S(2)}) copy-start(f32[32,64,128]{2,1,0:T(8,128)} %get-tuple-element.46.keep_ref) | copy-start | bytes 3145732
  18.4 7.7 %copy-start.13 = (f32[32,256]{1,0:T(8,128)S(1)}, f32[32,256]{1,0:T(8,128)}, u32[]{:S(2)}) copy-start(f32[32,256]{1,0:T(8,128)} %get-tuple-element.51.refs_5_.cum_ref) | copy-start | bytes 98308
  27.5 67.8 %copy-start.14 = (bf16[1,256,128]{2,1,0:T(8,128)(2,1)S(1)}, bf16[1,256,128]{2,1,0:T(8,128)(2,1)}, u32[]{:S(2)}) copy-start(bf16[1,256,128]{2,1,0:T(8,128)(2,1)} %param.8) | copy-start | bytes 196612
  27.6 67.8 %copy-start.15 = (bf16[1,256,128]{2,1,0:T(8,128)(2,1)S(1)}, bf16[1,256,128]{2,1,0:T(8,128)(2,1)}, u32[]{:S(2)}) copy-start(bf16[1,256,128]{2,1,0:T(8,128)(2,1)} %param.9) | copy-start | bytes 196612
  58.5 29.0 %copy-start.11 = (f32[16,64,128]{2,1,0:T(8,128)S(1)}, f32[16,64,128]{2,1,0:T(8,128)}, u32[]{:S(2)}) copy-start(f32[16,64,128]{2,1,0:T(8,128)} %get-tuple-element.47.low_ref) | copy-start | bytes 1572868
  58.5 29.0 %copy-start.12 = (f32[16,64,128]{2,1,0:T(8,128)S(1)}, f32[16,64,128]{2,1,0:T(8,128)}, u32[]{:S(2)}) copy-start(f32[16,64,128]{2,1,0:T(8,128)} %get-tuple-element.48.high_ref) | copy-start | bytes 1572868
  58.5 36.8 %copy-start.10 = (bf16[1,256,2048]{2,1,0:T(8,128)(2,1)S(1)}, bf16[1,256,2048]{2,1,0:T(8,128)(2,1)}, u32[]{:S(2)}) copy-start(bf16[1,256,2048]{2,1,0:T(8,128)(2,1)} %param.13) | copy-start | bytes 3145732
  58.6 36.7 %copy-start.5 = (bf16[2048,256]{1,0:T(8,128)(2,1)S(1)}, bf16[2048,256]{1,0:T(8,128)(2,1)}, u32[]{:S(2)}) copy-start(bf16[2048,256]{1,0:T(8,128)(2,1)} %get-tuple-element.59.refs_7_) | copy-start | bytes 3145732
  58.6 36.7 %copy-start.7 = (bf16[2048,256]{1,0:T(8,128)(2,1)S(1)}, bf16[2048,256]{1,0:T(8,128)(2,1)}, u32[]{:S(2)}) copy-start(bf16[2048,256]{1,0:T(8,128)(2,1)} %get-tuple-element.60.refs_8_) | copy-start | bytes 3145732
  87.5 12.3 %copy-start = (f32[32,64,128]{2,1,0:T(8,128)}, f32[32,64,128]{2,1,0:T(8,128)S(1)}, u32[]{:S(2)}) copy-start(f32[32,64,128]{2,1,0:T(8,128)S(1)} %all_to_all.21.mine_ref) | copy-start | bytes 3145732
  87.5 7.8 %copy-start.3 = (bf16[2048,256]{1,0:T(8,128)(2,1)S(1)}, bf16[2048,256]{1,0:T(8,128)(2,1)}, u32[]{:S(2)}) copy-start(bf16[2048,256]{1,0:T(8,128)(2,1)} %get-tuple-element.49.refs_1_.xt_ref) | copy-start | bytes 3145732
  87.5 7.8 %copy-start.4 = (bf16[2048,256]{1,0:T(8,128)(2,1)S(1)}, bf16[2048,256]{1,0:T(8,128)(2,1)}, u32[]{:S(2)}) copy-start(bf16[2048,256]{1,0:T(8,128)(2,1)} %get-tuple-element.50.refs_2_.gt_ref) | copy-start | bytes 3145732
  87.8 7.6 %copy-start.21 = (f32[32]{0:T(128)S(1)}, f32[32]{0:T(128)}, u32[]{:S(2)}) copy-start(f32[32]{0:T(128)} %refs_6_.3) | copy-start | bytes 388
  87.8 16.2 %collective-permute-start.2 = (f32[16,64,128]{2,1,0:T(8,128)S(1)}, f32[16,64,128]{2,1,0:T(8,128)S(1)}, u32[]{:S(2)}, u32[]{:S(2)}) collective-permute-start(f32[16,64,128]{2,1,0:T(8,128)S(1)} %get-tuple-element.57), channel_id=1, source_target_pairs={{0,1},{1,0},{2,3},{3,2},{4,5},{5,4},{6,7},{7,6},{8,9},{9,8},{10,11... | collective-permute-start | bytes 1572872 | tf_op jit(solution)/shard_map/ppermute | solution.py:487
  92.0 7.8 %copy-start.22 = (f32[16,256]{1,0:T(8,128)S(1)}, f32[16,256]{1,0:T(8,128)}, u32[]{:S(2)}) copy-start(f32[16,256]{1,0:T(8,128)} %get-tuple-element.63.low_row_ref) | copy-start | bytes 49156
  92.0 7.8 %copy-start.23 = (f32[16,256]{1,0:T(8,128)S(1)}, f32[16,256]{1,0:T(8,128)}, u32[]{:S(2)}) copy-start(f32[16,256]{1,0:T(8,128)} %get-tuple-element.65.low_skiprow_ref) | copy-start | bytes 49156
  92.0 11.9 %collective-permute-start.3 = (f32[16,64,128]{2,1,0:T(8,128)S(1)}, f32[16,64,128]{2,1,0:T(8,128)S(1)}, u32[]{:S(2)}, u32[]{:S(2)}) collective-permute-start(f32[16,64,128]{2,1,0:T(8,128)S(1)} %get-tuple-element.58), channel_id=1, source_target_pairs={{1,2},{2,1},{3,4},{4,3},{5,6},{6,5},{7,8},{8,7},{9,10},{10,9},{11,... | collective-permute-start | bytes 1572872 | tf_op jit(solution)/shard_map/ppermute | solution.py:487
  98.5 0.7 copy-start.16
  99.1 0.6 copy-start.17
  99.8 2.2 %copy-start.6 = (bf16[2048,256]{1,0:T(8,128)(2,1)}, bf16[2048,256]{1,0:T(8,128)(2,1)S(1)}, u32[]{:S(2)}) copy-start(bf16[2048,256]{1,0:T(8,128)(2,1)S(1)} %get-tuple-element.61.yt_ref) | copy-start | bytes 3145732
  99.8 2.2 %copy-start.8 = (bf16[2048,256]{1,0:T(8,128)(2,1)}, bf16[2048,256]{1,0:T(8,128)(2,1)S(1)}, u32[]{:S(2)}) copy-start(bf16[2048,256]{1,0:T(8,128)(2,1)S(1)} %get-tuple-element.62.gxt_ref) | copy-start | bytes 3145732
  102.0 0.7 copy-start.18
  102.7 0.7 copy-start.19
  103.3 0.6 copy-start.20
  103.9 1.0 copy-start.1
  103.9 1.0 copy-start.2
  105.0 26.0 %all-to-all-start.3 = ((f32[256,1,128]{2,1,0:T(1,128)}), f32[256,1,128]{2,1,0:T(1,128)S(1)}, u32[]{:S(2)}, u32[]{:S(2)}) async-start(f32[256,1,128]{2,1,0:T(1,128)} %sums.1), calls=%async_computation.3 | async-start | bytes 262144 | tf_op jit(solution)/shard_map/all_to_all | solution.py:547

commit v8 on v7

--- a/solution.py
+++ b/solution.py
@@ -84,7 +84,7 @@
 
 def states_kernel(
     x_hbm, g_hbm, b_hbm, c_hbm, dt_hbm, alog_hbm,
-    low_ref, high_ref, keep_ref, gain_ref, xt_ref, gt_ref, cum_ref,
+    high_ref, low_ref, keep_ref, gain_ref, xt_ref, gt_ref, cum_ref,
     x_s, g_s, b_s, c_s, dt_s, alog_s, sems,
 ):
     def copy(source, target, slot):
@@ -141,7 +141,7 @@
             gain_ref[i * STEP + j] = jnp.broadcast_to(gain[j : j + 1], (1, STATE))
 
 
-def join_kernel(keep_ref, low_ref, high_ref, cum_ref, out_ref):
+def join_kernel(keep_ref, high_ref, low_ref, cum_ref, out_ref):
     gain = jnp.exp(cum_ref[:, GROUP - 1 :])
     for h in range(HEADS):
         other = low_ref[h] if h < HALF else high_ref[h - HALF]
@@ -182,7 +182,7 @@
         out_ref[0] = adjoint
 
 
-def pass_on_kernel(mine_ref, low_ref, high_ref, cum_ref, out_low_ref, out_high_ref):
+def pass_on_kernel(mine_ref, high_ref, low_ref, cum_ref, out_high_ref, out_low_ref):
     gain = jnp.exp(cum_ref[:, GROUP - 1 :])
     low_gain = gain[:HALF] * unpaired(0)
     high_gain = gain[HALF:] * unpaired(GRID - 1)
@@ -396,7 +396,7 @@
         made.wait()
 
 
-def sums_kernel(weights_ref, low_ref, high_ref, base_ref, sums_ref):
+def sums_kernel(weights_ref, high_ref, low_ref, base_ref, sums_ref):
     product = jnp.concatenate(
         [
             jnp.sum(weights_ref[:HALF] * low_ref[...], axis=1),
@@ -419,7 +419,7 @@
 
 
 def other_kernel(
-    low_ref, high_ref, yt_ref, gxt_ref, xt_ref, gt_ref, b_ref, c_ref, cum_ref,
+    high_ref, low_ref, yt_ref, gxt_ref, xt_ref, gt_ref, b_ref, c_ref, cum_ref,
     gct_ref, gbt_ref, low_gc_ref, high_gc_ref, low_gb_ref, high_gb_ref,
     mine_ref, row_ref, alog_ref, y_in, gx_in,
     y_hbm, gx_hbm, gc_ref, gb_ref, gdt_ref,
@@ -484,7 +484,8 @@
     count = lax.axis_size("seq")
     low_pairs = [(i, i ^ 1) for i in range(count)]
     high_pairs = [(i, ((i - 1 ^ 1) + 1) % count) for i in range(1, count)] + [(0, count - 1)]
-    return lax.ppermute(low, "seq", low_pairs), lax.ppermute(high, "seq", high_pairs)
+    high = lax.ppermute(high, "seq", high_pairs)
+    return lax.ppermute(low, "seq", low_pairs), high
 
 
 def shards(x_in, b_in, c_in, dt, a_log, skip, cotangent):
@@ -498,7 +499,7 @@
     wide = shape_of((feat, GROUP), BF16)
     tall = shape_of((GROUP, feat), BF16)
     rows = shape_of((HEADS, GROUP))
-    low, high, keep, gain, xt, gt, cum = call(
+    high, low, keep, gain, xt, gt, cum = call(
         states_kernel,
         "states",
         [half, half, all_heads, shape_of((HEADS, 1, STATE)), wide, wide, rows],
@@ -517,12 +518,12 @@
     low_in, high_in = swap(low, high)
     gains = lax.all_to_all(gain, "seq", 0, 0, tiled=True)
     yt, gxt, low_row, low_skiprow, low_gb, low_gc = inner(0, g, xt, gt, b, c, cum, skip)
-    low_in, high_in, yt, gxt = lax.optimization_barrier((low_in, high_in, yt, gxt))
-    joined = call(join_kernel, "join", all_heads)(keep, low_in, high_in, cum)
+    high_in, low_in, yt, gxt = lax.optimization_barrier((high_in, low_in, yt, gxt))
+    joined = call(join_kernel, "join", all_heads)(keep, high_in, low_in, cum)
     parts = lax.all_to_all(joined, "seq", 0, 0, tiled=True)
     scanned = call(scan_kernel, "scan", all_heads)(parts, gains)
     mine = lax.all_to_all(scanned, "seq", 0, 0, tiled=True)
-    low_out, high_out = call(pass_on_kernel, "pass_on", [half, half])(mine, low, high, cum)
+    high_out, low_out = call(pass_on_kernel, "pass_on", [half, half])(mine, high, low, cum)
     low_back, high_back = swap(low_out, high_out)
     yt, gxt, high_row, high_skiprow, high_gb, high_gc = inner(
         HALF_STEPS, g, xt, gt, b, c, cum, skip, (yt, gxt)
@@ -542,7 +543,7 @@
     )(mine, yt, gxt, xt, gt, b, c, cum, low_row, high_row, low_skiprow, high_skiprow)
     everyone = lax.axis_size("dp") * lax.axis_size("seq")
     copies = call(sums_kernel, "sums", shape_of((everyone, 1, STATE)))(
-        weights, low_back, high_back, base
+        weights, high_back, low_back, base
     )
     sums = lax.all_to_all(copies, ("dp", "seq"), 0, 0, tiled=True)
     y, gx, gc, gb, gdt = call(
@@ -556,7 +557,7 @@
         cost=cost(4),
         limit=LARGE_LIMIT,
     )(
-        low_back, high_back, yt, gxt, xt, gt, b, c, cum, gct, gbt,
+        high_back, low_back, yt, gxt, xt, gt, b, c, cum, gct, gbt,
         low_gc, high_gc, low_gb, high_gb, mine, row, alog, y, gx,
     )
     galog, gskip = call(

time: 132 us -> 132 us (level)
    ppermute x4, starting transfers between devices: 16.9 us -> 13.9 us  [the longest x2 13.9 us: swap(): high = lax.ppermute(high, 'seq', high_pairs)]
  transfers between devices with their start and end apart: 6 -> 6, of which waited for: 3 -> 4; matrix products, arithmetic and copies ran while one was open for 0% -> 0% of each run, Pallas kernels for 12% -> 12%
where the time goes in v8:
time: 132 us; the launch traced here: 131 us
  blocking collectives  59.9 us (45%)
  starting transfers between devices  32.8 us (25%)
  Pallas kernels  22.8 us (17%)
  waiting for transfers between devices  11.5 us (9%)
  local copies, waits for them, and re-layouts  3.29 us (2%)
    all_to_all x1, blocking collectives, shards(): parts = lax.all_to_all(joined, 'seq', 0, 0, tiled=True)  31 us
    all_to_all x1, blocking collectives, shards(): mine = lax.all_to_all(scanned, 'seq', 0, 0, tiled=True)  28.9 us
    all_to_all x1, starting transfers between devices, shards(): sums = lax.all_to_all(copies, ('dp', 'seq'), 0, 0, tiled=True)  14.2 us
    ppermute x2, starting transfers between devices, swap(): high = lax.ppermute(high, 'seq', high_pairs)  13.9 us
    pallas_call x2, Pallas kernels, inner(): call(functools.partial(inner_kernel, offset), 'inner', [wide, wide, rows,...  7.88 us
    all_to_all x1, waiting for transfers between devices, shards(): sums = lax.all_to_all(copies, ('dp', 'seq'), 0, 0, tiled=True)  7.17 us
    pallas_call x1, Pallas kernels, shards(): call(other_kernel, 'other', [tall, tall, shape_of((GROUP, STATE), BF16),...  5.87 us
    all_to_all x1, starting transfers between devices, shards(): gains = lax.all_to_all(gain, 'seq', 0, 0, tiled=True)  4.74 us
  transfers between devices with their start and end apart: 6, of which 4 were waited for; matrix products, arithmetic and copies ran while one was open for 0% of the time, Pallas kernels for 12%

profile of v8, /device:TPU:1, one launch (start us, length us, event | category | flops | bytes accessed | tf_op | source)
XLA Modules:
  0.0 131.2 jit_solution(17370788001758716428)
XLA Ops:
  0.6 4.5 %states.1 = (f32[16,64,128]{2,1,0:T(8,128)}, f32[16,64,128]{2,1,0:T(8,128)}, f32[32,64,128]{2,1,0:T(8,128)}, f32[32,1,128]{2,1,0:T(1,128)}, bf16[2048,256]{1,0:T...) custom-call(bf16[256,2048]{1,0:T(8,128)(2,1)} %bitcast.28, bf16[256,2048]{1,0:T(8,128)(2,1)} %bitcast.13, ...), custom_call_target="tpu_custom_call" | custom-call | tf_op jit(solution)/shard_map/states/pallas_call | solution.py:502
  5.2 8.7 %collective-permute-start = (f32[16,64,128]{2,1,0:T(8,128)}, f32[16,64,128]{2,1,0:T(8,128)S(1)}, u32[]{:S(2)}, u32[]{:S(2)}) collective-permute-start(f32[16,64,128]{2,1,0:T(8,128)} %get-tuple-element.47.high_ref), channel_id=1, source_target_pairs={{1,2},{2,1},{3,4},{4,3},{5,6},{6,5},{7,8},{8,7},{9,10},{10,9},{11,... | collective-permute-start | bytes 1572872 | tf_op jit(solution)/shard_map/ppermute | solution.py:487
  13.9 0.0 collective-permute-start.1
  13.9 4.7 %all-to-all-start.1 = ((f32[32,1,128]{2,1,0:T(1,128)}), f32[32,1,128]{2,1,0:T(1,128)S(1)}, u32[]{:S(2)}, u32[]{:S(2)}) async-start(f32[32,1,128]{2,1,0:T(1,128)} %get-tuple-element.56), calls=%async_computation.1 | async-start | bytes 32768 | tf_op jit(solution)/shard_map/all_to_all | solution.py:519
  18.6 0.0 copy-start.9
  18.6 4.7 %inner.2 = (bf16[2048,256]{1,0:T(8,128)(2,1)}, bf16[2048,256]{1,0:T(8,128)(2,1)}, f32[16,256]{1,0:T(8,128)}, f32[16,256]{1,0:T(8,128)}, f32[256,128]{1,0:T(8,128)}, /*index=5*/f32[256,128]{1,0:T(8,128)}) custom-call(bf16[256,2048]{1,0:T(8,128)(2,1)} %bitcast.14, bf16[2048,256]{1,0:T(8,128)(2,1)} %get-tuple-element.49.refs_1_.xt_ref, ...), custom_call_target="tpu_custom_call" | custom-call | flops 2000000000 | bytes 8388608 | tf_op jit(solution)/shard_map/inner/pallas_call | solution.py:265
  23.4 2.3 %collective-permute-done.high_ref = f32[16,64,128]{2,1,0:T(8,128)S(1)} collective-permute-done((f32[16,64,128]{2,1,0:T(8,128)}, f32[16,64,128]{2,1,0:T(8,128)S(1)}, u32[]{:S(2)}, u32[]{:S(2)}) %collective-permute-start) | collective-permute-done | bytes 524320 | tf_op jit(solution)/shard_map/ppermute | solution.py:487
  25.7 1.0 collective-permute-done.1.low_ref
  26.7 0.2 join.1
  27.0 1.0 all-to-all-done.1.gain_ref
  27.9 31.0 %all_to_all.20.part_ref = f32[32,64,128]{2,1,0:T(8,128)S(1)} all-to-all(f32[32,64,128]{2,1,0:T(8,128)S(1)} %join.1), channel_id=1, replica_groups=mesh['dp'=8,'seq'=32] {'seq'}, dimensions={0} | all-to-all | bytes 2097152 | tf_op jit(solution)/shard_map/all_to_all | solution.py:523
  58.9 0.1 scan.1
  59.0 0.0 copy-start.5
  59.0 28.9 %all_to_all.21.mine_ref = f32[32,64,128]{2,1,0:T(8,128)S(1)} all-to-all(f32[32,64,128]{2,1,0:T(8,128)S(1)} %scan.1), channel_id=1, replica_groups=mesh['dp'=8,'seq'=32] {'seq'}, dimensions={0} | all-to-all | bytes 2097152 | tf_op jit(solution)/shard_map/all_to_all | solution.py:525
  88.0 0.2 pass_on.1
  88.2 0.0 copy-start.21
  88.2 5.3 %collective-permute-start.2 = (f32[16,64,128]{2,1,0:T(8,128)S(1)}, f32[16,64,128]{2,1,0:T(8,128)S(1)}, u32[]{:S(2)}, u32[]{:S(2)}) collective-permute-start(f32[16,64,128]{2,1,0:T(8,128)S(1)} %get-tuple-element.57), channel_id=1, source_target_pairs={{1,2},{2,1},{3,4},{4,3},{5,6},{6,5},{7,8},{8,7},{9,10},{10,9},{11,... | collective-permute-start | bytes 1572872 | tf_op jit(solution)/shard_map/ppermute | solution.py:487
  93.5 0.0 collective-permute-start.3
  93.6 3.1 %inner.3 = (bf16[2048,256]{1,0:T(8,128)(2,1)S(1)}, bf16[2048,256]{1,0:T(8,128)(2,1)S(1)}, f32[16,256]{1,0:T(8,128)S(1)}, f32[16,256]{1,0:T(8,128)S(1)}, f32[256,128]{1,0:T(8,128)S(1)}, /*index=5*/f32[256,128]{1,0:T(8,128)S(1)}) custom-call(bf16[256,2048]{1,0:T(8,128)(2,1)S(1)} %bitcast.15, ...), custom_call_target="tpu_custom_call", output_to_operand_aliasing={{0}: (7, {}), {1}: (8, {})} | custom-call | flops 2000000000 | bytes 8388608 | tf_op jit(solution)/shard_map/inner/pallas_call | solution.py:265
  96.7 0.6 copy-done.16
  97.3 0.6 copy-done.17
  98.0 2.1 %own.1 = (bf16[256,2048]{1,0:T(8,128)(2,1)}, bf16[256,2048]{1,0:T(8,128)(2,1)}, f32[32,256]{1,0:T(8,128)S(1)}, f32[128,256]{1,0:T(8,128)S(1)}, f32[128,256]{1,0:...) custom-call(f32[32,64,128]{2,1,0:T(8,128)S(1)} %all_to_all.21.mine_ref, ...), custom_call_target="tpu_custom_call" | custom-call | flops 2000000000 | bytes 8388608 | tf_op jit(solution)/shard_map/own/pallas_call | solution.py:536
  100.2 0.7 copy-done.18
  100.9 0.6 copy-done.19
  101.5 0.6 copy-done.20
  102.1 0.0 collective-permute-done.2.high_ref
  102.1 0.0 collective-permute-done.3.low_ref
  102.1 1.0 sums.1
  103.2 14.2 %all-to-all-start.3 = ((f32[256,1,128]{2,1,0:T(1,128)}), f32[256,1,128]{2,1,0:T(1,128)S(1)}, u32[]{:S(2)}, u32[]{:S(2)}) async-start(f32[256,1,128]{2,1,0:T(1,128)} %sums.1), calls=%async_computation.3 | async-start | bytes 262144 | tf_op jit(solution)/shard_map/all_to_all | solution.py:548
  117.3 5.9 %other.1 = (bf16[256,2048]{1,0:T(8,128)(2,1)}, bf16[256,2048]{1,0:T(8,128)(2,1)}, bf16[256,128]{1,0:T(8,128)(2,1)}, bf16[256,128]{1,0:T(8,128)(2,1)}, f32[32,256]{1,0:T(8,128)}) custom-call(f32[16,64,128]{2,1,0:T(8,128)} %copy-done.1, f32[16,64,128]{2,1,0:T(8,128)} %copy-done.2, ...), custom_call_target="tpu_custom_call", output_to_operand_aliasing={{0}: (18, {}), {1}: (19, {})} | custom-call | flops 2000000000 | bytes 8388608 | tf_op jit(solution)/shard_map/other/pallas_call | solution.py:549
  123.2 7.2 %all-to-all-done.3.sums_ref = f32[256,1,128]{2,1,0:T(1,128)S(1)} async-done(((f32[256,1,128]{2,1,0:T(1,128)}), f32[256,1,128]{2,1,0:T(1,128)S(1)}, u32[]{:S(2)}, u32[]{:S(2)}) %all-to-all-start.3) | async-done | bytes 131104 | tf_op jit(solution)/shard_map/all_to_all | solution.py:548
  130.4 0.8 total.1
  (40 shorter events, 0.1 us)
Async XLA Ops:
  5.2 20.5 %collective-permute-start = (f32[16,64,128]{2,1,0:T(8,128)}, f32[16,64,128]{2,1,0:T(8,128)S(1)}, u32[]{:S(2)}, u32[]{:S(2)}) collective-permute-start(f32[16,64,128]{2,1,0:T(8,128)} %get-tuple-element.47.high_ref), channel_id=1, source_target_pairs={{1,2},{2,1},{3,4},{4,3},{5,6},{6,5},{7,8},{8,7},{9,10},{10,9},{11,... | collective-permute-start | bytes 1572872 | tf_op jit(solution)/shard_map/ppermute | solution.py:487
  13.9 12.9 %collective-permute-start.1 = (f32[16,64,128]{2,1,0:T(8,128)}, f32[16,64,128]{2,1,0:T(8,128)S(1)}, u32[]{:S(2)}, u32[]{:S(2)}) collective-permute-start(f32[16,64,128]{2,1,0:T(8,128)} %get-tuple-element.48.low_ref), channel_id=1, source_target_pairs={{0,1},{1,0},{2,3},{3,2},{4,5},{5,4},{6,7},{7,6},{8,9},{9,8},{10,11... | collective-permute-start | bytes 1572872 | tf_op jit(solution)/shard_map/ppermute | solution.py:488
  13.9 14.1 %all-to-all-start.1 = ((f32[32,1,128]{2,1,0:T(1,128)}), f32[32,1,128]{2,1,0:T(1,128)S(1)}, u32[]{:S(2)}, u32[]{:S(2)}) async-start(f32[32,1,128]{2,1,0:T(1,128)} %get-tuple-element.56), calls=%async_computation.1 | async-start | bytes 32768 | tf_op jit(solution)/shard_map/all_to_all | solution.py:519
  18.6 8.1 %copy-start.9 = (f32[32,64,128]{2,1,0:T(8,128)S(1)}, f32[32,64,128]{2,1,0:T(8,128)}, u32[]{:S(2)}) copy-start(f32[32,64,128]{2,1,0:T(8,128)} %get-tuple-element.46.keep_ref) | copy-start | bytes 3145732
  18.6 8.1 %copy-start.13 = (f32[32,256]{1,0:T(8,128)S(1)}, f32[32,256]{1,0:T(8,128)}, u32[]{:S(2)}) copy-start(f32[32,256]{1,0:T(8,128)} %get-tuple-element.51.refs_5_.cum_ref) | copy-start | bytes 98308
  27.9 65.6 %copy-start.14 = (bf16[1,256,128]{2,1,0:T(8,128)(2,1)S(1)}, bf16[1,256,128]{2,1,0:T(8,128)(2,1)}, u32[]{:S(2)}) copy-start(bf16[1,256,128]{2,1,0:T(8,128)(2,1)} %param.8) | copy-start | bytes 196612
  27.9 65.6 %copy-start.15 = (bf16[1,256,128]{2,1,0:T(8,128)(2,1)S(1)}, bf16[1,256,128]{2,1,0:T(8,128)(2,1)}, u32[]{:S(2)}) copy-start(bf16[1,256,128]{2,1,0:T(8,128)(2,1)} %param.9) | copy-start | bytes 196612
  58.9 29.0 %copy-start.11 = (f32[16,64,128]{2,1,0:T(8,128)S(1)}, f32[16,64,128]{2,1,0:T(8,128)}, u32[]{:S(2)}) copy-start(f32[16,64,128]{2,1,0:T(8,128)} %get-tuple-element.47.high_ref) | copy-start | bytes 1572868
  58.9 29.0 %copy-start.12 = (f32[16,64,128]{2,1,0:T(8,128)S(1)}, f32[16,64,128]{2,1,0:T(8,128)}, u32[]{:S(2)}) copy-start(f32[16,64,128]{2,1,0:T(8,128)} %get-tuple-element.48.low_ref) | copy-start | bytes 1572868
  58.9 34.6 %copy-start.10 = (bf16[1,256,2048]{2,1,0:T(8,128)(2,1)S(1)}, bf16[1,256,2048]{2,1,0:T(8,128)(2,1)}, u32[]{:S(2)}) copy-start(bf16[1,256,2048]{2,1,0:T(8,128)(2,1)} %param.13) | copy-start | bytes 3145732
  59.0 34.5 %copy-start.5 = (bf16[2048,256]{1,0:T(8,128)(2,1)S(1)}, bf16[2048,256]{1,0:T(8,128)(2,1)}, u32[]{:S(2)}) copy-start(bf16[2048,256]{1,0:T(8,128)(2,1)} %get-tuple-element.59.refs_7_) | copy-start | bytes 3145732
  59.0 34.5 %copy-start.7 = (bf16[2048,256]{1,0:T(8,128)(2,1)S(1)}, bf16[2048,256]{1,0:T(8,128)(2,1)}, u32[]{:S(2)}) copy-start(bf16[2048,256]{1,0:T(8,128)(2,1)} %get-tuple-element.60.refs_8_) | copy-start | bytes 3145732
  88.0 10.0 %copy-start = (f32[32,64,128]{2,1,0:T(8,128)}, f32[32,64,128]{2,1,0:T(8,128)S(1)}, u32[]{:S(2)}) copy-start(f32[32,64,128]{2,1,0:T(8,128)S(1)} %all_to_all.21.mine_ref) | copy-start | bytes 3145732
  88.0 5.6 %copy-start.3 = (bf16[2048,256]{1,0:T(8,128)(2,1)S(1)}, bf16[2048,256]{1,0:T(8,128)(2,1)}, u32[]{:S(2)}) copy-start(bf16[2048,256]{1,0:T(8,128)(2,1)} %get-tuple-element.49.refs_1_.xt_ref) | copy-start | bytes 3145732
  88.0 5.6 %copy-start.4 = (bf16[2048,256]{1,0:T(8,128)(2,1)S(1)}, bf16[2048,256]{1,0:T(8,128)(2,1)}, u32[]{:S(2)}) copy-start(bf16[2048,256]{1,0:T(8,128)(2,1)} %get-tuple-element.50.refs_2_.gt_ref) | copy-start | bytes 3145732
  88.2 5.3 %copy-start.21 = (f32[32]{0:T(128)S(1)}, f32[32]{0:T(128)}, u32[]{:S(2)}) copy-start(f32[32]{0:T(128)} %refs_6_.3) | copy-start | bytes 388
  88.2 13.9 %collective-permute-start.2 = (f32[16,64,128]{2,1,0:T(8,128)S(1)}, f32[16,64,128]{2,1,0:T(8,128)S(1)}, u32[]{:S(2)}, u32[]{:S(2)}) collective-permute-start(f32[16,64,128]{2,1,0:T(8,128)S(1)} %get-tuple-element.57), channel_id=1, source_target_pairs={{1,2},{2,1},{3,4},{4,3},{5,6},{6,5},{7,8},{8,7},{9,10},{10,9},{11,... | collective-permute-start | bytes 1572872 | tf_op jit(solution)/shard_map/ppermute | solution.py:487
  93.5 4.5 %copy-start.22 = (f32[16,256]{1,0:T(8,128)S(1)}, f32[16,256]{1,0:T(8,128)}, u32[]{:S(2)}) copy-start(f32[16,256]{1,0:T(8,128)} %get-tuple-element.63.low_row_ref) | copy-start | bytes 49156
  93.5 4.5 %copy-start.23 = (f32[16,256]{1,0:T(8,128)S(1)}, f32[16,256]{1,0:T(8,128)}, u32[]{:S(2)}) copy-start(f32[16,256]{1,0:T(8,128)} %get-tuple-element.65.low_skiprow_ref) | copy-start | bytes 49156
  93.5 8.7 %collective-permute-start.3 = (f32[16,64,128]{2,1,0:T(8,128)S(1)}, f32[16,64,128]{2,1,0:T(8,128)S(1)}, u32[]{:S(2)}, u32[]{:S(2)}) collective-permute-start(f32[16,64,128]{2,1,0:T(8,128)S(1)} %get-tuple-element.58), channel_id=1, source_target_pairs={{0,1},{1,0},{2,3},{3,2},{4,5},{5,4},{6,7},{7,6},{8,9},{9,8},{10,11... | collective-permute-start | bytes 1572872 | tf_op jit(solution)/shard_map/ppermute | solution.py:488
  96.7 0.7 copy-start.16
  97.3 0.6 copy-start.17
  98.0 2.2 %copy-start.6 = (bf16[2048,256]{1,0:T(8,128)(2,1)}, bf16[2048,256]{1,0:T(8,128)(2,1)S(1)}, u32[]{:S(2)}) copy-start(bf16[2048,256]{1,0:T(8,128)(2,1)S(1)} %get-tuple-element.61.yt_ref) | copy-start | bytes 3145732
  98.0 2.2 %copy-start.8 = (bf16[2048,256]{1,0:T(8,128)(2,1)}, bf16[2048,256]{1,0:T(8,128)(2,1)S(1)}, u32[]{:S(2)}) copy-start(bf16[2048,256]{1,0:T(8,128)(2,1)S(1)} %get-tuple-element.62.gxt_ref) | copy-start | bytes 3145732
  100.2 0.7 copy-start.18
  100.9 0.7 copy-start.19
  101.5 0.6 copy-start.20
  102.1 1.0 copy-start.1
  102.1 1.0 copy-start.2
  103.2 27.2 %all-to-all-start.3 = ((f32[256,1,128]{2,1,0:T(1,128)}), f32[256,1,128]{2,1,0:T(1,128)S(1)}, u32[]{:S(2)}, u32[]{:S(2)}) async-start(f32[256,1,128]{2,1,0:T(1,128)} %sums.1), calls=%async_computation.3 | async-start | bytes 262144 | tf_op jit(solution)/shard_map/all_to_all | solution.py:548

commit v9 on v8

--- a/solution.py
+++ b/solution.py
@@ -555,7 +555,7 @@
         input_output_aliases={18: 0, 19: 1},
         scratch_shapes=[out_scratch[0], pltpu.VMEM((HEADS, GROUP), F32), out_scratch[1]],
         cost=cost(4),
-        limit=LARGE_LIMIT,
+        limit=52 * 1024 * 1024,
     )(
         high_back, low_back, yt, gxt, xt, gt, b, c, cum, gct, gbt,
         low_gc, high_gc, low_gb, high_gb, mine, row, alog, y, gx,

time: 132 us -> 131 us (level)
    unnamed x48 -> x54, local copies, waits for them, and re-layouts: 3.29 us -> 2.63 us
  transfers between devices with their start and end apart: 6 -> 6, of which waited for: 4 -> 5; matrix products, arithmetic and copies ran while one was open for 0% -> 0% of each run, Pallas kernels for 12% -> 12%
where the time goes in v9:
time: 131 us
  blocking collectives  59.9 us (46%)
  starting transfers between devices  33.3 us (25%)
  Pallas kernels  22.4 us (17%)
  waiting for transfers between devices  11.8 us (9%)
  local copies, waits for them, and re-layouts  2.63 us (2%)
    all_to_all x1, blocking collectives, shards(): parts = lax.all_to_all(joined, 'seq', 0, 0, tiled=True)  31 us
    all_to_all x1, blocking collectives, shards(): mine = lax.all_to_all(scanned, 'seq', 0, 0, tiled=True)  28.9 us
    all_to_all x1, starting transfers between devices, shards(): sums = lax.all_to_all(copies, ('dp', 'seq'), 0, 0, tiled=True)  14.6 us
    ppermute x2, starting transfers between devices, swap(): high = lax.ppermute(high, 'seq', high_pairs)  13.9 us
    pallas_call x2, Pallas kernels, inner(): call(functools.partial(inner_kernel, offset), 'inner', [wide, wide, rows,...  7.89 us
    all_to_all x1, waiting for transfers between devices, shards(): sums = lax.all_to_all(copies, ('dp', 'seq'), 0, 0, tiled=True)  6.9 us
    pallas_call x1, Pallas kernels, shards(): call(other_kernel, 'other', [tall, tall, shape_of((GROUP, STATE), BF16),...  5.48 us
    all_to_all x1, starting transfers between devices, shards(): gains = lax.all_to_all(gain, 'seq', 0, 0, tiled=True)  4.74 us
  transfers between devices with their start and end apart: 6, of which 5 were waited for; matrix products, arithmetic and copies ran while one was open for 0% of the time, Pallas kernels for 12%

profile of v9, /device:TPU:1, one launch (start us, length us, event | category | flops | bytes accessed | tf_op | source)
XLA Modules:
  0.0 131.0 jit_solution(10101789615659007536)
XLA Ops:
  0.6 4.5 %states.1 = (f32[16,64,128]{2,1,0:T(8,128)}, f32[16,64,128]{2,1,0:T(8,128)}, f32[32,64,128]{2,1,0:T(8,128)}, f32[32,1,128]{2,1,0:T(1,128)}, bf16[2048,256]{1,0:T...) custom-call(bf16[256,2048]{1,0:T(8,128)(2,1)} %bitcast.30, bf16[256,2048]{1,0:T(8,128)(2,1)} %bitcast.13, ...), custom_call_target="tpu_custom_call" | custom-call | tf_op jit(solution)/shard_map/states/pallas_call | solution.py:502
  5.2 8.7 %collective-permute-start = (f32[16,64,128]{2,1,0:T(8,128)}, f32[16,64,128]{2,1,0:T(8,128)S(1)}, u32[]{:S(2)}, u32[]{:S(2)}) collective-permute-start(f32[16,64,128]{2,1,0:T(8,128)} %get-tuple-element.47.high_ref), channel_id=1, source_target_pairs={{1,2},{2,1},{3,4},{4,3},{5,6},{6,5},{7,8},{8,7},{9,10},{10,9},{11,... | collective-permute-start | bytes 1572872 | tf_op jit(solution)/shard_map/ppermute | solution.py:487
  13.8 0.0 collective-permute-start.1
  13.8 4.7 %all-to-all-start.1 = ((f32[32,1,128]{2,1,0:T(1,128)}), f32[32,1,128]{2,1,0:T(1,128)S(1)}, u32[]{:S(2)}, u32[]{:S(2)}) async-start(f32[32,1,128]{2,1,0:T(1,128)} %get-tuple-element.56), calls=%async_computation.1 | async-start | bytes 32768 | tf_op jit(solution)/shard_map/all_to_all | solution.py:519
  18.6 0.0 copy-start.8
  18.6 0.0 copy-start.12
  18.6 4.8 %inner.2 = (bf16[2048,256]{1,0:T(8,128)(2,1)}, bf16[2048,256]{1,0:T(8,128)(2,1)}, f32[16,256]{1,0:T(8,128)}, f32[16,256]{1,0:T(8,128)}, f32[256,128]{1,0:T(8,128)}, /*index=5*/f32[256,128]{1,0:T(8,128)}) custom-call(bf16[256,2048]{1,0:T(8,128)(2,1)} %bitcast.14, bf16[2048,256]{1,0:T(8,128)(2,1)} %get-tuple-element.49.refs_1_.xt_ref, ...), custom_call_target="tpu_custom_call" | custom-call | flops 2000000000 | bytes 8388608 | tf_op jit(solution)/shard_map/inner/pallas_call | solution.py:265
  23.4 2.3 %collective-permute-done.high_ref = f32[16,64,128]{2,1,0:T(8,128)S(1)} collective-permute-done((f32[16,64,128]{2,1,0:T(8,128)}, f32[16,64,128]{2,1,0:T(8,128)S(1)}, u32[]{:S(2)}, u32[]{:S(2)}) %collective-permute-start) | collective-permute-done | bytes 524320 | tf_op jit(solution)/shard_map/ppermute | solution.py:487
  25.7 1.0 collective-permute-done.1.low_ref
  26.7 0.2 join.1
  26.9 1.0 all-to-all-done.1.gain_ref
  27.9 31.0 %all_to_all.20.part_ref = f32[32,64,128]{2,1,0:T(8,128)S(1)} all-to-all(f32[32,64,128]{2,1,0:T(8,128)S(1)} %join.1), channel_id=1, replica_groups=mesh['dp'=8,'seq'=32] {'seq'}, dimensions={0} | all-to-all | bytes 2097152 | tf_op jit(solution)/shard_map/all_to_all | solution.py:523
  58.9 0.1 scan.1
  59.0 0.0 copy-start.4
  59.0 28.9 %all_to_all.21.mine_ref = f32[32,64,128]{2,1,0:T(8,128)S(1)} all-to-all(f32[32,64,128]{2,1,0:T(8,128)S(1)} %scan.1), channel_id=1, replica_groups=mesh['dp'=8,'seq'=32] {'seq'}, dimensions={0} | all-to-all | bytes 2097152 | tf_op jit(solution)/shard_map/all_to_all | solution.py:525
  87.9 0.2 pass_on.1
  88.2 0.0 copy-start.24
  88.2 5.3 %collective-permute-start.2 = (f32[16,64,128]{2,1,0:T(8,128)S(1)}, f32[16,64,128]{2,1,0:T(8,128)S(1)}, u32[]{:S(2)}, u32[]{:S(2)}) collective-permute-start(f32[16,64,128]{2,1,0:T(8,128)S(1)} %get-tuple-element.57), channel_id=1, source_target_pairs={{1,2},{2,1},{3,4},{4,3},{5,6},{6,5},{7,8},{8,7},{9,10},{10,9},{11,... | collective-permute-start | bytes 1572872 | tf_op jit(solution)/shard_map/ppermute | solution.py:487
  93.4 0.0 collective-permute-start.3
  93.5 3.1 %inner.3 = (bf16[2048,256]{1,0:T(8,128)(2,1)S(1)}, bf16[2048,256]{1,0:T(8,128)(2,1)S(1)}, f32[16,256]{1,0:T(8,128)S(1)}, f32[16,256]{1,0:T(8,128)S(1)}, f32[256,128]{1,0:T(8,128)S(1)}, /*index=5*/f32[256,128]{1,0:T(8,128)S(1)}) custom-call(bf16[256,2048]{1,0:T(8,128)(2,1)S(1)} %bitcast.15, ...), custom_call_target="tpu_custom_call", output_to_operand_aliasing={{0}: (7, {}), {1}: (8, {})} | custom-call | flops 2000000000 | bytes 8388608 | tf_op jit(solution)/shard_map/inner/pallas_call | solution.py:265
  96.7 0.6 copy-done.17
  97.3 2.1 %own.1 = (bf16[256,2048]{1,0:T(8,128)(2,1)}, bf16[256,2048]{1,0:T(8,128)(2,1)}, f32[32,256]{1,0:T(8,128)S(1)}, f32[128,256]{1,0:T(8,128)S(1)}, f32[128,256]{1,0:...) custom-call(f32[32,64,128]{2,1,0:T(8,128)S(1)} %all_to_all.21.mine_ref, ...), custom_call_target="tpu_custom_call" | custom-call | flops 2000000000 | bytes 8388608 | tf_op jit(solution)/shard_map/own/pallas_call | solution.py:536
  99.5 0.6 copy-done.19
  100.2 0.6 copy-done.21
  100.8 0.7 collective-permute-done.3.low_ref
  101.5 1.0 sums.1
  102.5 14.6 %all-to-all-start.3 = ((f32[256,1,128]{2,1,0:T(1,128)}), f32[256,1,128]{2,1,0:T(1,128)S(1)}, u32[]{:S(2)}, u32[]{:S(2)}) async-start(f32[256,1,128]{2,1,0:T(1,128)} %sums.1), calls=%async_computation.3 | async-start | bytes 262144 | tf_op jit(solution)/shard_map/all_to_all | solution.py:548
  117.1 0.0 copy-start.23
  117.2 0.6 copy-done.23
  117.8 5.5 %other.1 = (bf16[256,2048]{1,0:T(8,128)(2,1)}, bf16[256,2048]{1,0:T(8,128)(2,1)}, bf16[256,128]{1,0:T(8,128)(2,1)}, bf16[256,128]{1,0:T(8,128)(2,1)}, f32[32,256]{1,0:T(8,128)}) custom-call(f32[16,64,128]{2,1,0:T(8,128)S(1)} %collective-permute-done.2.high_ref, f32[16,64,128]{2,1,0:T(8,128)} %copy-done.1, ...), custom_call_target="tpu_custom_call", output_to_operand_aliasing={{0}: (18, {}), {1}: (19, {})} | custom-call | flops 2000000000 | bytes 8388608 | tf_op jit(solution)/shard_map/other/pallas_call | solution.py:549
  123.2 6.9 %all-to-all-done.3.sums_ref = f32[256,1,128]{2,1,0:T(1,128)S(1)} async-done(((f32[256,1,128]{2,1,0:T(1,128)}), f32[256,1,128]{2,1,0:T(1,128)S(1)}, u32[]{:S(2)}, u32[]{:S(2)}) %all-to-all-start.3) | async-done | bytes 131104 | tf_op jit(solution)/shard_map/all_to_all | solution.py:548
  130.1 0.8 total.1
  (46 shorter events, 0.1 us)
Async XLA Ops:
  5.2 20.5 %collective-permute-start = (f32[16,64,128]{2,1,0:T(8,128)}, f32[16,64,128]{2,1,0:T(8,128)S(1)}, u32[]{:S(2)}, u32[]{:S(2)}) collective-permute-start(f32[16,64,128]{2,1,0:T(8,128)} %get-tuple-element.47.high_ref), channel_id=1, source_target_pairs={{1,2},{2,1},{3,4},{4,3},{5,6},{6,5},{7,8},{8,7},{9,10},{10,9},{11,... | collective-permute-start | bytes 1572872 | tf_op jit(solution)/shard_map/ppermute | solution.py:487
  13.8 12.8 %collective-permute-start.1 = (f32[16,64,128]{2,1,0:T(8,128)}, f32[16,64,128]{2,1,0:T(8,128)S(1)}, u32[]{:S(2)}, u32[]{:S(2)}) collective-permute-start(f32[16,64,128]{2,1,0:T(8,128)} %get-tuple-element.48.low_ref), channel_id=1, source_target_pairs={{0,1},{1,0},{2,3},{3,2},{4,5},{5,4},{6,7},{7,6},{8,9},{9,8},{10,11... | collective-permute-start | bytes 1572872 | tf_op jit(solution)/shard_map/ppermute | solution.py:488
  13.8 14.1 %all-to-all-start.1 = ((f32[32,1,128]{2,1,0:T(1,128)}), f32[32,1,128]{2,1,0:T(1,128)S(1)}, u32[]{:S(2)}, u32[]{:S(2)}) async-start(f32[32,1,128]{2,1,0:T(1,128)} %get-tuple-element.56), calls=%async_computation.1 | async-start | bytes 32768 | tf_op jit(solution)/shard_map/all_to_all | solution.py:519
  18.6 8.1 %copy-start.8 = (f32[32,64,128]{2,1,0:T(8,128)S(1)}, f32[32,64,128]{2,1,0:T(8,128)}, u32[]{:S(2)}) copy-start(f32[32,64,128]{2,1,0:T(8,128)} %get-tuple-element.46.keep_ref) | copy-start | bytes 3145732
  18.6 8.1 %copy-start.12 = (f32[32,256]{1,0:T(8,128)S(1)}, f32[32,256]{1,0:T(8,128)}, u32[]{:S(2)}) copy-start(f32[32,256]{1,0:T(8,128)} %get-tuple-element.51.refs_5_.cum_ref) | copy-start | bytes 98308
  27.9 65.6 %copy-start.13 = (bf16[1,256,128]{2,1,0:T(8,128)(2,1)S(1)}, bf16[1,256,128]{2,1,0:T(8,128)(2,1)}, u32[]{:S(2)}) copy-start(bf16[1,256,128]{2,1,0:T(8,128)(2,1)} %param.8) | copy-start | bytes 196612
  27.9 65.6 %copy-start.14 = (bf16[1,256,128]{2,1,0:T(8,128)(2,1)S(1)}, bf16[1,256,128]{2,1,0:T(8,128)(2,1)}, u32[]{:S(2)}) copy-start(bf16[1,256,128]{2,1,0:T(8,128)(2,1)} %param.9) | copy-start | bytes 196612
  58.9 29.0 %copy-start.10 = (f32[16,64,128]{2,1,0:T(8,128)S(1)}, f32[16,64,128]{2,1,0:T(8,128)}, u32[]{:S(2)}) copy-start(f32[16,64,128]{2,1,0:T(8,128)} %get-tuple-element.47.high_ref) | copy-start | bytes 1572868
  58.9 29.0 %copy-start.11 = (f32[16,64,128]{2,1,0:T(8,128)S(1)}, f32[16,64,128]{2,1,0:T(8,128)}, u32[]{:S(2)}) copy-start(f32[16,64,128]{2,1,0:T(8,128)} %get-tuple-element.48.low_ref) | copy-start | bytes 1572868
  58.9 34.6 %copy-start.9 = (bf16[1,256,2048]{2,1,0:T(8,128)(2,1)S(1)}, bf16[1,256,2048]{2,1,0:T(8,128)(2,1)}, u32[]{:S(2)}) copy-start(bf16[1,256,2048]{2,1,0:T(8,128)(2,1)} %param.13) | copy-start | bytes 3145732
  59.0 34.5 %copy-start.4 = (bf16[2048,256]{1,0:T(8,128)(2,1)S(1)}, bf16[2048,256]{1,0:T(8,128)(2,1)}, u32[]{:S(2)}) copy-start(bf16[2048,256]{1,0:T(8,128)(2,1)} %get-tuple-element.59.refs_7_) | copy-start | bytes 3145732
  59.0 34.5 %copy-start.6 = (bf16[2048,256]{1,0:T(8,128)(2,1)S(1)}, bf16[2048,256]{1,0:T(8,128)(2,1)}, u32[]{:S(2)}) copy-start(bf16[2048,256]{1,0:T(8,128)(2,1)} %get-tuple-element.60.refs_8_) | copy-start | bytes 3145732
  87.9 9.4 %copy-start = (f32[32,64,128]{2,1,0:T(8,128)}, f32[32,64,128]{2,1,0:T(8,128)S(1)}, u32[]{:S(2)}) copy-start(f32[32,64,128]{2,1,0:T(8,128)S(1)} %all_to_all.21.mine_ref) | copy-start | bytes 3145732
  87.9 5.6 %copy-start.2 = (bf16[2048,256]{1,0:T(8,128)(2,1)S(1)}, bf16[2048,256]{1,0:T(8,128)(2,1)}, u32[]{:S(2)}) copy-start(bf16[2048,256]{1,0:T(8,128)(2,1)} %get-tuple-element.49.refs_1_.xt_ref) | copy-start | bytes 3145732
  87.9 5.6 %copy-start.3 = (bf16[2048,256]{1,0:T(8,128)(2,1)S(1)}, bf16[2048,256]{1,0:T(8,128)(2,1)}, u32[]{:S(2)}) copy-start(bf16[2048,256]{1,0:T(8,128)(2,1)} %get-tuple-element.50.refs_2_.gt_ref) | copy-start | bytes 3145732
  88.2 5.3 %copy-start.24 = (f32[32]{0:T(128)S(1)}, f32[32]{0:T(128)}, u32[]{:S(2)}) copy-start(f32[32]{0:T(128)} %refs_6_.3) | copy-start | bytes 388
  88.2 12.6 %collective-permute-start.2 = (f32[16,64,128]{2,1,0:T(8,128)S(1)}, f32[16,64,128]{2,1,0:T(8,128)S(1)}, u32[]{:S(2)}, u32[]{:S(2)}) collective-permute-start(f32[16,64,128]{2,1,0:T(8,128)S(1)} %get-tuple-element.57), channel_id=1, source_target_pairs={{1,2},{2,1},{3,4},{4,3},{5,6},{6,5},{7,8},{8,7},{9,10},{10,9},{11,... | collective-permute-start | bytes 1572872 | tf_op jit(solution)/shard_map/ppermute | solution.py:487
  93.4 3.9 %copy-start.25 = (f32[16,256]{1,0:T(8,128)S(1)}, f32[16,256]{1,0:T(8,128)}, u32[]{:S(2)}) copy-start(f32[16,256]{1,0:T(8,128)} %get-tuple-element.63.low_row_ref) | copy-start | bytes 49156
  93.4 3.9 %copy-start.26 = (f32[16,256]{1,0:T(8,128)S(1)}, f32[16,256]{1,0:T(8,128)}, u32[]{:S(2)}) copy-start(f32[16,256]{1,0:T(8,128)} %get-tuple-element.65.low_skiprow_ref) | copy-start | bytes 49156
  93.4 8.0 %collective-permute-start.3 = (f32[16,64,128]{2,1,0:T(8,128)S(1)}, f32[16,64,128]{2,1,0:T(8,128)S(1)}, u32[]{:S(2)}, u32[]{:S(2)}) collective-permute-start(f32[16,64,128]{2,1,0:T(8,128)S(1)} %get-tuple-element.58), channel_id=1, source_target_pairs={{0,1},{1,0},{2,3},{3,2},{4,5},{5,4},{6,7},{7,6},{8,9},{9,8},{10,11... | collective-permute-start | bytes 1572872 | tf_op jit(solution)/shard_map/ppermute | solution.py:488
  97.3 2.2 %copy-start.5 = (bf16[2048,256]{1,0:T(8,128)(2,1)}, bf16[2048,256]{1,0:T(8,128)(2,1)S(1)}, u32[]{:S(2)}) copy-start(bf16[2048,256]{1,0:T(8,128)(2,1)S(1)} %get-tuple-element.61.yt_ref) | copy-start | bytes 3145732
  97.3 2.2 %copy-start.7 = (bf16[2048,256]{1,0:T(8,128)(2,1)}, bf16[2048,256]{1,0:T(8,128)(2,1)S(1)}, u32[]{:S(2)}) copy-start(bf16[2048,256]{1,0:T(8,128)(2,1)S(1)} %get-tuple-element.62.gxt_ref) | copy-start | bytes 3145732
  99.5 0.7 copy-start.19
  100.2 0.6 copy-start.21
  101.5 1.0 copy-start.1
  101.5 15.6 %copy-start.18 = (f32[256,128]{1,0:T(8,128)S(1)}, f32[256,128]{1,0:T(8,128)}, u32[]{:S(2)}) copy-start(f32[256,128]{1,0:T(8,128)} %copy-done.17) | copy-start | bytes 393220
  101.5 15.6 %copy-start.20 = (f32[128,256]{1,0:T(8,128)S(1)}, f32[128,256]{1,0:T(8,128)}, u32[]{:S(2)}) copy-start(f32[128,256]{1,0:T(8,128)} %copy-done.19) | copy-start | bytes 393220
  101.5 15.6 %copy-start.22 = (f32[128,256]{1,0:T(8,128)S(1)}, f32[128,256]{1,0:T(8,128)}, u32[]{:S(2)}) copy-start(f32[128,256]{1,0:T(8,128)} %copy-done.21) | copy-start | bytes 393220
  102.5 14.6 %copy-start.15 = (f32[256,128]{1,0:T(8,128)S(1)}, f32[256,128]{1,0:T(8,128)}, u32[]{:S(2)}) copy-start(f32[256,128]{1,0:T(8,128)} %get-tuple-element.71.low_gb_ref) | copy-start | bytes 393220
  102.5 14.7 %copy-start.16 = (f32[256,128]{1,0:T(8,128)S(1)}, f32[256,128]{1,0:T(8,128)}, u32[]{:S(2)}) copy-start(f32[256,128]{1,0:T(8,128)} %get-tuple-element.69.low_gc_ref) | copy-start | bytes 393220
  102.5 27.6 %all-to-all-start.3 = ((f32[256,1,128]{2,1,0:T(1,128)}), f32[256,1,128]{2,1,0:T(1,128)S(1)}, u32[]{:S(2)}, u32[]{:S(2)}) async-start(f32[256,1,128]{2,1,0:T(1,128)} %sums.1), calls=%async_computation.3 | async-start | bytes 262144 | tf_op jit(solution)/shard_map/all_to_all | solution.py:548
  117.1 0.7 copy-start.23
  (1 other events, 0.6 us)
